TPU v7x, 768 devices: a whole 4x8x12 slice. The times are simulated.
768 devices in a mesh: grp: 4 (over x), gx: 48 (over y_hi, z), gy: 4 (over y_lo, core).
Axes of the slice: x: 4, y: 8 (y_hi: 4, y_lo: 2; y = y_hi * 2 + y_lo), z: 12, core: 2. Of those that a mesh axis runs over, the one named last changes fastest.
Arguments:
- potential_thermal_anomaly: float32 [192, 192, 128], P('gx', 'grp', 'gy'), may hold values from -6 to 6
- saltiness_anomaly: float32 [192, 192, 128], P('gx', 'grp', 'gy'), may hold values from -6 to 6
- x_boundary_transport_speed: float32 [192, 192, 128], P('gx', 'grp', 'gy'), may hold values from -1.8 to 1.8
- y_boundary_transport_speed: float32 [192, 192, 128], P('gx', 'grp', 'gy'), may hold values from -1.8 to 1.8
- solute_concentrations: float32 [192, 192, 17, 128], P('gx', ('grp', 'gy')), may hold values from 0.05 to 2
- ocean_site_indicator: int32 [192, 192], P('gx', 'grp'), may hold values 0 or 1
- flooded_layer_number: int32 [192, 192], P('gx', 'grp'), may hold values from 1 to 128
Outputs:
- temperature_out: float32 [192, 192, 128], P('gx', 'grp', 'gy')
- salinity_out: float32 [192, 192, 128], P('gx', 'grp', 'gy')
- east_out: float32 [192, 192, 128], P('gx', 'grp', 'gy')
- north_out: float32 [192, 192, 128], P('gx', 'grp', 'gy')
- tracers_out: float32 [192, 192, 17, 128], P('gx', ('grp', 'gy'))
All inputs are finite; a program needn't handle non-finite values. No bound on the sum of `ocean_site_indicator` on one device may be relied on, other than what follows from the above.
Results may differ from a plain program's by a relative error of at most 0.0065.
Values sent between devices are 32-bit elements; how exact they have to be, the bound alone decides.
No kernel may reach another device: no remote copies, remote signals or barrier semaphores. Data moves between devices by JAX's collectives and lax.ppermute only.
A program may use at most 32 MiB of HBM per device.

v0:
```python
import jax
import jax.numpy as jnp
from jax import lax
from jax.sharding import PartitionSpec as P

STEPS = 2


ADV_STEP = 0.1
DIFFUSION = 0.1
TURN_COS = 0.955336489125606
TURN_SIN = 0.29552020666134
PRESSURE = 0.2
HALINE = 0.8
BIO_STEP = 0.5
WATER_ATT = 0.005
CHLORO_ATT = 0.003
HEATING = 20.0
TEMP_RATE = 0.0633
NUTRIENT_HALF = 0.5
PREY_HALF = 0.5
GRAZING = 0.8
PHYTO_LOSS = 0.1
GRAZER_LOSS = 0.15
ASSIMILATE = 0.3


def from_behind(block, axis, distance):
    devices = range(lax.axis_size(axis))
    route = [((i - distance) % len(devices), i) for i in devices]
    return lax.ppermute(block, axis, route)


def with_halo(block, sides, width):
    for axis, dim in sides:
        count = lax.axis_size(axis)
        forward = [(i, i + 1) for i in range(count - 1)]
        forward.append((count - 1, 0))
        backward = [(target, source) for source, target in forward]
        low = lax.ppermute(
            lax.slice_in_dim(block, block.shape[dim] - width, None, axis=dim), axis, forward
        )
        high = lax.ppermute(lax.slice_in_dim(block, 0, width, axis=dim), axis, backward)
        block = jnp.concatenate([low, block, high], axis=dim)
    return block


def limiter(first, second):
    return jnp.where(
        first * second > 0, jnp.where(jnp.abs(first) < jnp.abs(second), first, second), 0.0
    )


def advect(tracer, east_flow, north_flow):
    along_x = tracer[:, 2:-2]
    count_x = along_x.shape[0] - 4
    diff_x = along_x[1:] - along_x[:-1]
    slope_x = limiter(diff_x[:-1], diff_x[1:])
    left_x = along_x[1 : count_x + 2] + 0.5 * slope_x[0 : count_x + 1]
    right_x = along_x[2 : count_x + 3] - 0.5 * slope_x[1 : count_x + 2]
    face_x = east_flow[0 : count_x + 1, 1:-1][:, :, None, :]
    flux_x = jnp.maximum(face_x, 0.0) * left_x + jnp.minimum(face_x, 0.0) * right_x
    along_y = tracer[2:-2]
    count_y = along_y.shape[1] - 4
    diff_y = along_y[:, 1:] - along_y[:, :-1]
    slope_y = limiter(diff_y[:, :-1], diff_y[:, 1:])
    left_y = along_y[:, 1 : count_y + 2] + 0.5 * slope_y[:, 0 : count_y + 1]
    right_y = along_y[:, 2 : count_y + 3] - 0.5 * slope_y[:, 1 : count_y + 2]
    face_y = north_flow[1:-1, 0 : count_y + 1][:, :, None, :]
    flux_y = jnp.maximum(face_y, 0.0) * left_y + jnp.minimum(face_y, 0.0) * right_y
    centre = tracer[2:-2, 2:-2]
    return centre - ADV_STEP * (flux_x[1:] - flux_x[:-1] + (flux_y[:, 1:] - flux_y[:, :-1]))


def react(tracer, temper, wetness):
    depth = tracer.shape[-1]
    upper_rows = lax.broadcasted_iota(jnp.int32, (depth, depth), 0)
    upper_cols = lax.broadcasted_iota(jnp.int32, (depth, depth), 1)
    upper = jnp.where(
        upper_rows < upper_cols, 1.0, jnp.where(upper_rows == upper_cols, 0.5, 0.0)
    ).astype(jnp.float32)
    classes = jnp.arange(8, dtype=jnp.float32)
    theta = (0.3 + 0.1 * classes)[:, None]
    growth_rate = (0.6 + 0.15 * classes)[:, None]
    light_half = (0.1 + 0.1 * classes)[:, None]
    nutrient = tracer[:, :, 0]
    phyto = tracer[:, :, 1:9]
    grazer = tracer[:, :, 9:17]
    chloro = jnp.sum(theta * phyto, axis=2)
    absorb = WATER_ATT + CHLORO_ATT * jnp.abs(chloro)
    optical = jnp.dot(
        absorb, upper, precision=lax.Precision.HIGHEST, preferred_element_type=jnp.float32
    )
    light = jnp.exp(-optical)
    thermal_energy_sum = HEATING * absorb * light * wetness
    warm = jnp.exp(TEMP_RATE * temper)
    limit = nutrient / (jnp.abs(nutrient) + NUTRIENT_HALF)
    lit = light[:, :, None]
    growth = growth_rate * (warm * limit)[:, :, None] * lit / (lit + light_half) * phyto
    grazed = GRAZING * grazer * phyto / (jnp.abs(phyto) + PREY_HALF)
    new_phyto = phyto + BIO_STEP * (growth - grazed - PHYTO_LOSS * phyto)
    new_grazer = grazer + BIO_STEP * (ASSIMILATE * grazed - GRAZER_LOSS * grazer)
    new_nutrient = nutrient + BIO_STEP * (
        -jnp.sum(growth, axis=2)
        + PHYTO_LOSS * jnp.sum(phyto, axis=2)
        + GRAZER_LOSS * jnp.sum(grazer, axis=2)
        + (1.0 - ASSIMILATE) * jnp.sum(grazed, axis=2)
    )
    result = (
        jnp.concatenate([new_nutrient[:, :, None], new_phyto, new_grazer], axis=2)
        * wetness[:, :, None]
    )
    return (result, thermal_energy_sum)


def dynamics_update(temp_rim, salt_rim, flooded_edge_indicator, east_flow, north_flow):
    wet_mid = flooded_edge_indicator[1:-1, 1:-1]
    open_east = wet_mid * flooded_edge_indicator[2:, 1:-1]
    open_west = flooded_edge_indicator[:-2, 1:-1] * wet_mid
    open_north = wet_mid * flooded_edge_indicator[1:-1, 2:]
    open_south = flooded_edge_indicator[1:-1, :-2] * wet_mid

    def laplace(field):
        middle = field[1:-1, 1:-1]
        return (
            open_east * (field[2:, 1:-1] - middle)
            - open_west * (middle - field[:-2, 1:-1])
            + open_north * (field[1:-1, 2:] - middle)
            - open_south * (middle - field[1:-1, :-2])
        )

    buoyancy = temp_rim - HALINE * salt_rim
    buoy_mid = buoyancy[1:-1, 1:-1]
    new_temp = wet_mid * (temp_rim[1:-1, 1:-1] + DIFFUSION * laplace(temp_rim))
    new_salt = wet_mid * (salt_rim[1:-1, 1:-1] + DIFFUSION * laplace(salt_rim))
    new_east = open_east * (
        TURN_COS * east_flow + TURN_SIN * north_flow - PRESSURE * (buoyancy[2:, 1:-1] - buoy_mid)
    )
    new_north = open_north * (
        -TURN_SIN * east_flow + TURN_COS * north_flow - PRESSURE * (buoyancy[1:-1, 2:] - buoy_mid)
    )
    return (new_temp, new_salt, new_east, new_north)


def flow_margin(east_tile, north_tile):
    west_column = from_behind(east_tile[-1:], "gx", 1)
    south_row = from_behind(north_tile[:, -1:], ("grp", "gy"), 1)
    east_near = jnp.concatenate([west_column, east_tile, jnp.zeros_like(west_column)], axis=0)
    east_near = jnp.pad(east_near, ((0, 0), (1, 1), (0, 0)))
    north_near = jnp.concatenate([south_row, north_tile, jnp.zeros_like(south_row)], axis=1)
    north_near = jnp.pad(north_near, ((1, 1), (0, 0), (0, 0)))
    return (east_near, north_near)


def on_device(
    potential_thermal_anomaly,
    saltiness_anomaly,
    x_boundary_transport_speed,
    y_boundary_transport_speed,
    solute_concentrations,
    ocean_site_indicator,
    flooded_layer_number,
):
    vertical_share = potential_thermal_anomaly.shape[2]
    total_levels = solute_concentrations.shape[3]
    tile_rows = solute_concentrations.shape[1]
    row_start = lax.axis_index("gy") * tile_rows
    mask_tile = lax.dynamic_slice_in_dim(ocean_site_indicator, row_start, tile_rows, 1)
    bottom_tile = lax.dynamic_slice_in_dim(flooded_layer_number, row_start, tile_rows, 1)
    column_levels = lax.broadcasted_iota(jnp.int32, (1, 1, total_levels), 2)
    wet_tile = ((mask_tile[:, :, None] > 0) & (column_levels < bottom_tile[:, :, None])).astype(
        jnp.float32
    )
    forwarded_fields = solute_concentrations
    level_start = lax.axis_index("gy") * vertical_share
    phys_levels = level_start + lax.broadcasted_iota(jnp.int32, (1, 1, vertical_share), 2)
    wet_phys = (
        (ocean_site_indicator[:, :, None] > 0) & (phys_levels < flooded_layer_number[:, :, None])
    ).astype(jnp.float32)
    for section in range(STEPS):
        temp_rim, salt_rim, flooded_edge_indicator = (
            with_halo(potential_thermal_anomaly, (("gx", 0), ("grp", 1)), 1),
            with_halo(saltiness_anomaly, (("gx", 0), ("grp", 1)), 1),
            with_halo(wet_phys, (("gx", 0), ("grp", 1)), 1),
        )
        (
            thermal_halfway_value,
            saltiness_anomaly,
            x_boundary_transport_speed,
            y_boundary_transport_speed,
        ) = dynamics_update(
            temp_rim,
            salt_rim,
            flooded_edge_indicator,
            x_boundary_transport_speed,
            y_boundary_transport_speed,
        )
        east_tile, north_tile, temp_tile = (
            lax.all_to_all(
                x_boundary_transport_speed, "gy", split_axis=1, concat_axis=2, tiled=True
            ),
            lax.all_to_all(
                y_boundary_transport_speed, "gy", split_axis=1, concat_axis=2, tiled=True
            ),
            lax.all_to_all(thermal_halfway_value, "gy", split_axis=1, concat_axis=2, tiled=True),
        )
        tracer_near = with_halo(forwarded_fields, (("gx", 0), (("grp", "gy"), 1)), 2)
        east_near, north_near = flow_margin(east_tile, north_tile)
        moved = advect(tracer_near, east_near, north_near)
        forwarded_fields, heat_tile = react(moved, temp_tile, wet_tile)
        thermal_energy_layerwise = lax.all_to_all(
            heat_tile, "gy", split_axis=2, concat_axis=1, tiled=True
        )
        potential_thermal_anomaly = thermal_halfway_value + thermal_energy_layerwise
    return (
        potential_thermal_anomaly,
        saltiness_anomaly,
        x_boundary_transport_speed,
        y_boundary_transport_speed,
        forwarded_fields,
    )


def solution(mesh):
    return jax.shard_map(
        on_device,
        mesh=mesh,
        in_specs=(
            P("gx", "grp", "gy"),
            P("gx", "grp", "gy"),
            P("gx", "grp", "gy"),
            P("gx", "grp", "gy"),
            P("gx", ("grp", "gy"), None, None),
            P("gx", "grp"),
            P("gx", "grp"),
        ),
        out_specs=(
            P("gx", "grp", "gy"),
            P("gx", "grp", "gy"),
            P("gx", "grp", "gy"),
            P("gx", "grp", "gy"),
            P("gx", ("grp", "gy"), None, None),
        ),
        check_vma=False,
    )
```

profile of v0, /device:TPU:1, one launch (start us, length us, event | category | flops | bytes accessed | tf_op | source)
XLA Modules:
  0.0 234.0 jit_solution(727347275254162805)
XLA Ops:
  0.6 0.8 fusion.158
  1.4 18.8 %collective-permute-start.1 = (f32[1,48,32]{1,2,0:T(8,128)S(1)}, f32[1,48,32]{1,2,0:T(8,128)S(1)}, u32[]{:S(2)}, u32[]{:S(2)}) collective-permute-start(f32[1,48,32]{1,2,0:T(8,128)S(1)} %get-tuple-element.90), channel_id=1, source_target_pairs={{4,0},{8,4},{12,8},{16,12},{20,16},{24,20},{28,24},{32,28},{36,32}... | collective-permute-start | bytes 18440 | tf_op jit(solution)/shard_map/ppermute | solution.py:43
  20.2 1.9 collective-permute-start.3
  22.2 7.6 %collective-permute-start.9 = (f32[1,48,32]{1,2,0:T(8,128)S(1)}, f32[1,48,32]{1,2,0:T(8,128)S(1)}, u32[]{:S(2)}, u32[]{:S(2)}) collective-permute-start(f32[1,48,32]{1,2,0:T(8,128)S(1)} %get-tuple-element.94), channel_id=1, source_target_pairs={{4,0},{8,4},{12,8},{16,12},{20,16},{24,20},{28,24},{32,28},{36,32}... | collective-permute-start | bytes 18440 | tf_op jit(solution)/shard_map/ppermute | solution.py:43
  30.6 1.9 collective-permute-start
  32.5 3.4 %collective-permute-start.2 = (f32[1,48,32]{1,2,0:T(8,128)S(1)}, f32[1,48,32]{1,2,0:T(8,128)S(1)}, u32[]{:S(2)}, u32[]{:S(2)}) collective-permute-start(f32[1,48,32]{1,2,0:T(8,128)S(1)} %get-tuple-element.93), channel_id=1, source_target_pairs={{0,4},{4,8},{8,12},{12,16},{16,20},{20,24},{24,28},{28,32},{32,36}... | collective-permute-start | bytes 18440 | tf_op jit(solution)/shard_map/ppermute | solution.py:40
  36.0 1.3 fusion.150
  37.4 1.9 collective-permute-start.8
  39.4 1.8 collective-permute-done.2
  41.2 1.9 collective-permute-start.13
  43.2 2.9 %collective-permute-done.8 = f32[1,48,32]{1,2,0:T(8,128)S(1)} collective-permute-done((f32[1,48,32]{1,2,0:T(8,128)S(1)}, f32[1,48,32]{1,2,0:T(8,128)S(1)}, u32[]{:S(2)}, u32[]{:S(2)}) %collective-permute-start.8) | collective-permute-done | bytes 6176 | tf_op jit(solution)/shard_map/ppermute | solution.py:40
  46.2 0.8 copy-done.1
  47.0 3.1 %collective-permute-start.6 = (f32[6,1,32]{1,2,0:T(8,128)S(1)}, f32[6,1,32]{1,2,0:T(8,128)S(1)}, u32[]{:S(2)}, u32[]{:S(2)}) collective-permute-start(f32[6,1,32]{1,2,0:T(8,128)S(1)} %get-tuple-element.82), channel_id=1, source_target_pairs={{0,192},{192,384},{384,576},{576,0},{1,193},{193,385},{385,577},{5... | collective-permute-start | bytes 2312 | tf_op jit(solution)/shard_map/ppermute | solution.py:40
  50.1 3.4 %collective-permute-start.4 = (f32[6,1,32]{1,2,0:T(8,128)S(1)}, f32[6,1,32]{1,2,0:T(8,128)S(1)}, u32[]{:S(2)}, u32[]{:S(2)}) collective-permute-start(f32[6,1,32]{1,2,0:T(8,128)S(1)} %get-tuple-element.83), channel_id=1, source_target_pairs={{192,0},{384,192},{576,384},{0,576},{193,1},{385,193},{577,385},{1... | collective-permute-start | bytes 2312 | tf_op jit(solution)/shard_map/ppermute | solution.py:43
  53.6 3.2 %collective-permute-start.11 = (f32[6,1,32]{1,2,0:T(8,128)S(1)}, f32[6,1,32]{1,2,0:T(8,128)S(1)}, u32[]{:S(2)}, u32[]{:S(2)}) collective-permute-start(f32[6,1,32]{1,2,0:T(8,128)S(1)} %get-tuple-element.84), channel_id=1, source_target_pairs={{192,0},{384,192},{576,384},{0,576},{193,1},{385,193},{577,385},{1... | collective-permute-start | bytes 2312 | tf_op jit(solution)/shard_map/ppermute | solution.py:43
  56.8 2.1 collective-permute-start.10
  59.0 4.7 %collective-permute-start.14 = (f32[2,12,17,128]{3,0,1,2:T(2,128)S(1)}, f32[2,12,17,128]{3,0,1,2:T(2,128)S(1)}, u32[]{:S(2)}, u32[]{:S(2)}) collective-permute-start(f32[2,12,17,128]{3,0,1,2:T(2,128)S(1)} %get-tuple-element.71), channel_id=1, source_target_pairs={{4,0},{8,4},{12,8},{16,12},{20,16},{24,20},{28,24},{32,28},{36,32}... | collective-permute-start | bytes 626696 | tf_op jit(solution)/shard_map/ppermute | solution.py:43
  63.7 1.9 collective-permute-start.7
  65.7 4.6 %collective-permute-start.5 = (f32[6,1,32]{1,2,0:T(8,128)S(1)}, f32[6,1,32]{1,2,0:T(8,128)S(1)}, u32[]{:S(2)}, u32[]{:S(2)}) collective-permute-start(f32[6,1,32]{1,2,0:T(8,128)S(1)} %get-tuple-element.81), channel_id=1, source_target_pairs={{192,0},{384,192},{576,384},{0,576},{193,1},{385,193},{577,385},{1... | collective-permute-start | bytes 2312 | tf_op jit(solution)/shard_map/ppermute | solution.py:43
  70.5 1.4 collective-permute-done.5
  72.3 0.7 reshape.202
  73.0 8.7 %all-to-all-start.1 = ((f32[4,1,1536]{2,1,0:T(1,128)}), f32[4,1,1536]{2,1,0:T(1,128)S(1)}, u32[]{:S(2)}, u32[]{:S(2)}) async-start(f32[4,1,1536]{2,1,0:T(1,128)} %reshape.202), calls=%async_computation.1 | async-start | bytes 49152 | tf_op jit(solution)/shard_map/all_to_all | solution.py:202
  81.9 0.7 reshape.204
  82.6 2.3 all-to-all-done.1
  84.9 4.0 %all-to-all-start = ((f32[4,1,1536]{2,1,0:T(1,128)}), f32[4,1,1536]{2,1,0:T(1,128)S(1)}, u32[]{:S(2)}, u32[]{:S(2)}) async-start(f32[4,1,1536]{2,1,0:T(1,128)} %reshape.204), calls=%async_computation | async-start | bytes 49152 | tf_op jit(solution)/shard_map/all_to_all | solution.py:199
  90.5 3.5 %collective-permute-start.15 = (f32[4,1,128]{2,0,1:T(4,128)S(1)}, f32[4,1,128]{2,0,1:T(4,128)S(1)}, u32[]{:S(2)}, u32[]{:S(2)}) collective-permute-start(f32[4,1,128]{2,0,1:T(4,128)S(1)} %slice.504), channel_id=1, source_target_pairs={{579,0},{0,1},{1,2},{2,3},{3,192},{192,193},{193,194},{194,195},{1... | collective-permute-start | bytes 6152 | tf_op jit(solution)/shard_map/ppermute | solution.py:31
  94.0 1.9 collective-permute-start.22
  95.9 7.6 %collective-permute-start.23 = (f32[1,48,32]{1,2,0:T(8,128)S(1)}, f32[1,48,32]{1,2,0:T(8,128)S(1)}, u32[]{:S(2)}, u32[]{:S(2)}) collective-permute-start(f32[1,48,32]{1,2,0:T(8,128)S(1)} %get-tuple-element.87), channel_id=1, source_target_pairs={{4,0},{8,4},{12,8},{16,12},{20,16},{24,20},{28,24},{32,28},{36,32}... | collective-permute-start | bytes 18440 | tf_op jit(solution)/shard_map/ppermute | solution.py:43
  104.7 1.9 collective-permute-start.12
  106.7 6.8 %collective-permute-done.12 = f32[1,12,128]{2,0,1:T(1,128)S(1)} collective-permute-done((f32[1,12,128]{2,0,1:T(1,128)S(1)}, f32[1,12,128]{2,0,1:T(1,128)S(1)}, u32[]{:S(2)}, u32[]{:S(2)}) %collective-permute-start.12) | collective-permute-done | bytes 6176 | tf_op jit(solution)/shard_map/ppermute | solution.py:31
  113.6 3.6 %collective-permute-start.16 = (f32[8,2,17,128]{3,0,1,2:T(8,128)S(1)}, f32[8,2,17,128]{3,0,1,2:T(8,128)S(1)}, u32[]{:S(2)}, u32[]{:S(2)}) collective-permute-start(f32[8,2,17,128]{3,0,1,2:T(8,128)S(1)} %get-tuple-element.58), channel_id=1, source_target_pairs={{0,1},{1,2},{2,3},{3,192},{192,193},{193,194},{194,195},{195,384},... | collective-permute-start | bytes 417800 | tf_op jit(solution)/shard_map/ppermute | solution.py:40
  117.2 1.9 collective-permute-start.17
  120.4 3.1 %collective-permute-done.17 = f32[8,2,17,128]{3,0,1,2:T(8,128)S(1)} collective-permute-done((f32[8,2,17,128]{3,0,1,2:T(8,128)S(1)}, f32[8,2,17,128]{3,0,1,2:T(8,128)S(1)}, u32[]{:S(2)}, u32[]{:S(2)}) %collective-permute-start.17) | collective-permute-done | bytes 139296 | tf_op jit(solution)/shard_map/ppermute | solution.py:43
  125.6 0.9 reshape.206
  126.5 3.9 %all-to-all-start.2 = ((f32[4,1,1536]{2,1,0:T(1,128)}), f32[4,1,1536]{2,1,0:T(1,128)S(1)}, u32[]{:S(2)}, u32[]{:S(2)}) async-start(f32[4,1,1536]{2,1,0:T(1,128)} %reshape.206), calls=%async_computation.2 | async-start | bytes 49152 | tf_op jit(solution)/shard_map/all_to_all | solution.py:211
  130.5 3.1 %all-to-all-done.2 = f32[4,1,1536]{2,1,0:T(1,128)S(1)} async-done(((f32[4,1,1536]{2,1,0:T(1,128)}), f32[4,1,1536]{2,1,0:T(1,128)S(1)}, u32[]{:S(2)}, u32[]{:S(2)}) %all-to-all-start.2) | async-done | bytes 24608 | tf_op jit(solution)/shard_map/all_to_all | solution.py:211
  135.1 1.9 collective-permute-start.19
  137.0 7.6 %collective-permute-start.18 = (f32[1,48,32]{1,2,0:T(8,128)S(1)}, f32[1,48,32]{1,2,0:T(8,128)S(1)}, u32[]{:S(2)}, u32[]{:S(2)}) collective-permute-start(f32[1,48,32]{1,2,0:T(8,128)S(1)} %get-tuple-element.89), channel_id=1, source_target_pairs={{4,0},{8,4},{12,8},{16,12},{20,16},{24,20},{28,24},{32,28},{36,32}... | collective-permute-start | bytes 18440 | tf_op jit(solution)/shard_map/ppermute | solution.py:43
  144.7 3.1 %collective-permute-start.24 = (f32[6,1,32]{1,2,0:T(8,128)S(1)}, f32[6,1,32]{1,2,0:T(8,128)S(1)}, u32[]{:S(2)}, u32[]{:S(2)}) collective-permute-start(f32[6,1,32]{1,2,0:T(8,128)S(1)} %get-tuple-element.76), channel_id=1, source_target_pairs={{0,192},{192,384},{384,576},{576,0},{1,193},{193,385},{385,577},{5... | collective-permute-start | bytes 2312 | tf_op jit(solution)/shard_map/ppermute | solution.py:40
  147.8 3.4 %collective-permute-start.25 = (f32[6,1,32]{1,2,0:T(8,128)S(1)}, f32[6,1,32]{1,2,0:T(8,128)S(1)}, u32[]{:S(2)}, u32[]{:S(2)}) collective-permute-start(f32[6,1,32]{1,2,0:T(8,128)S(1)} %get-tuple-element.77), channel_id=1, source_target_pairs={{192,0},{384,192},{576,384},{0,576},{193,1},{385,193},{577,385},{1... | collective-permute-start | bytes 2312 | tf_op jit(solution)/shard_map/ppermute | solution.py:43
  151.3 1.9 collective-permute-start.21
  153.3 4.6 %collective-permute-start.20 = (f32[6,1,32]{1,2,0:T(8,128)S(1)}, f32[6,1,32]{1,2,0:T(8,128)S(1)}, u32[]{:S(2)}, u32[]{:S(2)}) collective-permute-start(f32[6,1,32]{1,2,0:T(8,128)S(1)} %get-tuple-element.79), channel_id=1, source_target_pairs={{192,0},{384,192},{576,384},{0,576},{193,1},{385,193},{577,385},{1... | collective-permute-start | bytes 2312 | tf_op jit(solution)/shard_map/ppermute | solution.py:43
  158.0 0.7 reshape.208
  158.7 5.7 %all-to-all-start.3 = ((f32[4,1,1536]{2,1,0:T(1,128)}), f32[4,1,1536]{2,1,0:T(1,128)S(1)}, u32[]{:S(2)}, u32[]{:S(2)}) async-start(f32[4,1,1536]{2,1,0:T(1,128)} %reshape.208), calls=%async_computation.3 | async-start | bytes 49152 | tf_op jit(solution)/shard_map/all_to_all | solution.py:205
  165.3 0.7 reshape.212
  166.2 0.7 reshape.210
  167.5 4.0 %all-to-all-start.5 = ((f32[4,1,1536]{2,1,0:T(1,128)}), f32[4,1,1536]{2,1,0:T(1,128)S(1)}, u32[]{:S(2)}, u32[]{:S(2)}) async-start(f32[4,1,1536]{2,1,0:T(1,128)} %reshape.210), calls=%async_computation.5 | async-start | bytes 49152 | tf_op jit(solution)/shard_map/all_to_all | solution.py:202
  173.1 1.5 all-to-all-done.5
  174.7 4.0 %all-to-all-start.4 = ((f32[4,1,1536]{2,1,0:T(1,128)}), f32[4,1,1536]{2,1,0:T(1,128)S(1)}, u32[]{:S(2)}, u32[]{:S(2)}) async-start(f32[4,1,1536]{2,1,0:T(1,128)} %reshape.212), calls=%async_computation.4 | async-start | bytes 49152 | tf_op jit(solution)/shard_map/all_to_all | solution.py:199
  179.7 3.5 %collective-permute-start.29 = (f32[4,1,128]{2,0,1:T(4,128)S(1)}, f32[4,1,128]{2,0,1:T(4,128)S(1)}, u32[]{:S(2)}, u32[]{:S(2)}) collective-permute-start(f32[4,1,128]{2,0,1:T(4,128)S(1)} %slice.536), channel_id=1, source_target_pairs={{579,0},{0,1},{1,2},{2,3},{3,192},{192,193},{193,194},{194,195},{1... | collective-permute-start | bytes 6152 | tf_op jit(solution)/shard_map/ppermute | solution.py:31
  183.4 1.9 collective-permute-start.27
  185.3 7.6 %collective-permute-start.28 = (f32[2,12,17,128]{3,0,1,2:T(2,128)S(1)}, f32[2,12,17,128]{3,0,1,2:T(2,128)S(1)}, u32[]{:S(2)}, u32[]{:S(2)}) collective-permute-start(f32[2,12,17,128]{3,0,1,2:T(2,128)S(1)} %get-tuple-element.67), channel_id=1, source_target_pairs={{4,0},{8,4},{12,8},{16,12},{20,16},{24,20},{28,24},{32,28},{36,32}... | collective-permute-start | bytes 626696 | tf_op jit(solution)/shard_map/ppermute | solution.py:43
  194.0 1.9 collective-permute-start.26
  196.0 6.8 %collective-permute-done.26 = f32[1,12,128]{2,0,1:T(1,128)S(1)} collective-permute-done((f32[1,12,128]{2,0,1:T(1,128)S(1)}, f32[1,12,128]{2,0,1:T(1,128)S(1)}, u32[]{:S(2)}, u32[]{:S(2)}) %collective-permute-start.26) | collective-permute-done | bytes 6176 | tf_op jit(solution)/shard_map/ppermute | solution.py:31
  202.9 3.6 %collective-permute-start.30 = (f32[8,2,17,128]{3,0,1,2:T(8,128)S(1)}, f32[8,2,17,128]{3,0,1,2:T(8,128)S(1)}, u32[]{:S(2)}, u32[]{:S(2)}) collective-permute-start(f32[8,2,17,128]{3,0,1,2:T(8,128)S(1)} %get-tuple-element.56), channel_id=1, source_target_pairs={{0,1},{1,2},{2,3},{3,192},{192,193},{193,194},{194,195},{195,384},... | collective-permute-start | bytes 417800 | tf_op jit(solution)/shard_map/ppermute | solution.py:40
  206.5 2.1 collective-permute-start.31
  209.9 3.0 %collective-permute-done.31 = f32[8,2,17,128]{3,0,1,2:T(8,128)S(1)} collective-permute-done((f32[8,2,17,128]{3,0,1,2:T(8,128)S(1)}, f32[8,2,17,128]{3,0,1,2:T(8,128)S(1)}, u32[]{:S(2)}, u32[]{:S(2)}) %collective-permute-start.31) | collective-permute-done | bytes 139296 | tf_op jit(solution)/shard_map/ppermute | solution.py:43
  215.2 6.2 %all_to_all.126 = f32[4,1,1536]{2,1,0:T(1,128)S(1)} all-to-all(f32[4,1,1536]{2,1,0:T(1,128)S(1)} %reshape.214), channel_id=1, replica_groups=mesh['grp'=4,'gx'=48,'gy'=4] {'gy'}, dimensions={0} | all-to-all | bytes 49152 | tf_op jit(solution)/shard_map/all_to_all | solution.py:211
  222.7 0.8 fusion.141
  223.6 0.7 reshape.216
  224.4 4.0 %all-to-all-start.7 = ((f32[4,1,1536]{2,1,0:T(1,128)}), f32[4,1,1536]{2,1,0:T(1,128)S(1)}, u32[]{:S(2)}, u32[]{:S(2)}) async-start(f32[4,1,1536]{2,1,0:T(1,128)} %reshape.216), calls=%async_computation.7 | async-start | bytes 49152 | tf_op jit(solution)/shard_map/all_to_all | solution.py:205
  228.3 0.8 fusion.35
  229.1 2.4 %all-to-all-done.7 = f32[4,1,1536]{2,1,0:T(1,128)S(1)} async-done(((f32[4,1,1536]{2,1,0:T(1,128)}), f32[4,1,1536]{2,1,0:T(1,128)S(1)}, u32[]{:S(2)}, u32[]{:S(2)}) %all-to-all-start.7) | async-done | bytes 24608 | tf_op jit(solution)/shard_map/all_to_all | solution.py:205
  233.1 0.8 copy.347
  (173 shorter events, 22.0 us)
Async XLA Ops:
  0.6 21.5 %copy-start.2 = (f32[4,48,32]{1,2,0:T(8,128)S(1)}, f32[4,48,32]{1,2,0:T(8,128)}, u32[]{:S(2)}) copy-start(f32[4,48,32]{1,2,0:T(8,128)} %param.8) | copy-start | bytes 73732
  1.4 55.4 %collective-permute-start.1 = (f32[1,48,32]{1,2,0:T(8,128)S(1)}, f32[1,48,32]{1,2,0:T(8,128)S(1)}, u32[]{:S(2)}, u32[]{:S(2)}) collective-permute-start(f32[1,48,32]{1,2,0:T(8,128)S(1)} %get-tuple-element.90), channel_id=1, source_target_pairs={{4,0},{8,4},{12,8},{16,12},{20,16},{24,20},{28,24},{32,28},{36,32}... | collective-permute-start | bytes 18440 | tf_op jit(solution)/shard_map/ppermute | solution.py:43
  20.2 25.9 %collective-permute-start.3 = (f32[1,48,32]{1,2,0:T(8,128)S(1)}, f32[1,48,32]{1,2,0:T(8,128)S(1)}, u32[]{:S(2)}, u32[]{:S(2)}) collective-permute-start(f32[1,48,32]{1,2,0:T(8,128)S(1)} %get-tuple-element.91), channel_id=1, source_target_pairs={{0,4},{4,8},{8,12},{12,16},{16,20},{20,24},{24,28},{28,32},{32,36}... | collective-permute-start | bytes 18440 | tf_op jit(solution)/shard_map/ppermute | solution.py:40
  22.2 31.3 %collective-permute-start.9 = (f32[1,48,32]{1,2,0:T(8,128)S(1)}, f32[1,48,32]{1,2,0:T(8,128)S(1)}, u32[]{:S(2)}, u32[]{:S(2)}) collective-permute-start(f32[1,48,32]{1,2,0:T(8,128)S(1)} %get-tuple-element.94), channel_id=1, source_target_pairs={{4,0},{8,4},{12,8},{16,12},{20,16},{24,20},{28,24},{32,28},{36,32}... | collective-permute-start | bytes 18440 | tf_op jit(solution)/shard_map/ppermute | solution.py:43
  29.8 0.7 copy-start.8
  29.8 0.7 copy-start.5
  30.6 6.9 %collective-permute-start = (f32[1,48,32]{1,2,0:T(8,128)S(1)}, f32[1,48,32]{1,2,0:T(8,128)S(1)}, u32[]{:S(2)}, u32[]{:S(2)}) collective-permute-start(f32[1,48,32]{1,2,0:T(8,128)S(1)} %get-tuple-element.92), channel_id=1, source_target_pairs={{4,0},{8,4},{12,8},{16,12},{20,16},{24,20},{28,24},{32,28},{36,32}... | collective-permute-start | bytes 18440 | tf_op jit(solution)/shard_map/ppermute | solution.py:43
  32.5 8.7 %collective-permute-start.2 = (f32[1,48,32]{1,2,0:T(8,128)S(1)}, f32[1,48,32]{1,2,0:T(8,128)S(1)}, u32[]{:S(2)}, u32[]{:S(2)}) collective-permute-start(f32[1,48,32]{1,2,0:T(8,128)S(1)} %get-tuple-element.93), channel_id=1, source_target_pairs={{0,4},{4,8},{8,12},{12,16},{16,20},{20,24},{24,28},{28,32},{32,36}... | collective-permute-start | bytes 18440 | tf_op jit(solution)/shard_map/ppermute | solution.py:40
  37.4 8.7 %collective-permute-start.8 = (f32[1,48,32]{1,2,0:T(8,128)S(1)}, f32[1,48,32]{1,2,0:T(8,128)S(1)}, u32[]{:S(2)}, u32[]{:S(2)}) collective-permute-start(f32[1,48,32]{1,2,0:T(8,128)S(1)} %get-tuple-element.95), channel_id=1, source_target_pairs={{0,4},{4,8},{8,12},{12,16},{16,20},{20,24},{24,28},{28,32},{32,36}... | collective-permute-start | bytes 18440 | tf_op jit(solution)/shard_map/ppermute | solution.py:40
  41.2 72.3 %collective-permute-start.13 = (f32[2,12,17,128]{3,0,1,2:T(2,128)S(1)}, f32[2,12,17,128]{3,0,1,2:T(2,128)S(1)}, u32[]{:S(2)}, u32[]{:S(2)}) collective-permute-start(f32[2,12,17,128]{3,0,1,2:T(2,128)S(1)} %get-tuple-element.70), channel_id=1, source_target_pairs={{0,4},{4,8},{8,12},{12,16},{16,20},{20,24},{24,28},{28,32},{32,36}... | collective-permute-start | bytes 626696 | tf_op jit(solution)/shard_map/ppermute | solution.py:40
  46.1 0.8 copy-start.1
  47.0 12.0 %collective-permute-start.6 = (f32[6,1,32]{1,2,0:T(8,128)S(1)}, f32[6,1,32]{1,2,0:T(8,128)S(1)}, u32[]{:S(2)}, u32[]{:S(2)}) collective-permute-start(f32[6,1,32]{1,2,0:T(8,128)S(1)} %get-tuple-element.82), channel_id=1, source_target_pairs={{0,192},{192,384},{384,576},{576,0},{1,193},{193,385},{385,577},{5... | collective-permute-start | bytes 2312 | tf_op jit(solution)/shard_map/ppermute | solution.py:40
  50.1 13.6 %collective-permute-start.4 = (f32[6,1,32]{1,2,0:T(8,128)S(1)}, f32[6,1,32]{1,2,0:T(8,128)S(1)}, u32[]{:S(2)}, u32[]{:S(2)}) collective-permute-start(f32[6,1,32]{1,2,0:T(8,128)S(1)} %get-tuple-element.83), channel_id=1, source_target_pairs={{192,0},{384,192},{576,384},{0,576},{193,1},{385,193},{577,385},{1... | collective-permute-start | bytes 2312 | tf_op jit(solution)/shard_map/ppermute | solution.py:43
  53.6 12.1 %collective-permute-start.11 = (f32[6,1,32]{1,2,0:T(8,128)S(1)}, f32[6,1,32]{1,2,0:T(8,128)S(1)}, u32[]{:S(2)}, u32[]{:S(2)}) collective-permute-start(f32[6,1,32]{1,2,0:T(8,128)S(1)} %get-tuple-element.84), channel_id=1, source_target_pairs={{192,0},{384,192},{576,384},{0,576},{193,1},{385,193},{577,385},{1... | collective-permute-start | bytes 2312 | tf_op jit(solution)/shard_map/ppermute | solution.py:43
  56.8 13.5 %collective-permute-start.10 = (f32[6,1,32]{1,2,0:T(8,128)S(1)}, f32[6,1,32]{1,2,0:T(8,128)S(1)}, u32[]{:S(2)}, u32[]{:S(2)}) collective-permute-start(f32[6,1,32]{1,2,0:T(8,128)S(1)} %get-tuple-element.85), channel_id=1, source_target_pairs={{0,192},{192,384},{384,576},{576,0},{1,193},{193,385},{385,577},{5... | collective-permute-start | bytes 2312 | tf_op jit(solution)/shard_map/ppermute | solution.py:40
  59.0 54.5 %collective-permute-start.14 = (f32[2,12,17,128]{3,0,1,2:T(2,128)S(1)}, f32[2,12,17,128]{3,0,1,2:T(2,128)S(1)}, u32[]{:S(2)}, u32[]{:S(2)}) collective-permute-start(f32[2,12,17,128]{3,0,1,2:T(2,128)S(1)} %get-tuple-element.71), channel_id=1, source_target_pairs={{4,0},{8,4},{12,8},{16,12},{20,16},{24,20},{28,24},{32,28},{36,32}... | collective-permute-start | bytes 626696 | tf_op jit(solution)/shard_map/ppermute | solution.py:43
  63.7 6.7 %collective-permute-start.7 = (f32[6,1,32]{1,2,0:T(8,128)S(1)}, f32[6,1,32]{1,2,0:T(8,128)S(1)}, u32[]{:S(2)}, u32[]{:S(2)}) collective-permute-start(f32[6,1,32]{1,2,0:T(8,128)S(1)} %get-tuple-element.80), channel_id=1, source_target_pairs={{0,192},{192,384},{384,576},{576,0},{1,193},{193,385},{385,577},{5... | collective-permute-start | bytes 2312 | tf_op jit(solution)/shard_map/ppermute | solution.py:40
  65.7 6.2 %collective-permute-start.5 = (f32[6,1,32]{1,2,0:T(8,128)S(1)}, f32[6,1,32]{1,2,0:T(8,128)S(1)}, u32[]{:S(2)}, u32[]{:S(2)}) collective-permute-start(f32[6,1,32]{1,2,0:T(8,128)S(1)} %get-tuple-element.81), channel_id=1, source_target_pairs={{192,0},{384,192},{576,384},{0,576},{193,1},{385,193},{577,385},{1... | collective-permute-start | bytes 2312 | tf_op jit(solution)/shard_map/ppermute | solution.py:43
  70.5 1.6 copy-start.6
  70.5 1.6 copy-start.7
  73.0 11.9 %all-to-all-start.1 = ((f32[4,1,1536]{2,1,0:T(1,128)}), f32[4,1,1536]{2,1,0:T(1,128)S(1)}, u32[]{:S(2)}, u32[]{:S(2)}) async-start(f32[4,1,1536]{2,1,0:T(1,128)} %reshape.202), calls=%async_computation.1 | async-start | bytes 49152 | tf_op jit(solution)/shard_map/all_to_all | solution.py:202
  84.9 18.6 %all-to-all-start = ((f32[4,1,1536]{2,1,0:T(1,128)}), f32[4,1,1536]{2,1,0:T(1,128)S(1)}, u32[]{:S(2)}, u32[]{:S(2)}) async-start(f32[4,1,1536]{2,1,0:T(1,128)} %reshape.204), calls=%async_computation | async-start | bytes 49152 | tf_op jit(solution)/shard_map/all_to_all | solution.py:199
  90.5 14.2 %collective-permute-start.15 = (f32[4,1,128]{2,0,1:T(4,128)S(1)}, f32[4,1,128]{2,0,1:T(4,128)S(1)}, u32[]{:S(2)}, u32[]{:S(2)}) collective-permute-start(f32[4,1,128]{2,0,1:T(4,128)S(1)} %slice.504), channel_id=1, source_target_pairs={{579,0},{0,1},{1,2},{2,3},{3,192},{192,193},{193,194},{194,195},{1... | collective-permute-start | bytes 6152 | tf_op jit(solution)/shard_map/ppermute | solution.py:31
  94.0 36.4 %collective-permute-start.22 = (f32[1,48,32]{1,2,0:T(8,128)S(1)}, f32[1,48,32]{1,2,0:T(8,128)S(1)}, u32[]{:S(2)}, u32[]{:S(2)}) collective-permute-start(f32[1,48,32]{1,2,0:T(8,128)S(1)} %get-tuple-element.86), channel_id=1, source_target_pairs={{0,4},{4,8},{8,12},{12,16},{16,20},{20,24},{24,28},{28,32},{32,36}... | collective-permute-start | bytes 18440 | tf_op jit(solution)/shard_map/ppermute | solution.py:40
  95.9 34.5 %collective-permute-start.23 = (f32[1,48,32]{1,2,0:T(8,128)S(1)}, f32[1,48,32]{1,2,0:T(8,128)S(1)}, u32[]{:S(2)}, u32[]{:S(2)}) collective-permute-start(f32[1,48,32]{1,2,0:T(8,128)S(1)} %get-tuple-element.87), channel_id=1, source_target_pairs={{4,0},{8,4},{12,8},{16,12},{20,16},{24,20},{28,24},{32,28},{36,32}... | collective-permute-start | bytes 18440 | tf_op jit(solution)/shard_map/ppermute | solution.py:43
  104.2 9.3 %copy-start = (f32[4,12,17,128]{3,0,2,1:T(4,128)S(1)}, f32[4,12,17,128]{3,0,2,1:T(4,128)}, u32[]{:S(2)}) copy-start(f32[4,12,17,128]{3,0,2,1:T(4,128)} %param.11) | copy-start | bytes 1253380
  104.7 8.8 %collective-permute-start.12 = (f32[1,12,128]{2,0,1:T(1,128)S(1)}, f32[1,12,128]{2,0,1:T(1,128)S(1)}, u32[]{:S(2)}, u32[]{:S(2)}) collective-permute-start(f32[1,12,128]{2,0,1:T(1,128)S(1)} %slice.399), channel_id=1, source_target_pairs={{188,0},{0,4},{4,8},{8,12},{12,16},{16,20},{20,24},{24,28},{28,32}... | collective-permute-start | bytes 18440 | tf_op jit(solution)/shard_map/ppermute | solution.py:31
  113.6 6.8 %collective-permute-start.16 = (f32[8,2,17,128]{3,0,1,2:T(8,128)S(1)}, f32[8,2,17,128]{3,0,1,2:T(8,128)S(1)}, u32[]{:S(2)}, u32[]{:S(2)}) collective-permute-start(f32[8,2,17,128]{3,0,1,2:T(8,128)S(1)} %get-tuple-element.58), channel_id=1, source_target_pairs={{0,1},{1,2},{2,3},{3,192},{192,193},{193,194},{194,195},{195,384},... | collective-permute-start | bytes 417800 | tf_op jit(solution)/shard_map/ppermute | solution.py:40
  117.2 6.4 %collective-permute-start.17 = (f32[8,2,17,128]{3,0,1,2:T(8,128)S(1)}, f32[8,2,17,128]{3,0,1,2:T(8,128)S(1)}, u32[]{:S(2)}, u32[]{:S(2)}) collective-permute-start(f32[8,2,17,128]{3,0,1,2:T(8,128)S(1)} %get-tuple-element.59), channel_id=1, source_target_pairs={{1,0},{2,1},{3,2},{192,3},{193,192},{194,193},{195,194},{384,195},... | collective-permute-start | bytes 417800 | tf_op jit(solution)/shard_map/ppermute | solution.py:43
  126.5 7.1 %all-to-all-start.2 = ((f32[4,1,1536]{2,1,0:T(1,128)}), f32[4,1,1536]{2,1,0:T(1,128)S(1)}, u32[]{:S(2)}, u32[]{:S(2)}) async-start(f32[4,1,1536]{2,1,0:T(1,128)} %reshape.206), calls=%async_computation.2 | async-start | bytes 49152 | tf_op jit(solution)/shard_map/all_to_all | solution.py:211
  135.1 16.1 %collective-permute-start.19 = (f32[1,48,32]{1,2,0:T(8,128)S(1)}, f32[1,48,32]{1,2,0:T(8,128)S(1)}, u32[]{:S(2)}, u32[]{:S(2)}) collective-permute-start(f32[1,48,32]{1,2,0:T(8,128)S(1)} %get-tuple-element.88), channel_id=1, source_target_pairs={{0,4},{4,8},{8,12},{12,16},{16,20},{20,24},{24,28},{28,32},{32,36}... | collective-permute-start | bytes 18440 | tf_op jit(solution)/shard_map/ppermute | solution.py:40
  137.0 14.2 %collective-permute-start.18 = (f32[1,48,32]{1,2,0:T(8,128)S(1)}, f32[1,48,32]{1,2,0:T(8,128)S(1)}, u32[]{:S(2)}, u32[]{:S(2)}) collective-permute-start(f32[1,48,32]{1,2,0:T(8,128)S(1)} %get-tuple-element.89), channel_id=1, source_target_pairs={{4,0},{8,4},{12,8},{16,12},{20,16},{24,20},{28,24},{32,28},{36,32}... | collective-permute-start | bytes 18440 | tf_op jit(solution)/shard_map/ppermute | solution.py:43
  144.7 19.7 %collective-permute-start.24 = (f32[6,1,32]{1,2,0:T(8,128)S(1)}, f32[6,1,32]{1,2,0:T(8,128)S(1)}, u32[]{:S(2)}, u32[]{:S(2)}) collective-permute-start(f32[6,1,32]{1,2,0:T(8,128)S(1)} %get-tuple-element.76), channel_id=1, source_target_pairs={{0,192},{192,384},{384,576},{576,0},{1,193},{193,385},{385,577},{5... | collective-permute-start | bytes 2312 | tf_op jit(solution)/shard_map/ppermute | solution.py:40
  147.8 16.6 %collective-permute-start.25 = (f32[6,1,32]{1,2,0:T(8,128)S(1)}, f32[6,1,32]{1,2,0:T(8,128)S(1)}, u32[]{:S(2)}, u32[]{:S(2)}) collective-permute-start(f32[6,1,32]{1,2,0:T(8,128)S(1)} %get-tuple-element.77), channel_id=1, source_target_pairs={{192,0},{384,192},{576,384},{0,576},{193,1},{385,193},{577,385},{1... | collective-permute-start | bytes 2312 | tf_op jit(solution)/shard_map/ppermute | solution.py:43
  151.3 13.1 %collective-permute-start.21 = (f32[6,1,32]{1,2,0:T(8,128)S(1)}, f32[6,1,32]{1,2,0:T(8,128)S(1)}, u32[]{:S(2)}, u32[]{:S(2)}) collective-permute-start(f32[6,1,32]{1,2,0:T(8,128)S(1)} %get-tuple-element.78), channel_id=1, source_target_pairs={{0,192},{192,384},{384,576},{576,0},{1,193},{193,385},{385,577},{5... | collective-permute-start | bytes 2312 | tf_op jit(solution)/shard_map/ppermute | solution.py:40
  153.3 11.1 %collective-permute-start.20 = (f32[6,1,32]{1,2,0:T(8,128)S(1)}, f32[6,1,32]{1,2,0:T(8,128)S(1)}, u32[]{:S(2)}, u32[]{:S(2)}) collective-permute-start(f32[6,1,32]{1,2,0:T(8,128)S(1)} %get-tuple-element.79), channel_id=1, source_target_pairs={{192,0},{384,192},{576,384},{0,576},{193,1},{385,193},{577,385},{1... | collective-permute-start | bytes 2312 | tf_op jit(solution)/shard_map/ppermute | solution.py:43
  158.7 8.8 %all-to-all-start.3 = ((f32[4,1,1536]{2,1,0:T(1,128)}), f32[4,1,1536]{2,1,0:T(1,128)S(1)}, u32[]{:S(2)}, u32[]{:S(2)}) async-start(f32[4,1,1536]{2,1,0:T(1,128)} %reshape.208), calls=%async_computation.3 | async-start | bytes 49152 | tf_op jit(solution)/shard_map/all_to_all | solution.py:205
  164.7 0.6 copy-start.3
  164.7 1.4 copy-start.4
  167.5 7.1 %all-to-all-start.5 = ((f32[4,1,1536]{2,1,0:T(1,128)}), f32[4,1,1536]{2,1,0:T(1,128)S(1)}, u32[]{:S(2)}, u32[]{:S(2)}) async-start(f32[4,1,1536]{2,1,0:T(1,128)} %reshape.210), calls=%async_computation.5 | async-start | bytes 49152 | tf_op jit(solution)/shard_map/all_to_all | solution.py:202
  174.7 18.2 %all-to-all-start.4 = ((f32[4,1,1536]{2,1,0:T(1,128)}), f32[4,1,1536]{2,1,0:T(1,128)S(1)}, u32[]{:S(2)}, u32[]{:S(2)}) async-start(f32[4,1,1536]{2,1,0:T(1,128)} %reshape.212), calls=%async_computation.4 | async-start | bytes 49152 | tf_op jit(solution)/shard_map/all_to_all | solution.py:199
  179.7 16.3 %collective-permute-start.29 = (f32[4,1,128]{2,0,1:T(4,128)S(1)}, f32[4,1,128]{2,0,1:T(4,128)S(1)}, u32[]{:S(2)}, u32[]{:S(2)}) collective-permute-start(f32[4,1,128]{2,0,1:T(4,128)S(1)} %slice.536), channel_id=1, source_target_pairs={{579,0},{0,1},{1,2},{2,3},{3,192},{192,193},{193,194},{194,195},{1... | collective-permute-start | bytes 6152 | tf_op jit(solution)/shard_map/ppermute | solution.py:31
  183.4 19.5 %collective-permute-start.27 = (f32[2,12,17,128]{3,0,1,2:T(2,128)S(1)}, f32[2,12,17,128]{3,0,1,2:T(2,128)S(1)}, u32[]{:S(2)}, u32[]{:S(2)}) collective-permute-start(f32[2,12,17,128]{3,0,1,2:T(2,128)S(1)} %get-tuple-element.66), channel_id=1, source_target_pairs={{0,4},{4,8},{8,12},{12,16},{16,20},{20,24},{24,28},{28,32},{32,36}... | collective-permute-start | bytes 626696 | tf_op jit(solution)/shard_map/ppermute | solution.py:40
  185.3 17.5 %collective-permute-start.28 = (f32[2,12,17,128]{3,0,1,2:T(2,128)S(1)}, f32[2,12,17,128]{3,0,1,2:T(2,128)S(1)}, u32[]{:S(2)}, u32[]{:S(2)}) collective-permute-start(f32[2,12,17,128]{3,0,1,2:T(2,128)S(1)} %get-tuple-element.67), channel_id=1, source_target_pairs={{4,0},{8,4},{12,8},{16,12},{20,16},{24,20},{28,24},{32,28},{36,32}... | collective-permute-start | bytes 626696 | tf_op jit(solution)/shard_map/ppermute | solution.py:43
  194.0 8.8 %collective-permute-start.26 = (f32[1,12,128]{2,0,1:T(1,128)S(1)}, f32[1,12,128]{2,0,1:T(1,128)S(1)}, u32[]{:S(2)}, u32[]{:S(2)}) collective-permute-start(f32[1,12,128]{2,0,1:T(1,128)S(1)} %slice.448), channel_id=1, source_target_pairs={{188,0},{0,4},{4,8},{8,12},{12,16},{16,20},{20,24},{24,28},{28,32}... | collective-permute-start | bytes 18440 | tf_op jit(solution)/shard_map/ppermute | solution.py:31
  202.9 7.0 %collective-permute-start.30 = (f32[8,2,17,128]{3,0,1,2:T(8,128)S(1)}, f32[8,2,17,128]{3,0,1,2:T(8,128)S(1)}, u32[]{:S(2)}, u32[]{:S(2)}) collective-permute-start(f32[8,2,17,128]{3,0,1,2:T(8,128)S(1)} %get-tuple-element.56), channel_id=1, source_target_pairs={{0,1},{1,2},{2,3},{3,192},{192,193},{193,194},{194,195},{195,384},... | collective-permute-start | bytes 417800 | tf_op jit(solution)/shard_map/ppermute | solution.py:40
  206.5 6.4 %collective-permute-start.31 = (f32[8,2,17,128]{3,0,1,2:T(8,128)S(1)}, f32[8,2,17,128]{3,0,1,2:T(8,128)S(1)}, u32[]{:S(2)}, u32[]{:S(2)}) collective-permute-start(f32[8,2,17,128]{3,0,1,2:T(8,128)S(1)} %get-tuple-element.57), channel_id=1, source_target_pairs={{1,0},{2,1},{3,2},{192,3},{193,192},{194,193},{195,194},{384,195},... | collective-permute-start | bytes 417800 | tf_op jit(solution)/shard_map/ppermute | solution.py:43
  224.4 7.1 %all-to-all-start.7 = ((f32[4,1,1536]{2,1,0:T(1,128)}), f32[4,1,1536]{2,1,0:T(1,128)S(1)}, u32[]{:S(2)}, u32[]{:S(2)}) async-start(f32[4,1,1536]{2,1,0:T(1,128)} %reshape.216), calls=%async_computation.7 | async-start | bytes 49152 | tf_op jit(solution)/shard_map/all_to_all | solution.py:205
where the time goes:
time: 236 us; the launch traced here: 234 us
  starting transfers between devices  158 us (67%)
  waiting for transfers between devices  35.9 us (15%)
  local copies, waits for them, and re-layouts  15.8 us (7%)
  other arithmetic  15.6 us (7%)
  blocking collectives  6.2 us (3%)
    ppermute x14, starting transfers between devices, with_halo(): lax.ppermute(lax.slice_in_dim(block, 0, width, axis=dim), axis, backward)  78.8 us
    ppermute x14, starting transfers between devices, with_halo(): lax.ppermute(lax.slice_in_dim(block, block.shape[dim] - width, None, axis...  34.2 us
    ppermute x4, waiting for transfers between devices, from_behind(): return lax.ppermute(block, axis, route)  13.6 us
    all_to_all x2, starting transfers between devices, on_device(): lax.all_to_all(y_boundary_transport_speed, 'gy', split_axis=1, concat_axi...  12.7 us
    ppermute x4, starting transfers between devices, from_behind(): return lax.ppermute(block, axis, route)  10.9 us
    unnamed x41, local copies, waits for them, and re-layouts  9.83 us
    all_to_all x2, starting transfers between devices, on_device(): lax.all_to_all(thermal_halfway_value, 'gy', split_axis=1, concat_axis=2,...  9.64 us
    all_to_all x2, starting transfers between devices, on_device(): lax.all_to_all(x_boundary_transport_speed, 'gy', split_axis=1, concat_axi...  7.96 us
  transfers between devices with their start and end apart: 39, of which 12 were waited for; matrix products, arithmetic and copies ran while one was open for 8% of the time, Pallas kernels for 0%

commit v1 on v0

v1 whole, which is shorter than its diff:
```python
import jax
import jax.numpy as jnp
from jax import lax
from jax.sharding import PartitionSpec as P

STEPS = 2
ADV_STEP = 0.1
DIFFUSION = 0.1
TURN_COS = 0.955336489125606
TURN_SIN = 0.29552020666134
PRESSURE = 0.2
HALINE = 0.8
BIO_STEP = 0.5
WATER_ATT = 0.005
CHLORO_ATT = 0.003
HEATING = 20.0
TEMP_RATE = 0.0633
NUTRIENT_HALF = 0.5
PREY_HALF = 0.5
GRAZING = 0.8
PHYTO_LOSS = 0.1
GRAZER_LOSS = 0.15
ASSIMILATE = 0.3
NTR = 17
ROWS = ("grp", "gy")


def ring_send(block, axis, step):
    names = axis if isinstance(axis, tuple) else (axis,)
    count = 1
    for name in names:
        count *= lax.axis_size(name)
    return lax.ppermute(block, axis, [(i, (i + step) % count) for i in range(count)])


def limiter(first, second):
    return jnp.where(
        first * second > 0, jnp.where(jnp.abs(first) < jnp.abs(second), first, second), 0.0
    )


def face_flux(q, face, axis):
    n = q.shape[axis] - 4

    def cut(a, lo, size):
        return lax.slice_in_dim(a, lo, lo + size, axis=axis)

    diff = cut(q, 1, n + 3) - cut(q, 0, n + 3)
    slope = limiter(cut(diff, 0, n + 2), cut(diff, 1, n + 2))
    left = cut(q, 1, n + 1) + 0.5 * cut(slope, 0, n + 1)
    right = cut(q, 2, n + 1) - 0.5 * cut(slope, 1, n + 1)
    face = face[:, :, None, :]
    flux = jnp.maximum(face, 0.0) * left + jnp.minimum(face, 0.0) * right
    return cut(flux, 1, n) - cut(flux, 0, n)


def react(tracer, temper, wetness):
    depth = tracer.shape[-1]
    upper_rows = lax.broadcasted_iota(jnp.int32, (depth, depth), 0)
    upper_cols = lax.broadcasted_iota(jnp.int32, (depth, depth), 1)
    upper = jnp.where(
        upper_rows < upper_cols, 1.0, jnp.where(upper_rows == upper_cols, 0.5, 0.0)
    ).astype(jnp.float32)
    classes = jnp.arange(8, dtype=jnp.float32)
    theta = (0.3 + 0.1 * classes)[:, None]
    growth_rate = (0.6 + 0.15 * classes)[:, None]
    light_half = (0.1 + 0.1 * classes)[:, None]
    nutrient = tracer[:, :, 0]
    phyto = tracer[:, :, 1:9]
    grazer = tracer[:, :, 9:17]
    chloro = jnp.sum(theta * phyto, axis=2)
    absorb = WATER_ATT + CHLORO_ATT * jnp.abs(chloro)
    optical = jnp.dot(
        absorb, upper, precision=lax.Precision.HIGHEST, preferred_element_type=jnp.float32
    )
    light = jnp.exp(-optical)
    heat = HEATING * absorb * light * wetness
    warm = jnp.exp(TEMP_RATE * temper)
    limit = nutrient / (jnp.abs(nutrient) + NUTRIENT_HALF)
    lit = light[:, :, None]
    growth = growth_rate * (warm * limit)[:, :, None] * lit / (lit + light_half) * phyto
    grazed = GRAZING * grazer * phyto / (jnp.abs(phyto) + PREY_HALF)
    new_phyto = phyto + BIO_STEP * (growth - grazed - PHYTO_LOSS * phyto)
    new_grazer = grazer + BIO_STEP * (ASSIMILATE * grazed - GRAZER_LOSS * grazer)
    new_nutrient = nutrient + BIO_STEP * (
        -jnp.sum(growth, axis=2)
        + PHYTO_LOSS * jnp.sum(phyto, axis=2)
        + GRAZER_LOSS * jnp.sum(grazer, axis=2)
        + (1.0 - ASSIMILATE) * jnp.sum(grazed, axis=2)
    )
    result = (
        jnp.concatenate([new_nutrient[:, :, None], new_phyto, new_grazer], axis=2)
        * wetness[:, :, None]
    )
    return (result, heat)


def to_columns(fields):
    parts = lax.axis_size("gy")
    packed = jnp.stack(fields, axis=2)
    nx, ny, nf, nl = packed.shape
    packed = packed.reshape(nx, parts, ny // parts, nf * nl).transpose(1, 0, 2, 3)
    packed = lax.all_to_all(packed, "gy", split_axis=0, concat_axis=0, tiled=True)
    packed = packed.reshape(parts, nx, ny // parts, nf, nl).transpose(1, 2, 3, 0, 4)
    packed = packed.reshape(nx, ny // parts, nf, parts * nl)
    return [packed[:, :, i] for i in range(nf)]


def to_levels(fields):
    parts = lax.axis_size("gy")
    packed = jnp.stack(fields, axis=2)
    nx, ny, nf, nl = packed.shape
    packed = packed.reshape(nx, ny, nf, parts, nl // parts).transpose(3, 0, 1, 2, 4)
    packed = packed.reshape(parts, nx, ny, nf * nl // parts)
    packed = lax.all_to_all(packed, "gy", split_axis=0, concat_axis=0, tiled=True)
    packed = packed.reshape(parts, nx, ny, nf, nl // parts).transpose(1, 0, 2, 3, 4)
    packed = packed.reshape(nx, parts * ny, nf, nl // parts)
    return tuple(packed[:, :, i] for i in range(nf))


def rims(axis, name, tracer, ahead, behind):
    n = tracer.shape[axis]

    def gather(lines, fields, edge):
        parts = [lax.index_in_dim(tracer, k, axis, keepdims=False) for k in lines]
        parts += [lax.index_in_dim(f, edge, axis, keepdims=False)[:, None] for f in fields]
        return jnp.concatenate(parts, axis=1)

    def open_up(block):
        lines = jnp.stack([block[:, :NTR], block[:, NTR : 2 * NTR]], axis=axis)
        rest = [
            jnp.expand_dims(block[:, k], axis) for k in range(2 * NTR, block.shape[1])
        ]
        return lines, rest

    low = ring_send(gather((n - 2, n - 1), ahead, n - 1), name, 1)
    high = ring_send(gather((0, 1), behind, 0), name, -1)
    return open_up(low), open_up(high)


def on_device(temp, salt, east, north, tracer, mask, bottom):
    levels = tracer.shape[3]
    tile_rows = tracer.shape[1]
    row_start = lax.axis_index("gy") * tile_rows
    mask_tile = lax.dynamic_slice_in_dim(mask, row_start, tile_rows, 1)
    bottom_tile = lax.dynamic_slice_in_dim(bottom, row_start, tile_rows, 1)
    column_levels = lax.broadcasted_iota(jnp.int32, (1, 1, levels), 2)
    wet = ((mask_tile[:, :, None] > 0) & (column_levels < bottom_tile[:, :, None])).astype(
        jnp.float32
    )
    temp, salt, east, north = to_columns([temp, salt, east, north])
    for step in range(STEPS):
        extra = [wet] if step == 0 else []
        ahead = [temp, salt, east, north] + extra
        behind = [temp, salt] + extra
        (t_west, f_west), (t_east, f_east) = rims(0, "gx", tracer, ahead, behind)
        (t_south, f_south), (t_north, f_north) = rims(1, ROWS, tracer, ahead, behind)
        if step == 0:
            wet_x = jnp.concatenate([f_west[4], wet, f_east[2]], axis=0)
            wet_y = jnp.concatenate([f_south[4], wet, f_north[2]], axis=1)
            open_x = wet_x[:-1] * wet_x[1:]
            open_y = wet_y[:, :-1] * wet_y[:, 1:]

        def laplace(q, qx, qy):
            return (
                open_x[1:] * (qx[2:] - q)
                - open_x[:-1] * (q - qx[:-2])
                + open_y[:, 1:] * (qy[:, 2:] - q)
                - open_y[:, :-1] * (q - qy[:, :-2])
            )

        temp_x = jnp.concatenate([f_west[0], temp, f_east[0]], axis=0)
        salt_x = jnp.concatenate([f_west[1], salt, f_east[1]], axis=0)
        temp_y = jnp.concatenate([f_south[0], temp, f_north[0]], axis=1)
        salt_y = jnp.concatenate([f_south[1], salt, f_north[1]], axis=1)
        buoy_x = temp_x - HALINE * salt_x
        buoy_y = temp_y - HALINE * salt_y
        halfway = wet * (temp + DIFFUSION * laplace(temp, temp_x, temp_y))
        salt = wet * (salt + DIFFUSION * laplace(salt, salt_x, salt_y))
        face_x = open_x * (
            TURN_COS * jnp.concatenate([f_west[2], east], axis=0)
            + TURN_SIN * jnp.concatenate([f_west[3], north], axis=0)
            - PRESSURE * (buoy_x[1:] - buoy_x[:-1])
        )
        face_y = open_y * (
            -TURN_SIN * jnp.concatenate([f_south[2], east], axis=1)
            + TURN_COS * jnp.concatenate([f_south[3], north], axis=1)
            - PRESSURE * (buoy_y[:, 1:] - buoy_y[:, :-1])
        )
        east, north = face_x[1:], face_y[:, 1:]
        moved = tracer - ADV_STEP * (
            face_flux(jnp.concatenate([t_west, tracer, t_east], axis=0), face_x, 0)
            + face_flux(jnp.concatenate([t_south, tracer, t_north], axis=1), face_y, 1)
        )
        tracer, heat = react(moved, halfway, wet)
        temp = halfway + heat
    temp, salt, east, north = to_levels([temp, salt, east, north])
    return temp, salt, east, north, tracer


def solution(mesh):
    field = P("gx", "grp", "gy")
    tracers = P("gx", ("grp", "gy"), None, None)
    columns = P("gx", "grp")
    return jax.shard_map(
        on_device,
        mesh=mesh,
        in_specs=(field, field, field, field, tracers, columns, columns),
        out_specs=(field, field, field, field, tracers),
    )
```

time: 236 us -> 88.1 us (0.37)
  starting transfers between devices: 158 us -> 54.3 us
  waiting for transfers between devices: 35.9 us -> 15.2 us
  other arithmetic: 15.6 us -> 5.54 us
  blocking collectives: 6.2 us -> 0 us
  local copies, waits for them, and re-layouts: 15.8 us -> 10.4 us
    ppermute x32 -> x8, starting transfers between devices: 124 us -> 36.1 us  [ring_send(): lax.ppermute(block, axis, [(i, (i + step) % count) for i in range(count)])]
    all_to_all x7 -> x2, starting transfers between devices: 34.2 us -> 18.2 us  [the longest x1 13.8 us: to_columns(): lax.all_to_all(packed, 'gy', split_axis=0, concat_axis=0, tiled=True)]
    ppermute x32 -> x8, waiting for transfers between devices: 25.9 us -> 11.1 us  [ring_send(): lax.ppermute(block, axis, [(i, (i + step) % count) for i in range(count)])]
    all_to_all x1 -> x0, blocking collectives: 6.2 us -> none  [on_device(): lax.all_to_all(heat_tile, 'gy', split_axis=2, concat_axis=1, tiled=True)]
    all_to_all x7 -> x2, waiting for transfers between devices: 9.96 us -> 4.05 us  [the longest x1 2.1 us: to_levels(): lax.all_to_all(packed, 'gy', split_axis=0, concat_axis=0, tiled=True)]
    all_to_all x8 -> x0, other arithmetic: 5.6 us -> none  [the longest x2 1.4 us: on_device(): lax.all_to_all(x_boundary_transport_speed, 'gy', split_axis=1, concat_axi...]
    unnamed x41 -> x28, local copies, waits for them, and re-layouts: 9.83 us -> 4.58 us
    add x9 -> x6, other arithmetic: 4.03 us -> 1.14 us  [the longest x4 0.95 us: face_flux(): flux = jnp.maximum(face, 0.0) * left + jnp.minimum(face, 0.0) * right]
  transfers between devices with their start and end apart: 39 -> 10, of which waited for: 12 -> 6; matrix products, arithmetic and copies ran while one was open for 8% -> 6% of each run, Pallas kernels for 0% -> 0%
where the time goes in v1:
time: 88.1 us; the launch traced here: 87.5 us
  starting transfers between devices  54.3 us (62%)
  waiting for transfers between devices  15.2 us (17%)
  local copies, waits for them, and re-layouts  10.4 us (12%)
  other arithmetic  5.54 us (6%)
  between operations  1.67 us (2%)
    ppermute x8, starting transfers between devices, ring_send(): lax.ppermute(block, axis, [(i, (i + step) % count) for i in range(count)])  36.1 us
    all_to_all x1, starting transfers between devices, to_columns(): lax.all_to_all(packed, 'gy', split_axis=0, concat_axis=0, tiled=True)  13.8 us
    ppermute x8, waiting for transfers between devices, ring_send(): lax.ppermute(block, axis, [(i, (i + step) % count) for i in range(count)])  11.1 us
    unnamed x28, local copies, waits for them, and re-layouts  4.58 us
    all_to_all x1, starting transfers between devices, to_levels(): lax.all_to_all(packed, 'gy', split_axis=0, concat_axis=0, tiled=True)  4.39 us
    all_to_all x1, waiting for transfers between devices, to_levels(): lax.all_to_all(packed, 'gy', split_axis=0, concat_axis=0, tiled=True)  2.1 us
    all_to_all x1, waiting for transfers between devices, to_columns(): lax.all_to_all(packed, 'gy', split_axis=0, concat_axis=0, tiled=True)  1.94 us
  transfers between devices with their start and end apart: 10, of which 6 were waited for; matrix products, arithmetic and copies ran while one was open for 6% of the time, Pallas kernels for 0%

profile of v1, /device:TPU:1, one launch (start us, length us, event | category | flops | bytes accessed | tf_op | source)
XLA Modules:
  0.0 87.5 jit_solution(5912473520488534740)
XLA Ops:
  0.6 1.0 %pad_maximum_fusion.1 = f32[4,48,4,32]{1,3,0,2:T(8,128)S(1)} fusion(f32[4,48,1,32]{1,3,0,2:T(8,128)} %bitcast.264, f32[4,48,1,32]{1,3,0,2:T(8,128)} %bitcast.265, f32[4,48,1,32]{1,3,0,2:T(8,128)} %bitcast.266, f32[4,48,1,32]{1,3,0,2:T(8,128)} %bitcast.267), kind=kLoop, calls=%fused_computation.62 | loop fusion | flops 73728 | bytes 196608 | tf_op jit(solution)/shard_map/stack | solution.py:100
  1.6 0.3 copy.74
  1.9 0.9 reshape.190
  2.8 13.8 %all-to-all-start = ((f32[4,4,12,128]{3,1,2,0:T(4,128)}), f32[4,4,12,128]{3,1,2,0:T(4,128)S(1)}, u32[]{:S(2)}, u32[]{:S(2)}) async-start(f32[4,4,12,128]{3,1,2,0:T(4,128)} %bitcast.4), calls=%async_computation | async-start | bytes 196608 | tf_op jit(solution)/shard_map/all_to_all | solution.py:103
  16.6 0.3 fusion.147
  17.0 0.6 copy-done.2
  18.0 1.9 %all-to-all-done = f32[4,4,12,128]{3,1,2,0:T(4,128)S(1)} async-done(((f32[4,4,12,128]{3,1,2,0:T(4,128)}), f32[4,4,12,128]{3,1,2,0:T(4,128)S(1)}, u32[]{:S(2)}, u32[]{:S(2)}) %all-to-all-start) | async-done | bytes 98336 | tf_op jit(solution)/shard_map/all_to_all | solution.py:103
  19.9 0.2 reshape.191
  20.1 0.3 copy.75
  20.4 0.2 reshape.192
  20.8 1.9 %collective-permute-start = (f32[12,39,128]{2,0,1:T(8,128)S(1)}, f32[12,39,128]{2,0,1:T(8,128)S(1)}, u32[]{:S(2)}, u32[]{:S(2)}) collective-permute-start(f32[12,39,128]{2,0,1:T(8,128)S(1)} %get-tuple-element.126), channel_id=1, source_target_pairs={{0,4},{4,8},{8,12},{12,16},{16,20},{20,24},{24,28},{28,32},{32,36}... | collective-permute-start | bytes 718856 | tf_op jit(solution)/shard_map/ppermute | solution.py:33
  22.8 9.0 %collective-permute-start.1 = (f32[12,37,128]{2,0,1:T(8,128)S(1)}, f32[12,37,128]{2,0,1:T(8,128)S(1)}, u32[]{:S(2)}, u32[]{:S(2)}) collective-permute-start(f32[12,37,128]{2,0,1:T(8,128)S(1)} %get-tuple-element.125), channel_id=1, source_target_pairs={{0,188},{4,0},{8,4},{12,8},{16,12},{20,16},{24,20},{28,24},{32,28}... | collective-permute-start | bytes 681992 | tf_op jit(solution)/shard_map/ppermute | solution.py:33
  31.8 0.2 concatenate.201
  32.0 3.1 %collective-permute-start.3 = (f32[4,37,128]{2,1,0:T(8,128)S(1)}, f32[4,37,128]{2,1,0:T(8,128)S(1)}, u32[]{:S(2)}, u32[]{:S(2)}) collective-permute-start(f32[4,37,128]{2,1,0:T(8,128)S(1)} %concatenate.201), channel_id=1, source_target_pairs={{0,579},{1,0},{2,1},{3,2},{192,3},{193,192},{194,193},{195,194},{3... | collective-permute-start | bytes 227336 | tf_op jit(solution)/shard_map/ppermute | solution.py:33
  35.2 0.2 concatenate.199
  35.4 2.4 %collective-permute-start.2 = (f32[4,39,128]{2,1,0:T(8,128)S(1)}, f32[4,39,128]{2,1,0:T(8,128)S(1)}, u32[]{:S(2)}, u32[]{:S(2)}) collective-permute-start(f32[4,39,128]{2,1,0:T(8,128)S(1)} %concatenate.199), channel_id=1, source_target_pairs={{0,1},{1,2},{2,3},{3,192},{192,193},{193,194},{194,195},{195,384},... | collective-permute-start | bytes 239624 | tf_op jit(solution)/shard_map/ppermute | solution.py:33
  37.8 0.2 collective-permute-done.3
  38.2 4.7 %collective-permute-done.2 = f32[4,39,128]{2,1,0:T(8,128)S(1)} collective-permute-done((f32[4,39,128]{2,1,0:T(8,128)S(1)}, f32[4,39,128]{2,1,0:T(8,128)S(1)}, u32[]{:S(2)}, u32[]{:S(2)}) %collective-permute-start.2) | collective-permute-done | bytes 79904 | tf_op jit(solution)/shard_map/ppermute | solution.py:33
  43.1 0.3 maximum_subtract_fusion.2
  43.4 0.2 select_select_fusion.3
  43.5 0.3 fusion.25
  44.0 0.1 maximum_subtract_fusion
  44.1 0.2 select_select_fusion.1
  44.3 0.2 fusion.9
  44.5 0.2 fusion.22
  44.8 0.2 fusion.1
  45.0 0.1 fusion.111
  45.1 0.2 fusion.136
  45.5 0.1 fusion.146
  45.6 0.1 select_add_fusion.1
  45.8 1.9 %collective-permute-start.5 = (f32[12,38,128]{2,0,1:T(8,128)S(1)}, f32[12,38,128]{2,0,1:T(8,128)S(1)}, u32[]{:S(2)}, u32[]{:S(2)}) collective-permute-start(f32[12,38,128]{2,0,1:T(8,128)S(1)} %constant_dynamic-update-slice_fusion.8), channel_id=1, source_target_pairs={{0,4},{4,8},{8,12},{12,16},{16,20},{20,24},{24,28},{28,32},{32,36}... | collective-permute-start | bytes 700424 | tf_op jit(solution)/shard_map/ppermute | solution.py:33
  47.8 4.1 %collective-permute-start.6 = (f32[4,36,128]{2,1,0:T(8,128)S(1)}, f32[4,36,128]{2,1,0:T(8,128)S(1)}, u32[]{:S(2)}, u32[]{:S(2)}) collective-permute-start(f32[4,36,128]{2,1,0:T(8,128)S(1)} %pad_maximum_fusion.2), channel_id=1, source_target_pairs={{0,579},{1,0},{2,1},{3,2},{192,3},{193,192},{194,193},{195,194},{3... | collective-permute-start | bytes 221192 | tf_op jit(solution)/shard_map/ppermute | solution.py:33
  51.9 11.7 %collective-permute-start.4 = (f32[12,36,128]{2,0,1:T(8,128)S(1)}, f32[12,36,128]{2,0,1:T(8,128)S(1)}, u32[]{:S(2)}, u32[]{:S(2)}) collective-permute-start(f32[12,36,128]{2,0,1:T(8,128)S(1)} %pad_maximum_fusion), channel_id=1, source_target_pairs={{0,188},{4,0},{8,4},{12,8},{16,12},{20,16},{24,20},{28,24},{32,28}... | collective-permute-start | bytes 663560 | tf_op jit(solution)/shard_map/ppermute | solution.py:33
  63.7 0.2 concatenate.232
  63.9 1.9 %collective-permute-start.7 = (f32[4,38,128]{2,1,0:T(8,128)S(1)}, f32[4,38,128]{2,1,0:T(8,128)S(1)}, u32[]{:S(2)}, u32[]{:S(2)}) collective-permute-start(f32[4,38,128]{2,1,0:T(8,128)S(1)} %concatenate.232), channel_id=1, source_target_pairs={{0,1},{1,2},{2,3},{3,192},{192,193},{193,194},{194,195},{195,384},... | collective-permute-start | bytes 233480 | tf_op jit(solution)/shard_map/ppermute | solution.py:33
  65.9 2.6 %collective-permute-done.7 = f32[4,38,128]{2,1,0:T(8,128)S(1)} collective-permute-done((f32[4,38,128]{2,1,0:T(8,128)S(1)}, f32[4,38,128]{2,1,0:T(8,128)S(1)}, u32[]{:S(2)}, u32[]{:S(2)}) %collective-permute-start.7) | collective-permute-done | bytes 77856 | tf_op jit(solution)/shard_map/ppermute | solution.py:33
  68.8 0.3 maximum_subtract_fusion.3
  69.1 0.2 select_select_fusion.2
  69.3 0.1 stack.102
  69.4 0.3 fusion.17
  69.7 3.6 %collective-permute-done.4 = f32[12,36,128]{2,0,1:T(8,128)S(1)} collective-permute-done((f32[12,36,128]{2,0,1:T(8,128)S(1)}, f32[12,36,128]{2,0,1:T(8,128)S(1)}, u32[]{:S(2)}, u32[]{:S(2)}) %collective-permute-start.4) | collective-permute-done | bytes 221216 | tf_op jit(solution)/shard_map/ppermute | solution.py:33
  73.3 0.1 maximum_subtract_fusion.1
  73.4 0.2 select_select_fusion
  73.7 0.2 fusion.4
  73.9 0.2 fusion.14
  74.1 0.1 fusion.138
  74.2 0.1 fusion.109
  74.3 0.2 fusion
  74.6 0.1 stack.100
  74.8 0.1 stack.99
  74.9 0.1 stack.101
  75.0 0.1 maximum_bitcast_fusion
  75.1 0.3 copy.147
  75.4 0.9 reshape.193
  76.3 4.4 %all-to-all-start.1 = ((f32[4,4,12,128]{3,1,2,0:T(4,128)}), f32[4,4,12,128]{3,1,2,0:T(4,128)S(1)}, u32[]{:S(2)}, u32[]{:S(2)}) async-start(f32[4,4,12,128]{3,1,2,0:T(4,128)} %reshape.193), calls=%async_computation.1 | async-start | bytes 196608 | tf_op jit(solution)/shard_map/all_to_all | solution.py:115
  80.7 0.2 fusion.137
  81.0 0.9 %copy.153 = f32[4,12,17,128]{3,0,2,1:T(4,128)} copy(f32[4,12,17,128]{3,1,0,2:T(8,128)S(1)} %maximum_multiply_fusion.1) | data formatting | bytes 835584
  81.9 2.1 %all-to-all-done.1 = f32[4,4,12,128]{3,1,2,0:T(4,128)S(1)} async-done(((f32[4,4,12,128]{3,1,2,0:T(4,128)}), f32[4,4,12,128]{3,1,2,0:T(4,128)S(1)}, u32[]{:S(2)}, u32[]{:S(2)}) %all-to-all-start.1) | async-done | bytes 98336 | tf_op jit(solution)/shard_map/all_to_all | solution.py:115
  84.0 0.2 reshape.194
  84.3 0.3 fusion.149
  84.6 0.7 copy.149
  85.3 0.7 copy.150
  86.0 0.7 copy.151
  86.8 0.7 copy.152
  (107 shorter events, 1.9 us)
Async XLA Ops:
  0.6 16.3 %copy-start = (s32[4,48]{1,0:T(4,128)S(1)}, s32[4,48]{1,0:T(4,128)}, u32[]{:S(2)}) copy-start(s32[4,48]{1,0:T(4,128)} %param.13) | copy-start | bytes 2308
  1.9 14.7 %copy-start.1 = (f32[4,12,17,128]{3,0,2,1:T(4,128)S(1)}, f32[4,12,17,128]{3,0,2,1:T(4,128)}, u32[]{:S(2)}) copy-start(f32[4,12,17,128]{3,0,2,1:T(4,128)} %param.11) | copy-start | bytes 1253380
  2.8 17.1 %all-to-all-start = ((f32[4,4,12,128]{3,1,2,0:T(4,128)}), f32[4,4,12,128]{3,1,2,0:T(4,128)S(1)}, u32[]{:S(2)}, u32[]{:S(2)}) async-start(f32[4,4,12,128]{3,1,2,0:T(4,128)} %bitcast.4), calls=%async_computation | async-start | bytes 196608 | tf_op jit(solution)/shard_map/all_to_all | solution.py:103
  16.9 0.7 copy-start.2
  20.8 23.1 %collective-permute-start = (f32[12,39,128]{2,0,1:T(8,128)S(1)}, f32[12,39,128]{2,0,1:T(8,128)S(1)}, u32[]{:S(2)}, u32[]{:S(2)}) collective-permute-start(f32[12,39,128]{2,0,1:T(8,128)S(1)} %get-tuple-element.126), channel_id=1, source_target_pairs={{0,4},{4,8},{8,12},{12,16},{16,20},{20,24},{24,28},{28,32},{32,36}... | collective-permute-start | bytes 718856 | tf_op jit(solution)/shard_map/ppermute | solution.py:33
  22.8 21.1 %collective-permute-start.1 = (f32[12,37,128]{2,0,1:T(8,128)S(1)}, f32[12,37,128]{2,0,1:T(8,128)S(1)}, u32[]{:S(2)}, u32[]{:S(2)}) collective-permute-start(f32[12,37,128]{2,0,1:T(8,128)S(1)} %get-tuple-element.125), channel_id=1, source_target_pairs={{0,188},{4,0},{8,4},{12,8},{16,12},{20,16},{24,20},{28,24},{32,28}... | collective-permute-start | bytes 681992 | tf_op jit(solution)/shard_map/ppermute | solution.py:33
  32.0 6.1 %collective-permute-start.3 = (f32[4,37,128]{2,1,0:T(8,128)S(1)}, f32[4,37,128]{2,1,0:T(8,128)S(1)}, u32[]{:S(2)}, u32[]{:S(2)}) collective-permute-start(f32[4,37,128]{2,1,0:T(8,128)S(1)} %concatenate.201), channel_id=1, source_target_pairs={{0,579},{1,0},{2,1},{3,2},{192,3},{193,192},{194,193},{195,194},{3... | collective-permute-start | bytes 227336 | tf_op jit(solution)/shard_map/ppermute | solution.py:33
  35.4 7.4 %collective-permute-start.2 = (f32[4,39,128]{2,1,0:T(8,128)S(1)}, f32[4,39,128]{2,1,0:T(8,128)S(1)}, u32[]{:S(2)}, u32[]{:S(2)}) collective-permute-start(f32[4,39,128]{2,1,0:T(8,128)S(1)} %concatenate.199), channel_id=1, source_target_pairs={{0,1},{1,2},{2,3},{3,192},{192,193},{193,194},{194,195},{195,384},... | collective-permute-start | bytes 239624 | tf_op jit(solution)/shard_map/ppermute | solution.py:33
  45.8 27.5 %collective-permute-start.5 = (f32[12,38,128]{2,0,1:T(8,128)S(1)}, f32[12,38,128]{2,0,1:T(8,128)S(1)}, u32[]{:S(2)}, u32[]{:S(2)}) collective-permute-start(f32[12,38,128]{2,0,1:T(8,128)S(1)} %constant_dynamic-update-slice_fusion.8), channel_id=1, source_target_pairs={{0,4},{4,8},{8,12},{12,16},{16,20},{20,24},{24,28},{28,32},{32,36}... | collective-permute-start | bytes 700424 | tf_op jit(solution)/shard_map/ppermute | solution.py:33
  47.8 18.0 %collective-permute-start.6 = (f32[4,36,128]{2,1,0:T(8,128)S(1)}, f32[4,36,128]{2,1,0:T(8,128)S(1)}, u32[]{:S(2)}, u32[]{:S(2)}) collective-permute-start(f32[4,36,128]{2,1,0:T(8,128)S(1)} %pad_maximum_fusion.2), channel_id=1, source_target_pairs={{0,579},{1,0},{2,1},{3,2},{192,3},{193,192},{194,193},{195,194},{3... | collective-permute-start | bytes 221192 | tf_op jit(solution)/shard_map/ppermute | solution.py:33
  51.9 21.4 %collective-permute-start.4 = (f32[12,36,128]{2,0,1:T(8,128)S(1)}, f32[12,36,128]{2,0,1:T(8,128)S(1)}, u32[]{:S(2)}, u32[]{:S(2)}) collective-permute-start(f32[12,36,128]{2,0,1:T(8,128)S(1)} %pad_maximum_fusion), channel_id=1, source_target_pairs={{0,188},{4,0},{8,4},{12,8},{16,12},{20,16},{24,20},{28,24},{32,28}... | collective-permute-start | bytes 663560 | tf_op jit(solution)/shard_map/ppermute | solution.py:33
  63.9 4.7 %collective-permute-start.7 = (f32[4,38,128]{2,1,0:T(8,128)S(1)}, f32[4,38,128]{2,1,0:T(8,128)S(1)}, u32[]{:S(2)}, u32[]{:S(2)}) collective-permute-start(f32[4,38,128]{2,1,0:T(8,128)S(1)} %concatenate.232), channel_id=1, source_target_pairs={{0,1},{1,2},{2,3},{3,192},{192,193},{193,194},{194,195},{195,384},... | collective-permute-start | bytes 233480 | tf_op jit(solution)/shard_map/ppermute | solution.py:33
  76.3 7.7 %all-to-all-start.1 = ((f32[4,4,12,128]{3,1,2,0:T(4,128)}), f32[4,4,12,128]{3,1,2,0:T(4,128)S(1)}, u32[]{:S(2)}, u32[]{:S(2)}) async-start(f32[4,4,12,128]{3,1,2,0:T(4,128)} %reshape.193), calls=%async_computation.1 | async-start | bytes 196608 | tf_op jit(solution)/shard_map/all_to_all | solution.py:115

commit v2 on v1

--- a/solution.py
+++ b/solution.py
@@ -54,6 +54,34 @@
     return cut(flux, 1, n) - cut(flux, 0, n)
 
 
+def advect(q, face_x, face_y):
+    return q[2:-2, 2:-2] - ADV_STEP * (
+        face_flux(q[:, 2:-2], face_x, 0) + face_flux(q[2:-2], face_y, 1)
+    )
+
+
+def dynamics(temp, salt, wet, east, north):
+    open_x = wet[:-1] * wet[1:]
+    open_y = wet[:, :-1] * wet[:, 1:]
+    inner = wet[1:-1, 1:-1]
+
+    def diffuse(q):
+        step_x = (open_x * (q[1:] - q[:-1]))[:, 1:-1]
+        step_y = (open_y * (q[:, 1:] - q[:, :-1]))[1:-1]
+        lap = step_x[1:] - step_x[:-1] + step_y[:, 1:] - step_y[:, :-1]
+        return inner * (q[1:-1, 1:-1] + DIFFUSION * lap)
+
+    buoy = temp - HALINE * salt
+    face_x = open_x * (
+        TURN_COS * east[:-1] + TURN_SIN * north[:-1] - PRESSURE * (buoy[1:] - buoy[:-1])
+    )
+    face_y = open_y * (
+        -TURN_SIN * east[:, :-1] + TURN_COS * north[:, :-1]
+        - PRESSURE * (buoy[:, 1:] - buoy[:, :-1])
+    )
+    return diffuse(temp), diffuse(salt), face_x, face_y
+
+
 def react(tracer, temper, wetness):
     depth = tracer.shape[-1]
     upper_rows = lax.broadcasted_iota(jnp.int32, (depth, depth), 0)
@@ -118,82 +146,83 @@
     return tuple(packed[:, :, i] for i in range(nf))
 
 
-def rims(axis, name, tracer, ahead, behind):
-    n = tracer.shape[axis]
-
-    def gather(lines, fields, edge):
-        parts = [lax.index_in_dim(tracer, k, axis, keepdims=False) for k in lines]
-        parts += [lax.index_in_dim(f, edge, axis, keepdims=False)[:, None] for f in fields]
-        return jnp.concatenate(parts, axis=1)
-
-    def open_up(block):
-        lines = jnp.stack([block[:, :NTR], block[:, NTR : 2 * NTR]], axis=axis)
-        rest = [
-            jnp.expand_dims(block[:, k], axis) for k in range(2 * NTR, block.shape[1])
-        ]
-        return lines, rest
-
-    low = ring_send(gather((n - 2, n - 1), ahead, n - 1), name, 1)
-    high = ring_send(gather((0, 1), behind, 0), name, -1)
-    return open_up(low), open_up(high)
+def flat(*pieces):
+    return jnp.concatenate([p.reshape(-1, p.shape[-1]) for p in pieces], axis=0)
+
+
+def unflat(block, *shapes):
+    out, at = [], 0
+    for shape in shapes:
+        size = 1
+        for length in shape[:-1]:
+            size *= length
+        out.append(block[at : at + size].reshape(shape))
+        at += size
+    return out
 
 
 def on_device(temp, salt, east, north, tracer, mask, bottom):
-    levels = tracer.shape[3]
-    tile_rows = tracer.shape[1]
-    row_start = lax.axis_index("gy") * tile_rows
-    mask_tile = lax.dynamic_slice_in_dim(mask, row_start, tile_rows, 1)
-    bottom_tile = lax.dynamic_slice_in_dim(bottom, row_start, tile_rows, 1)
+    nx, ny, ntr, levels = tracer.shape
+    row_start = lax.axis_index("gy") * ny
+    mask_tile = lax.dynamic_slice_in_dim(mask, row_start, ny, 1)
+    bottom_tile = lax.dynamic_slice_in_dim(bottom, row_start, ny, 1)
     column_levels = lax.broadcasted_iota(jnp.int32, (1, 1, levels), 2)
     wet = ((mask_tile[:, :, None] > 0) & (column_levels < bottom_tile[:, :, None])).astype(
         jnp.float32
     )
+    west = ring_send(tracer, "gx", 1)
+    east_t = ring_send(tracer, "gx", -1)
+
     temp, salt, east, north = to_columns([temp, salt, east, north])
+    state = jnp.stack([temp, salt, wet, east, north], axis=0)
+
+    y_shapes = ((nx, 4, ntr, levels), (5, nx, 3, levels))
+    south, s_state = unflat(
+        ring_send(flat(tracer[:, ny - 4 :], state[:, :, ny - 3 :]), ROWS, 1), *y_shapes
+    )
+    north_t, n_state = unflat(
+        ring_send(flat(tracer[:, :4], state[:, :, :3]), ROWS, -1), *y_shapes
+    )
+    state = jnp.concatenate([s_state, state, n_state], axis=2)
+
+    x_shapes = ((2, 2, ntr, levels), (2, 2, ntr, levels), (5, 3, ny + 4, levels))
+    sw, nw, w_state = unflat(
+        ring_send(
+            flat(south[nx - 2 :, 2:], north_t[nx - 2 :, :2], state[:, nx - 3 :, 1:-1]), "gx", 1
+        ),
+        *x_shapes,
+    )
+    se, ne, e_state = unflat(
+        ring_send(flat(south[:2, 2:], north_t[:2, :2], state[:, :3, 1:-1]), "gx", -1), *x_shapes
+    )
+    pad = ((0, 0), (0, 0), (1, 1), (0, 0))
+    state = jnp.concatenate([jnp.pad(w_state, pad), state, jnp.pad(e_state, pad)], axis=1)
+    corner = [
+        jnp.pad(sw, ((2, 0), (2, 0), (0, 0), (0, 0))),
+        jnp.pad(se, ((0, 2), (2, 0), (0, 0), (0, 0))),
+        jnp.pad(nw, ((2, 0), (0, 2), (0, 0), (0, 0))),
+        jnp.pad(ne, ((0, 2), (0, 2), (0, 0), (0, 0))),
+    ]
+    tracer = jnp.concatenate(
+        [
+            jnp.concatenate([corner[0], south, corner[1]], axis=0),
+            jnp.concatenate([west, tracer, east_t], axis=0),
+            jnp.concatenate([corner[2], north_t, corner[3]], axis=0),
+        ],
+        axis=1,
+    )
+    temp, salt, wet, east, north = [state[i] for i in range(5)]
     for step in range(STEPS):
-        extra = [wet] if step == 0 else []
-        ahead = [temp, salt, east, north] + extra
-        behind = [temp, salt] + extra
-        (t_west, f_west), (t_east, f_east) = rims(0, "gx", tracer, ahead, behind)
-        (t_south, f_south), (t_north, f_north) = rims(1, ROWS, tracer, ahead, behind)
-        if step == 0:
-            wet_x = jnp.concatenate([f_west[4], wet, f_east[2]], axis=0)
-            wet_y = jnp.concatenate([f_south[4], wet, f_north[2]], axis=1)
-            open_x = wet_x[:-1] * wet_x[1:]
-            open_y = wet_y[:, :-1] * wet_y[:, 1:]
-
-        def laplace(q, qx, qy):
-            return (
-                open_x[1:] * (qx[2:] - q)
-                - open_x[:-1] * (q - qx[:-2])
-                + open_y[:, 1:] * (qy[:, 2:] - q)
-                - open_y[:, :-1] * (q - qy[:, :-2])
-            )
-
-        temp_x = jnp.concatenate([f_west[0], temp, f_east[0]], axis=0)
-        salt_x = jnp.concatenate([f_west[1], salt, f_east[1]], axis=0)
-        temp_y = jnp.concatenate([f_south[0], temp, f_north[0]], axis=1)
-        salt_y = jnp.concatenate([f_south[1], salt, f_north[1]], axis=1)
-        buoy_x = temp_x - HALINE * salt_x
-        buoy_y = temp_y - HALINE * salt_y
-        halfway = wet * (temp + DIFFUSION * laplace(temp, temp_x, temp_y))
-        salt = wet * (salt + DIFFUSION * laplace(salt, salt_x, salt_y))
-        face_x = open_x * (
-            TURN_COS * jnp.concatenate([f_west[2], east], axis=0)
-            + TURN_SIN * jnp.concatenate([f_west[3], north], axis=0)
-            - PRESSURE * (buoy_x[1:] - buoy_x[:-1])
-        )
-        face_y = open_y * (
-            -TURN_SIN * jnp.concatenate([f_south[2], east], axis=1)
-            + TURN_COS * jnp.concatenate([f_south[3], north], axis=1)
-            - PRESSURE * (buoy_y[:, 1:] - buoy_y[:, :-1])
-        )
-        east, north = face_x[1:], face_y[:, 1:]
-        moved = tracer - ADV_STEP * (
-            face_flux(jnp.concatenate([t_west, tracer, t_east], axis=0), face_x, 0)
-            + face_flux(jnp.concatenate([t_south, tracer, t_north], axis=1), face_y, 1)
-        )
-        tracer, heat = react(moved, halfway, wet)
+        halfway, salt, east, north = dynamics(temp, salt, wet, east, north)
+        east, north = east[:, 1:-1], north[1:-1]
+        wet = wet[1:-1, 1:-1]
+        tracer, heat = react(advect(tracer, east, north), halfway, wet)
         temp = halfway + heat
+        east, north = east[1:], north[:, 1:]
+        if step + 1 < STEPS:
+            temp, salt, wet, east, north = [
+                f[1:-1, 1:-1] for f in (temp, salt, wet, east, north)
+            ]
     temp, salt, east, north = to_levels([temp, salt, east, north])
     return temp, salt, east, north, tracer
 

time: 88.1 us -> 85.3 us (0.968)
  starting transfers between devices: 54.3 us -> 47 us
  other arithmetic: 5.54 us -> 8.97 us
  local copies, waits for them, and re-layouts: 10.4 us -> 12 us
    ppermute x8 -> x6, starting transfers between devices: 36.1 us -> 25.2 us  [ring_send(): lax.ppermute(block, axis, [(i, (i + step) % count) for i in range(count)])]
    all_to_all x1, starting transfers between devices: 4.39 us -> 8.05 us  [to_levels(): lax.all_to_all(packed, 'gy', split_axis=0, concat_axis=0, tiled=True)]
    concatenate x2 -> x7, other arithmetic: 0.04 us -> 2.1 us  [the longest x1 1.91 us: on_device(): jnp.concatenate([jnp.concatenate([corner[0], south, corner[1]], axis=0),...]
    ppermute x8 -> x6, waiting for transfers between devices: 11.1 us -> 9.54 us  [ring_send(): lax.ppermute(block, axis, [(i, (i + step) % count) for i in range(count)])]
    slice x24 -> x19, local copies, waits for them, and re-layouts: 0.63 us -> 1.93 us  [the longest x8 1.78 us: unflat(): out.append(block[at:at + size].reshape(shape))]
    ppermute x0 -> x2, local copies, waits for them, and re-layouts: none -> 1.12 us  [ring_send(): lax.ppermute(block, axis, [(i, (i + step) % count) for i in range(count)])]
    all_to_all x1, waiting for transfers between devices: 1.94 us -> 3.05 us  [to_columns(): lax.all_to_all(packed, 'gy', split_axis=0, concat_axis=0, tiled=True)]
    unnamed x28 -> x19, local copies, waits for them, and re-layouts: 4.58 us -> 4.56 us
  transfers between devices with their start and end apart: 10 -> 8, of which waited for: 6 -> 3; matrix products, arithmetic and copies ran while one was open for 6% -> 4% of each run, Pallas kernels for 0% -> 0%
where the time goes in v2:
time: 85.3 us; the launch traced here: 84.7 us
  starting transfers between devices  47 us (55%)
  waiting for transfers between devices  14.7 us (17%)
  local copies, waits for them, and re-layouts  12 us (14%)
  other arithmetic  8.97 us (11%)
  between operations  1.52 us (2%)
    ppermute x6, starting transfers between devices, ring_send(): lax.ppermute(block, axis, [(i, (i + step) % count) for i in range(count)])  25.2 us
    all_to_all x1, starting transfers between devices, to_columns(): lax.all_to_all(packed, 'gy', split_axis=0, concat_axis=0, tiled=True)  13.8 us
    ppermute x6, waiting for transfers between devices, ring_send(): lax.ppermute(block, axis, [(i, (i + step) % count) for i in range(count)])  9.54 us
    all_to_all x1, starting transfers between devices, to_levels(): lax.all_to_all(packed, 'gy', split_axis=0, concat_axis=0, tiled=True)  8.05 us
    unnamed x19, local copies, waits for them, and re-layouts  4.56 us
    all_to_all x1, waiting for transfers between devices, to_columns(): lax.all_to_all(packed, 'gy', split_axis=0, concat_axis=0, tiled=True)  3.05 us
    all_to_all x1, waiting for transfers between devices, to_levels(): lax.all_to_all(packed, 'gy', split_axis=0, concat_axis=0, tiled=True)  2.1 us
    concatenate x1, other arithmetic, on_device(): jnp.concatenate([jnp.concatenate([corner[0], south, corner[1]], axis=0),...  1.91 us
  transfers between devices with their start and end apart: 8, of which 3 were waited for; matrix products, arithmetic and copies ran while one was open for 4% of the time, Pallas kernels for 0%

profile of v2, /device:TPU:1, one launch (start us, length us, event | category | flops | bytes accessed | tf_op | source)
XLA Modules:
  0.0 84.7 jit_solution(4722522965855990485)
XLA Ops:
  0.7 1.0 %pad_maximum_fusion = f32[4,48,4,32]{1,3,0,2:T(8,128)S(1)} fusion(f32[4,48,1,32]{1,3,0,2:T(8,128)} %bitcast.126, f32[4,48,1,32]{1,3,0,2:T(8,128)} %bitcast.127, f32[4,48,1,32]{1,3,0,2:T(8,128)} %bitcast.128, f32[4,48,1,32]{1,3,0,2:T(8,128)} %bitcast.129), kind=kLoop, calls=%fused_computation.86 | loop fusion | flops 73728 | bytes 196608 | tf_op jit(solution)/shard_map/stack | solution.py:128
  1.7 0.3 copy.45
  2.0 0.9 %reshape.264 = f32[4,4,12,128]{3,0,2,1:T(4,128)} reshape(f32[4,48,4,32]{3,2,0,1:T(4,128)S(1)} %copy.45) | data formatting | bytes 196608 | tf_op jit(solution)/shard_map/reshape | solution.py:130
  2.8 13.8 %all-to-all-start = ((f32[4,4,12,128]{3,1,2,0:T(4,128)}), f32[4,4,12,128]{3,1,2,0:T(4,128)S(1)}, u32[]{:S(2)}, u32[]{:S(2)}) async-start(f32[4,4,12,128]{3,1,2,0:T(4,128)} %bitcast.4), calls=%async_computation | async-start | bytes 196608 | tf_op jit(solution)/shard_map/all_to_all | solution.py:131
  16.7 0.1 dynamic-slice_compare_fusion
  16.8 0.1 constant_dynamic-slice_fusion
  16.9 3.1 %all-to-all-done = f32[4,4,12,128]{3,1,2,0:T(4,128)S(1)} async-done(((f32[4,4,12,128]{3,1,2,0:T(4,128)}), f32[4,4,12,128]{3,1,2,0:T(4,128)S(1)}, u32[]{:S(2)}, u32[]{:S(2)}) %all-to-all-start) | async-done | bytes 98336 | tf_op jit(solution)/shard_map/all_to_all | solution.py:131
  20.0 0.2 reshape.265
  20.2 0.3 copy.72
  20.5 0.2 reshape.294
  20.7 0.1 convert_dynamic-update-slice_fusion
  20.9 2.8 %collective-permute-start = (f32[332,128]{1,0:T(8,128)S(1)}, f32[332,128]{1,0:T(8,128)S(1)}, u32[]{:S(2)}, u32[]{:S(2)}) collective-permute-start(f32[332,128]{1,0:T(8,128)S(1)} %pad_maximum_fusion.4), channel_id=1, source_target_pairs={{0,1},{1,2},{2,3},{3,192},{192,193},{193,194},{194,195},{195,384},... | collective-permute-start | bytes 509960 | tf_op jit(solution)/shard_map/ppermute | solution.py:33
  23.7 2.0 %collective-permute-start.1 = (f32[332,128]{1,0:T(8,128)S(1)}, f32[332,128]{1,0:T(8,128)S(1)}, u32[]{:S(2)}, u32[]{:S(2)}) collective-permute-start(f32[332,128]{1,0:T(8,128)S(1)} %pad_maximum_fusion.5), channel_id=1, source_target_pairs={{0,579},{1,0},{2,1},{3,2},{192,3},{193,192},{194,193},{195,194},{3... | collective-permute-start | bytes 509960 | tf_op jit(solution)/shard_map/ppermute | solution.py:33
  25.7 1.9 %collective-permute-start.4 = (f32[4,12,17,128]{3,0,2,1:T(4,128)S(1)}, f32[4,12,17,128]{3,0,2,1:T(4,128)}, u32[]{:S(2)}, u32[]{:S(2)}) collective-permute-start(f32[4,12,17,128]{3,0,2,1:T(4,128)S(1)} %copy-done.1), channel_id=1, source_target_pairs={{0,4},{4,8},{8,12},{12,16},{16,20},{20,24},{24,28},{28,32},{32,36}... | collective-permute-start | bytes 1253384 | tf_op jit(solution)/shard_map/ppermute | solution.py:33
  27.7 9.0 %collective-permute-start.5 = (f32[4,12,17,128]{3,0,2,1:T(4,128)S(1)}, f32[4,12,17,128]{3,0,2,1:T(4,128)S(1)}, u32[]{:S(2)}, u32[]{:S(2)}) collective-permute-start(f32[4,12,17,128]{3,0,2,1:T(4,128)S(1)} %copy-done.1), channel_id=1, source_target_pairs={{0,188},{4,0},{8,4},{12,8},{16,12},{20,16},{24,20},{28,24},{32,28}... | collective-permute-start | bytes 1253384 | tf_op jit(solution)/shard_map/ppermute | solution.py:33
  37.1 1.9 %collective-permute-start.2 = (f32[376,128]{1,0:T(8,128)S(1)}, f32[376,128]{1,0:T(8,128)S(1)}, u32[]{:S(2)}, u32[]{:S(2)}) collective-permute-start(f32[376,128]{1,0:T(8,128)S(1)} %pad_maximum_fusion.2), channel_id=1, source_target_pairs={{0,4},{4,8},{8,12},{12,16},{16,20},{20,24},{24,28},{28,32},{32,36}... | collective-permute-start | bytes 577544 | tf_op jit(solution)/shard_map/ppermute | solution.py:33
  39.0 7.6 %collective-permute-start.3 = (f32[376,128]{1,0:T(8,128)S(1)}, f32[376,128]{1,0:T(8,128)S(1)}, u32[]{:S(2)}, u32[]{:S(2)}) collective-permute-start(f32[376,128]{1,0:T(8,128)S(1)} %pad_maximum_fusion.3), channel_id=1, source_target_pairs={{0,188},{4,0},{8,4},{12,8},{16,12},{20,16},{24,20},{28,24},{32,28}... | collective-permute-start | bytes 577544 | tf_op jit(solution)/shard_map/ppermute | solution.py:33
  46.8 1.1 %copy.55 = f32[4,12,17,128]{3,1,0,2:T(8,128)S(1)} copy(f32[4,12,17,128]{3,0,2,1:T(4,128)} %collective-permute-done.4) | data formatting | bytes 835584 | tf_op jit(solution)/shard_map/ppermute | solution.py:33
  47.9 9.5 %collective-permute-done.2 = f32[376,128]{1,0:T(8,128)S(1)} collective-permute-done((f32[376,128]{1,0:T(8,128)S(1)}, f32[376,128]{1,0:T(8,128)S(1)}, u32[]{:S(2)}, u32[]{:S(2)}) %collective-permute-start.2) | collective-permute-done | bytes 192544 | tf_op jit(solution)/shard_map/ppermute | solution.py:33
  57.5 0.6 copy-done.2
  58.2 0.1 select_maximum_fusion.4
  58.3 0.9 %fusion.119 = (f32[68,128]{1,0:T(8,128)S(1)}, f32[68,128]{1,0:T(8,128)S(1)}) fusion(f32[376,128]{1,0:T(8,128)} %copy-done.2), kind=kLoop, calls=%fused_computation.256 | loop fusion | bytes 139264 | tf_op jit(solution)/shard_map/slice | solution.py:159
  59.3 0.9 %fusion.120 = (f32[68,128]{1,0:T(8,128)S(1)}, f32[68,128]{1,0:T(8,128)S(1)}) fusion(f32[376,128]{1,0:T(8,128)} %copy-done.3), kind=kLoop, calls=%fused_computation.257 | loop fusion | bytes 139264 | tf_op jit(solution)/shard_map/slice | solution.py:159
  60.2 1.9 %fusion = f32[12,20,17,128]{3,1,0,2:T(8,128)S(1)} fusion(f32[2,2,17,128]{3,1,0,2:T(2,128)S(1)} %copy.59, f32[2,2,17,128]{3,1,0,2:T(2,128)S(1)} %copy.58, f32[2,2,17,128]{3,1,0,2:T(2,128)S(1)} %copy.53, f32[2,2,17,128]{3,1,0,2:T(2,128)S(1)} %copy.52, f32[4,4,17,128]{3,1,0,2:T(4,128)S(1)} %copy.60, f32[4,12,17,128]{3,1,0,2:T(8,128)S(1)} %copy.57, ...), kind=kLoop, calls=%fused_computation.1 | loop fusion | flops 12533760 | bytes 3760128 | tf_op jit(solution)/shard_map/concatenate | solution.py:206
  62.1 0.2 slice_subtract_fusion.1
  62.3 0.2 slice_subtract_fusion
  62.6 0.3 select_select_fusion.1
  62.9 0.1 fusion.39
  63.0 0.5 select_select_fusion
  63.5 0.4 fusion.13
  64.0 0.7 fusion.8
  64.7 0.5 fusion.19
  65.2 0.2 fusion.112
  65.4 0.2 fusion.16
  65.6 0.1 fusion.57
  65.6 0.4 fusion.109
  66.1 0.1 maximum_multiply_fusion
  66.1 0.1 slice_subtract_fusion.4
  66.3 0.1 slice_subtract_fusion.6
  66.6 0.2 select_select_fusion.2
  66.8 0.2 select_select_fusion.3
  67.0 0.2 fusion.23
  67.2 0.2 fusion.31
  67.4 0.2 fusion.28
  67.6 0.1 fusion.110
  67.8 0.2 multiply_add_fusion.7
  68.0 0.1 stack.40
  68.2 0.1 stack.41
  68.3 0.1 stack.42
  68.4 0.1 stack.43
  68.5 0.1 maximum_bitcast_fusion
  68.7 0.3 copy.65
  68.9 0.9 %reshape.286 = f32[4,4,12,128]{3,1,2,0:T(4,128)} reshape(f32[4,4,12,4,32]{4,3,1,2,0:T(4,128)S(1)} %copy.65) | data formatting | bytes 196608 | tf_op jit(solution)/shard_map/reshape | solution.py:142
  69.8 8.1 %all-to-all-start.1 = ((f32[4,4,12,128]{3,1,2,0:T(4,128)}), f32[4,4,12,128]{3,1,2,0:T(4,128)S(1)}, u32[]{:S(2)}, u32[]{:S(2)}) async-start(f32[4,4,12,128]{3,1,2,0:T(4,128)} %reshape.286), calls=%async_computation.1 | async-start | bytes 196608 | tf_op jit(solution)/shard_map/all_to_all | solution.py:143
  77.8 0.2 fusion.108
  78.2 0.9 %copy.71 = f32[4,12,17,128]{3,0,2,1:T(4,128)} copy(f32[4,12,17,128]{3,1,0,2:T(8,128)S(1)} %maximum_multiply_fusion.1) | data formatting | bytes 835584
  79.1 2.1 %all-to-all-done.1 = f32[4,4,12,128]{3,1,2,0:T(4,128)S(1)} async-done(((f32[4,4,12,128]{3,1,2,0:T(4,128)}), f32[4,4,12,128]{3,1,2,0:T(4,128)S(1)}, u32[]{:S(2)}, u32[]{:S(2)}) %all-to-all-start.1) | async-done | bytes 98336 | tf_op jit(solution)/shard_map/all_to_all | solution.py:143
  81.2 0.2 reshape.287
  81.4 0.1 copy.66
  81.5 0.3 fusion.115
  81.8 0.7 copy.67
  82.5 0.7 copy.68
  83.2 0.7 copy.69
  83.9 0.7 copy.70
  (83 shorter events, 1.4 us)
Async XLA Ops:
  0.6 16.2 %copy-start = (s32[4,48]{1,0:T(4,128)S(1)}, s32[4,48]{1,0:T(4,128)}, u32[]{:S(2)}) copy-start(s32[4,48]{1,0:T(4,128)} %param.13) | copy-start | bytes 2308
  0.6 16.0 %copy-start.1 = (f32[4,12,17,128]{3,0,2,1:T(4,128)S(1)}, f32[4,12,17,128]{3,0,2,1:T(4,128)}, u32[]{:S(2)}) copy-start(f32[4,12,17,128]{3,0,2,1:T(4,128)} %param.11) | copy-start | bytes 1253380
  0.7 16.0 %copy-start.4 = (s32[4,48]{1,0:T(4,128)S(1)}, s32[4,48]{1,0:T(4,128)}, u32[]{:S(2)}) copy-start(s32[4,48]{1,0:T(4,128)} %param.12) | copy-start | bytes 2308
  2.8 17.1 %all-to-all-start = ((f32[4,4,12,128]{3,1,2,0:T(4,128)}), f32[4,4,12,128]{3,1,2,0:T(4,128)S(1)}, u32[]{:S(2)}, u32[]{:S(2)}) async-start(f32[4,4,12,128]{3,1,2,0:T(4,128)} %bitcast.4), calls=%async_computation | async-start | bytes 196608 | tf_op jit(solution)/shard_map/all_to_all | solution.py:131
  20.9 15.8 %collective-permute-start = (f32[332,128]{1,0:T(8,128)S(1)}, f32[332,128]{1,0:T(8,128)S(1)}, u32[]{:S(2)}, u32[]{:S(2)}) collective-permute-start(f32[332,128]{1,0:T(8,128)S(1)} %pad_maximum_fusion.4), channel_id=1, source_target_pairs={{0,1},{1,2},{2,3},{3,192},{192,193},{193,194},{194,195},{195,384},... | collective-permute-start | bytes 509960 | tf_op jit(solution)/shard_map/ppermute | solution.py:33
  23.7 13.0 %collective-permute-start.1 = (f32[332,128]{1,0:T(8,128)S(1)}, f32[332,128]{1,0:T(8,128)S(1)}, u32[]{:S(2)}, u32[]{:S(2)}) collective-permute-start(f32[332,128]{1,0:T(8,128)S(1)} %pad_maximum_fusion.5), channel_id=1, source_target_pairs={{0,579},{1,0},{2,1},{3,2},{192,3},{193,192},{194,193},{195,194},{3... | collective-permute-start | bytes 509960 | tf_op jit(solution)/shard_map/ppermute | solution.py:33
  25.7 21.0 %collective-permute-start.4 = (f32[4,12,17,128]{3,0,2,1:T(4,128)S(1)}, f32[4,12,17,128]{3,0,2,1:T(4,128)}, u32[]{:S(2)}, u32[]{:S(2)}) collective-permute-start(f32[4,12,17,128]{3,0,2,1:T(4,128)S(1)} %copy-done.1), channel_id=1, source_target_pairs={{0,4},{4,8},{8,12},{12,16},{16,20},{20,24},{24,28},{28,32},{32,36}... | collective-permute-start | bytes 1253384 | tf_op jit(solution)/shard_map/ppermute | solution.py:33
  27.7 20.2 %collective-permute-start.5 = (f32[4,12,17,128]{3,0,2,1:T(4,128)S(1)}, f32[4,12,17,128]{3,0,2,1:T(4,128)S(1)}, u32[]{:S(2)}, u32[]{:S(2)}) collective-permute-start(f32[4,12,17,128]{3,0,2,1:T(4,128)S(1)} %copy-done.1), channel_id=1, source_target_pairs={{0,188},{4,0},{8,4},{12,8},{16,12},{20,16},{24,20},{28,24},{32,28}... | collective-permute-start | bytes 1253384 | tf_op jit(solution)/shard_map/ppermute | solution.py:33
  37.1 20.4 %collective-permute-start.2 = (f32[376,128]{1,0:T(8,128)S(1)}, f32[376,128]{1,0:T(8,128)S(1)}, u32[]{:S(2)}, u32[]{:S(2)}) collective-permute-start(f32[376,128]{1,0:T(8,128)S(1)} %pad_maximum_fusion.2), channel_id=1, source_target_pairs={{0,4},{4,8},{8,12},{12,16},{16,20},{20,24},{24,28},{28,32},{32,36}... | collective-permute-start | bytes 577544 | tf_op jit(solution)/shard_map/ppermute | solution.py:33
  39.0 18.4 %collective-permute-start.3 = (f32[376,128]{1,0:T(8,128)S(1)}, f32[376,128]{1,0:T(8,128)S(1)}, u32[]{:S(2)}, u32[]{:S(2)}) collective-permute-start(f32[376,128]{1,0:T(8,128)S(1)} %pad_maximum_fusion.3), channel_id=1, source_target_pairs={{0,188},{4,0},{8,4},{12,8},{16,12},{20,16},{24,20},{28,24},{32,28}... | collective-permute-start | bytes 577544 | tf_op jit(solution)/shard_map/ppermute | solution.py:33
  57.4 0.7 copy-start.2
  57.4 0.7 copy-start.3
  69.8 11.4 %all-to-all-start.1 = ((f32[4,4,12,128]{3,1,2,0:T(4,128)}), f32[4,4,12,128]{3,1,2,0:T(4,128)S(1)}, u32[]{:S(2)}, u32[]{:S(2)}) async-start(f32[4,4,12,128]{3,1,2,0:T(4,128)} %reshape.286), calls=%async_computation.1 | async-start | bytes 196608 | tf_op jit(solution)/shard_map/all_to_all | solution.py:143

commit v3 on v1

v3 whole, which is shorter than its diff:
```python
import jax
import jax.numpy as jnp
from jax import lax
from jax.experimental import pallas as pl
from jax.experimental.pallas import tpu as pltpu
from jax.sharding import PartitionSpec as P

STEPS = 2
ADV_STEP = 0.1
DIFFUSION = 0.1
TURN_COS = 0.955336489125606
TURN_SIN = 0.29552020666134
PRESSURE = 0.2
HALINE = 0.8
BIO_STEP = 0.5
WATER_ATT = 0.005
CHLORO_ATT = 0.003
HEATING = 20.0
TEMP_RATE = 0.0633
NUTRIENT_HALF = 0.5
PREY_HALF = 0.5
GRAZING = 0.8
PHYTO_LOSS = 0.1
GRAZER_LOSS = 0.15
ASSIMILATE = 0.3
NTR = 17
ROWS = ("grp", "gy")


def ring_send(block, axis, step):
    names = axis if isinstance(axis, tuple) else (axis,)
    count = 1
    for name in names:
        count *= lax.axis_size(name)
    return lax.ppermute(block, axis, [(i, (i + step) % count) for i in range(count)])


def minmod(a, b):
    return jnp.maximum(jnp.minimum(a, b), 0.0) + jnp.minimum(jnp.maximum(a, b), 0.0)


def upwind(face, left, right):
    return face * jnp.where(face > 0, left, right)


def physics_rows(get, rows, put_west, put_east, put_south, put_mid):
    def buoy(row, shift):
        return get(0, row, shift) - HALINE * get(1, row, shift)

    def face_x(row, shift):
        gate = get(2, row, shift) * get(2, row, shift + 1)
        turned = TURN_COS * get(3, row, shift) + TURN_SIN * get(4, row, shift)
        return gate * (turned - PRESSURE * (buoy(row, shift + 1) - buoy(row, shift)))

    def face_y(row):
        gate = get(2, row, 0) * get(2, row + 1, 0)
        turned = TURN_COS * get(4, row, 0) - TURN_SIN * get(3, row, 0)
        return gate * (turned - PRESSURE * (buoy(row + 1, 0) - buoy(row, 0)))

    def body(row, carry):
        put_west(row, face_x(row, -1))
        put_east(row, face_x(row, 0))
        put_south(row, face_y(row - 1))
        wet = get(2, row, 0)
        open_e, open_w = wet * get(2, row, 1), wet * get(2, row, -1)
        open_n, open_s = wet * get(2, row + 1, 0), wet * get(2, row - 1, 0)
        fresh = []
        for f in (0, 1):
            q = get(f, row, 0)
            lap = (
                open_e * (get(f, row, 1) - q)
                - open_w * (q - get(f, row, -1))
                + open_n * (get(f, row + 1, 0) - q)
                - open_s * (q - get(f, row - 1, 0))
            )
            fresh.append(wet * (q + DIFFUSION * lap))
        put_mid(row, *fresh)
        return carry

    lax.fori_loop(0, rows, body, 0)
    put_south(rows, face_y(rows - 1))


def advect_all(src, dst, width, rows, west, east, south):
    def body(t, carry):
        def cell(e, shift=0):
            return src[e, t, 2 + shift : 2 + shift + width, :]

        below, here = cell(1), cell(2)
        d_low = here - below
        left_y = below + 0.5 * minmod(below - cell(0), d_low)
        flux_prev = None
        change_x = None
        q_prev = None
        for e in range(2, rows + 3):
            above = cell(e + 1)
            d_high = above - here
            half = 0.5 * minmod(d_low, d_high)
            flux = upwind(south[e - 2, :width, :], left_y, here - half)
            if flux_prev is not None:
                dst[e - 3, t, :width, :] = q_prev - ADV_STEP * (change_x + (flux - flux_prev))
            if e < rows + 2:
                m2, m1, p1, p2 = cell(e, -2), cell(e, -1), cell(e, 1), cell(e, 2)
                d0, d1, d2, d3 = m1 - m2, here - m1, p1 - here, p2 - p1
                h_m, h_0, h_p = 0.5 * minmod(d0, d1), 0.5 * minmod(d1, d2), 0.5 * minmod(d2, d3)
                change_x = upwind(east[e - 2, :width, :], here + h_0, p1 - h_p) - upwind(
                    west[e - 2, :width, :], m1 + h_m, here - h_0
                )
            flux_prev, q_prev = flux, here
            left_y = here + half
            here, d_low = above, d_high
        return carry

    lax.fori_loop(0, NTR, body, 0)


def absorb_rows(cells, width, rows, absorb):
    def body(row, carry):
        chloro = 0.3 * cells[row, 1, :width, :]
        for c in range(1, 8):
            chloro = chloro + (0.3 + 0.1 * c) * cells[row, 1 + c, :width, :]
        absorb[row, :, :] = WATER_ATT + CHLORO_ATT * jnp.abs(chloro)
        return carry

    lax.fori_loop(0, rows, body, 0)


def dim_light(absorb, light, rows, width):
    depth = absorb.shape[-1]
    above = lax.broadcasted_iota(jnp.int32, (depth, depth), 0)
    level = lax.broadcasted_iota(jnp.int32, (depth, depth), 1)
    upper = jnp.where(above < level, 1.0, jnp.where(above == level, 0.5, 0.0))
    optical = jnp.dot(
        absorb[...].reshape(rows * width, depth),
        upper.astype(jnp.float32),
        precision=lax.Precision.HIGHEST,
        preferred_element_type=jnp.float32,
    )
    light[...] = jnp.exp(-optical).reshape(rows, width, depth)


def react_rows(cells, width, rows, absorb, light, halfway, wetness, put_temp):
    def body(row, carry):
        lit = light[row]
        wet = wetness(row)
        mid = halfway(row)
        nutrient = cells[row, 0, :width, :]
        drive = jnp.exp(TEMP_RATE * mid) * (nutrient / (jnp.abs(nutrient) + NUTRIENT_HALF)) * lit
        change = jnp.zeros_like(nutrient)
        for c in range(8):
            p = cells[row, 1 + c, :width, :]
            z = cells[row, 9 + c, :width, :]
            growth = (0.6 + 0.15 * c) * drive / (lit + (0.1 + 0.1 * c)) * p
            grazed = GRAZING * z * p / (jnp.abs(p) + PREY_HALF)
            change = change + (
                PHYTO_LOSS * p + GRAZER_LOSS * z + (1.0 - ASSIMILATE) * grazed - growth
            )
            cells[row, 1 + c, :width, :] = wet * (
                p + BIO_STEP * (growth - grazed - PHYTO_LOSS * p)
            )
            cells[row, 9 + c, :width, :] = wet * (
                z + BIO_STEP * (ASSIMILATE * grazed - GRAZER_LOSS * z)
            )
        cells[row, 0, :width, :] = wet * (nutrient + BIO_STEP * change)
        put_temp(row, mid + HEATING * absorb[row] * lit * wet)
        return carry

    lax.fori_loop(0, rows, body, 0)


def two_steps(
    own, west, east, south_in, north_in, west_in, east_in, state,
    out, mail,
    src, phys, u_west, u_east, v_south, mid, cells, absorb, light,
    u_west2, u_east2, v_south2, mid2, absorb2, light2, fields,
):
    ny, ntr, nx, depth = own.shape
    ry = ny + 4

    def place(y, carry):
        src[y + 4, :, 0:4, :] = west[y]
        src[y + 4, :, 4:8, :] = own[y]
        src[y + 4, :, 8:12, :] = east[y]
        for f in range(5):
            phys[f, y + 3, 4:8, :] = state[f, y]
        return carry

    lax.fori_loop(0, ny, place, 0)

    def place_rows(t, carry):
        for j in range(4):
            at = pl.multiple_of((j * ntr + t) * 4, 4)
            src[j, t, 4:8, :] = south_in[pl.ds(at, 4), :]
            src[ny + 4 + j, t, 4:8, :] = north_in[pl.ds(at, 4), :]
        for k, top in ((0, 2), (1, ny + 4)):
            for j in range(2):
                at = ((k * 2 + j) * ntr + t) * 2
                src[top + j, t, 2:4, :] = west_in[pl.ds(at, 2), :]
                src[top + j, t, 8:10, :] = east_in[pl.ds(at, 2), :]
        return carry

    lax.fori_loop(0, ntr, place_rows, 0)
    rows_y, rows_x = 16 * ntr, 8 * ntr
    for f in range(5):
        for j in range(3):
            at = rows_y + (f * 3 + j) * 4
            phys[f, j, 4:8, :] = south_in[at : at + 4, :]
            phys[f, ny + 3 + j, 4:8, :] = north_in[at : at + 4, :]
        for y in range(ry):
            at = rows_x + (f * ry + y) * 3
            phys[f, y + 1, 1:4, :] = west_in[at : at + 3, :]
            phys[f, y + 1, 8:11, :] = east_in[at : at + 3, :]

    def get(f, row, shift):
        return phys[f, row + 1, 2 + shift : 10 + shift, :]

    def put(ref):
        def store(row, value):
            ref[row] = value

        return store

    def put_mid(row, temp, salt):
        mid[0, row] = temp
        mid[1, row] = salt

    physics_rows(get, ry, put(u_west), put(u_east), put(v_south), put_mid)
    advect_all(src, cells, 8, ry, u_west, u_east, v_south)
    absorb_rows(cells, 8, ry, absorb)
    dim_light(absorb, light, ry, 8)

    def put_temp(row, value):
        mid[0, row] = value

    react_rows(
        cells, 8, ry, absorb, light, lambda row: mid[0, row], lambda row: get(2, row, 0), put_temp
    )

    def get2(f, row, shift):
        cut = slice(2 + shift, 6 + shift)
        if f < 2:
            return mid[f, row + 2, cut, :]
        if f == 2:
            return phys[2, row + 3, 4 + shift : 8 + shift, :]
        if f == 3:
            return u_east[row + 2, cut, :]
        return v_south[row + 3, cut, :]

    def put_mid2(row, temp, salt):
        mid2[row] = temp
        fields[1, pl.ds(row * 4, 4), :] = salt

    def put_east2(row, value):
        u_east2[row] = value
        fields[2, pl.ds(row * 4, 4), :] = value

    physics_rows(get2, ny, put(u_west2), put_east2, put(v_south2), put_mid2)
    advect_all(cells, out, 4, ny, u_west2, u_east2, v_south2)
    absorb_rows(out, 4, ny, absorb2)
    dim_light(absorb2, light2, ny, 4)

    def put_temp2(row, value):
        fields[0, pl.ds(row * 4, 4), :] = value
        fields[3, pl.ds(row * 4, 4), :] = v_south2[row + 1]

    react_rows(
        out, 4, ny, absorb2, light2, lambda row: mid2[row], lambda row: get2(2, row, 0), put_temp2
    )

    group = lax.broadcasted_iota(jnp.int32, (4 * ny, depth), 1) // 32
    for g in range(4):
        packed = None
        for f in range(4):
            turn = ((f - g) * 32) % depth
            part = fields[f]
            if turn:
                part = pltpu.roll(part, turn, 1)
            packed = part if packed is None else jnp.where(group == f, part, packed)
        mail[g] = packed


def run_two_steps(own, west, east, south, north, w_in, e_in, state):
    ny, ntr, nx, depth = own.shape
    ry = ny + 4
    f32 = jnp.float32
    vmem = pltpu.VMEM
    whole = pl.BlockSpec(memory_space=pltpu.VMEM)
    return pl.pallas_call(
        two_steps,
        out_shape=(
            jax.ShapeDtypeStruct((ny, ntr, nx, depth), f32),
            jax.ShapeDtypeStruct((4, ny * nx, depth), f32),
        ),
        in_specs=[whole] * 8,
        out_specs=(whole, whole),
        scratch_shapes=[
            vmem((ny + 8, ntr, 16, depth), f32),
            vmem((5, ny + 6, 16, depth), f32),
            vmem((ry, 8, depth), f32),
            vmem((ry, 8, depth), f32),
            vmem((ry + 1, 8, depth), f32),
            vmem((2, ry, 8, depth), f32),
            vmem((ry, ntr, 8, depth), f32),
            vmem((ry, 8, depth), f32),
            vmem((ry, 8, depth), f32),
            vmem((ny, nx, depth), f32),
            vmem((ny, nx, depth), f32),
            vmem((ny + 1, nx, depth), f32),
            vmem((ny, nx, depth), f32),
            vmem((ny, nx, depth), f32),
            vmem((ny, nx, depth), f32),
            vmem((4, ny * nx, depth), f32),
        ],
        compiler_params=pltpu.CompilerParams(vmem_limit_bytes=40 * 1024 * 1024),
        name="two_steps",
    )(own, west, east, south, north, w_in, e_in, state)


def flat(*pieces):
    return jnp.concatenate([p.reshape(-1, p.shape[-1]) for p in pieces], axis=0)


def on_device(temp, salt, east, north, tracer, mask, bottom):
    nx, ny, ntr, levels = tracer.shape
    parts = lax.axis_size("gy")
    share = levels // parts
    row_start = lax.axis_index("gy") * ny
    mask_tile = lax.dynamic_slice_in_dim(mask, row_start, ny, 1).T
    bottom_tile = lax.dynamic_slice_in_dim(bottom, row_start, ny, 1).T
    column_levels = lax.broadcasted_iota(jnp.int32, (1, 1, levels), 2)
    wet = ((mask_tile[:, :, None] > 0) & (column_levels < bottom_tile[:, :, None])).astype(
        jnp.float32
    )
    tracer = tracer.transpose(1, 2, 0, 3)
    west_t = ring_send(tracer, "gx", 1)
    east_t = ring_send(tracer, "gx", -1)

    packed = jnp.stack([temp, salt, east, north], axis=2)
    packed = packed.reshape(nx, parts, ny, 4 * share).transpose(1, 2, 0, 3)
    packed = lax.all_to_all(packed, "gy", split_axis=0, concat_axis=0, tiled=True)
    packed = packed.reshape(parts, ny, nx, 4, share).transpose(3, 1, 2, 0, 4)
    packed = packed.reshape(4, ny, nx, levels)
    state = jnp.concatenate([packed[:2], wet[None], packed[2:]], axis=0)

    south = ring_send(flat(tracer[ny - 4 :], state[:, ny - 3 :]), ROWS, 1)
    north = ring_send(flat(tracer[:4], state[:, :3]), ROWS, -1)
    west_t, east_t, south, north, state = lax.optimization_barrier(
        (west_t, east_t, south, north, state)
    )
    rows = 4 * ntr * nx
    south_t = south[:rows].reshape(4, ntr, nx, levels)
    north_t = north[:rows].reshape(4, ntr, nx, levels)
    south_p = south[rows:].reshape(5, 3, nx, levels)
    north_p = north[rows:].reshape(5, 3, nx, levels)
    tall = jnp.concatenate([south_p[:, 1:], state, north_p[:, :2]], axis=1)

    def side(lines, cells):
        return flat(south_t[2:, :, lines], north_t[:2, :, lines], tall[:, :, cells])

    w_in = ring_send(side(slice(nx - 2, nx), slice(nx - 3, nx)), "gx", 1)
    e_in = ring_send(side(slice(0, 2), slice(0, 3)), "gx", -1)
    tracer, mail = run_two_steps(tracer, west_t, east_t, south, north, w_in, e_in, state)
    mail = lax.all_to_all(mail, "gy", split_axis=0, concat_axis=0, tiled=True)
    mail = mail.reshape(parts, ny, nx, 4, share).transpose(3, 2, 0, 1, 4)
    mail = mail.reshape(4, nx, parts * ny, share)
    fields = [mail[i] for i in range(4)]
    return (*fields, tracer.transpose(2, 0, 1, 3))


def solution(mesh):
    field = P("gx", "grp", "gy")
    tracers = P("gx", ("grp", "gy"), None, None)
    columns = P("gx", "grp")
    return jax.shard_map(
        on_device,
        mesh=mesh,
        in_specs=(field, field, field, field, tracers, columns, columns),
        out_specs=(field, field, field, field, tracers),
        check_vma=False,
    )
```

time: 88.1 us -> 93.1 us (1.057)
  starting transfers between devices: 54.3 us -> 41.4 us
  waiting for transfers between devices: 15.2 us -> 24.2 us
  Pallas kernels: 0 us -> 7.41 us
  blocking collectives: 0 us -> 7.24 us
  other arithmetic: 5.54 us -> 1.25 us
    all_to_all x2 -> x1, starting transfers between devices: 18.2 us -> 4.23 us  [on_device(): lax.all_to_all(packed, 'gy', split_axis=0, concat_axis=0, tiled=True)]
    all_to_all x2 -> x1, waiting for transfers between devices: 4.05 us -> 13.8 us  [on_device(): lax.all_to_all(packed, 'gy', split_axis=0, concat_axis=0, tiled=True)]
    pallas_call x0 -> x1, Pallas kernels: none -> 7.41 us  [run_two_steps(): pl.pallas_call(two_steps, out_shape=(jax.ShapeDtypeStruct((ny, ntr, nx, d...]
    all_to_all x0 -> x1, blocking collectives: none -> 7.24 us  [on_device(): mail = lax.all_to_all(mail, 'gy', split_axis=0, concat_axis=0, tiled=True)]
    slice x25 -> x21, local copies, waits for them, and re-layouts: 0.91 us -> 2.42 us  [the longest x2 0.81 us: on_device(): north_t = north[:rows].reshape(4, ntr, nx, levels)]
    sub x10 -> x0, other arithmetic: 1.3 us -> none  [the longest x4 0.83 us: face_flux(): diff = cut(q, 1, n + 3) - cut(q, 0, n + 3)]
    add x10 -> x0, other arithmetic: 1.19 us -> none  [the longest x4 0.95 us: face_flux(): flux = jnp.maximum(face, 0.0) * left + jnp.minimum(face, 0.0) * right]
    ppermute x8 -> x6, starting transfers between devices: 36.1 us -> 37.2 us  [ring_send(): lax.ppermute(block, axis, [(i, (i + step) % count) for i in range(count)])]
  transfers between devices with their start and end apart: 10 -> 7, of which waited for: 6 -> 4; matrix products, arithmetic and copies ran while one was open for 6% -> 4% of each run, Pallas kernels for 0% -> 0%
where the time goes in v3:
time: 93.1 us; the launch traced here: 92.6 us
  starting transfers between devices  41.4 us (44%)
  waiting for transfers between devices  24.2 us (26%)
  local copies, waits for them, and re-layouts  10.1 us (11%)
  Pallas kernels  7.41 us (8%)
  blocking collectives  7.24 us (8%)
  other arithmetic  1.25 us (1%)
  between operations  1 us (1%)
    ppermute x6, starting transfers between devices, ring_send(): lax.ppermute(block, axis, [(i, (i + step) % count) for i in range(count)])  37.2 us
    all_to_all x1, waiting for transfers between devices, on_device(): lax.all_to_all(packed, 'gy', split_axis=0, concat_axis=0, tiled=True)  13.8 us
    ppermute x6, waiting for transfers between devices, ring_send(): lax.ppermute(block, axis, [(i, (i + step) % count) for i in range(count)])  10.4 us
    pallas_call x1, Pallas kernels, run_two_steps(): pl.pallas_call(two_steps, out_shape=(jax.ShapeDtypeStruct((ny, ntr, nx, d...  7.41 us
    all_to_all x1, blocking collectives, on_device(): mail = lax.all_to_all(mail, 'gy', split_axis=0, concat_axis=0, tiled=True)  7.24 us
    unnamed x22, local copies, waits for them, and re-layouts  5.43 us
    all_to_all x1, starting transfers between devices, on_device(): lax.all_to_all(packed, 'gy', split_axis=0, concat_axis=0, tiled=True)  4.23 us
  transfers between devices with their start and end apart: 7, of which 4 were waited for; matrix products, arithmetic and copies ran while one was open for 4% of the time, Pallas kernels for 0%

profile of v3, /device:TPU:1, one launch (start us, length us, event | category | flops | bytes accessed | tf_op | source)
XLA Modules:
  0.0 92.6 jit_solution(14035703776434094613)
XLA Ops:
  0.6 0.0 copy-start
  0.6 18.8 %collective-permute-start.1 = (f32[12,17,4,128]{3,2,1,0:T(4,128)}, f32[12,17,4,128]{3,2,1,0:T(4,128)S(1)}, u32[]{:S(2)}, u32[]{:S(2)}) collective-permute-start(f32[12,17,4,128]{3,2,1,0:T(4,128)} %bitcast.25), channel_id=1, source_target_pairs={{0,188},{4,0},{8,4},{12,8},{16,12},{20,16},{24,20},{28,24},{32,28}... | collective-permute-start | bytes 1253384 | tf_op jit(solution)/shard_map/ppermute | solution.py:35
  19.5 1.9 %collective-permute-start = (f32[12,17,4,128]{3,2,1,0:T(4,128)}, f32[12,17,4,128]{3,2,1,0:T(4,128)S(1)}, u32[]{:S(2)}, u32[]{:S(2)}) collective-permute-start(f32[12,17,4,128]{3,2,1,0:T(4,128)} %bitcast.26), channel_id=1, source_target_pairs={{0,4},{4,8},{8,12},{12,16},{16,20},{20,24},{24,28},{28,32},{32,36}... | collective-permute-start | bytes 1253384 | tf_op jit(solution)/shard_map/ppermute | solution.py:35
  21.4 1.0 %pad_maximum_fusion = f32[4,48,4,32]{1,3,0,2:T(8,128)S(1)} fusion(f32[4,48,1,32]{1,3,0,2:T(8,128)} %bitcast.39, f32[4,48,1,32]{1,3,0,2:T(8,128)} %bitcast.40, f32[4,48,1,32]{1,3,0,2:T(8,128)} %bitcast.41, f32[4,48,1,32]{1,3,0,2:T(8,128)} %bitcast.42), kind=kLoop, calls=%fused_computation.1 | loop fusion | flops 73728 | bytes 196608 | tf_op jit(solution)/shard_map/stack | solution.py:338
  22.4 0.3 copy.18
  22.6 0.0 copy-start.1
  22.7 0.9 reshape.92
  23.5 4.2 %all-to-all-start = ((f32[4,12,4,128]{3,2,1,0:T(4,128)}), f32[4,12,4,128]{3,2,1,0:T(4,128)S(1)}, u32[]{:S(2)}, u32[]{:S(2)}) async-start(f32[4,12,4,128]{3,2,1,0:T(4,128)} %bitcast.6), calls=%async_computation | async-start | bytes 196608 | tf_op jit(solution)/shard_map/all_to_all | solution.py:340
  27.8 0.0 copy-done.1
  27.8 0.0 copy-start.8
  27.8 0.7 copy-done.8
  28.5 0.1 fusion.2
  28.6 0.0 copy-done
  28.6 0.1 dynamic-slice_bitcast_fusion
  28.6 0.1 copy.20
  28.7 0.1 copy.21
  28.8 0.1 fusion.1
  28.9 13.8 %all-to-all-done = f32[4,12,4,128]{3,2,1,0:T(4,128)S(1)} async-done(((f32[4,12,4,128]{3,2,1,0:T(4,128)}), f32[4,12,4,128]{3,2,1,0:T(4,128)S(1)}, u32[]{:S(2)}, u32[]{:S(2)}) %all-to-all-start) | async-done | bytes 98336 | tf_op jit(solution)/shard_map/all_to_all | solution.py:340
  42.7 0.2 reshape.93
  42.9 0.2 fusion.5
  43.1 0.1 copy.19
  43.2 0.2 slice.78
  43.4 0.1 copy.22
  43.5 0.2 slice.80
  43.8 4.9 %collective-permute-start.2 = (f32[332,128]{1,0:T(8,128)S(1)}, f32[332,128]{1,0:T(8,128)S(1)}, u32[]{:S(2)}, u32[]{:S(2)}) collective-permute-start(f32[332,128]{1,0:T(8,128)S(1)} %pad_maximum_fusion.3), channel_id=1, source_target_pairs={{0,1},{1,2},{2,3},{3,192},{192,193},{193,194},{194,195},{195,384},... | collective-permute-start | bytes 509960 | tf_op jit(solution)/shard_map/ppermute | solution.py:35
  48.7 1.9 %collective-permute-start.3 = (f32[332,128]{1,0:T(8,128)S(1)}, f32[332,128]{1,0:T(8,128)S(1)}, u32[]{:S(2)}, u32[]{:S(2)}) collective-permute-start(f32[332,128]{1,0:T(8,128)S(1)} %pad_maximum_fusion.4), channel_id=1, source_target_pairs={{0,579},{1,0},{2,1},{3,2},{192,3},{193,192},{194,193},{195,194},{3... | collective-permute-start | bytes 509960 | tf_op jit(solution)/shard_map/ppermute | solution.py:35
  50.6 0.4 collective-permute-done.2.south_in
  51.0 0.0 copy-start.2
  51.0 4.4 %collective-permute-done.3.north_in = f32[332,128]{1,0:T(8,128)S(1)} collective-permute-done((f32[332,128]{1,0:T(8,128)S(1)}, f32[332,128]{1,0:T(8,128)S(1)}, u32[]{:S(2)}, u32[]{:S(2)}) %collective-permute-start.3) | collective-permute-done | bytes 170016 | tf_op jit(solution)/shard_map/ppermute | solution.py:35
  55.4 0.0 copy-start.4
  55.4 0.0 collective-permute-done.1.east
  55.4 0.0 collective-permute-done.west
  55.4 0.0 copy-done.2
  55.4 0.6 copy-done.4
  56.1 0.0 slice-start
  56.1 0.0 copy-start.6
  56.1 0.6 copy-done.6
  56.7 0.0 copy-start.7
  56.7 0.6 copy-done.7
  57.3 0.0 slice-done
  57.4 0.8 slice-done.1
  58.3 0.0 slice-start.2
  58.3 0.0 slice-start.3
  58.3 0.7 slice-done.2
  59.0 0.0 slice-done.3
  59.1 0.1 fusion.6
  59.2 0.1 reshape.106
  59.2 0.1 reshape.103
  59.3 0.0 copy-start.3
  59.3 0.0 copy-start.5
  59.3 2.1 %collective-permute-start.4 = (f32[376,128]{1,0:T(8,128)S(1)}, f32[376,128]{1,0:T(8,128)S(1)}, u32[]{:S(2)}, u32[]{:S(2)}) collective-permute-start(f32[376,128]{1,0:T(8,128)S(1)} %pad_maximum_fusion.1), channel_id=1, source_target_pairs={{0,4},{4,8},{8,12},{12,16},{16,20},{20,24},{24,28},{28,32},{32,36}... | collective-permute-start | bytes 577544 | tf_op jit(solution)/shard_map/ppermute | solution.py:35
  61.4 7.6 %collective-permute-start.5 = (f32[376,128]{1,0:T(8,128)S(1)}, f32[376,128]{1,0:T(8,128)S(1)}, u32[]{:S(2)}, u32[]{:S(2)}) collective-permute-start(f32[376,128]{1,0:T(8,128)S(1)} %pad_maximum_fusion.2), channel_id=1, source_target_pairs={{0,188},{4,0},{8,4},{12,8},{16,12},{20,16},{24,20},{28,24},{32,28}... | collective-permute-start | bytes 577544 | tf_op jit(solution)/shard_map/ppermute | solution.py:35
  69.0 5.6 %collective-permute-done.4.west_in = f32[376,128]{1,0:T(8,128)S(1)} collective-permute-done((f32[376,128]{1,0:T(8,128)S(1)}, f32[376,128]{1,0:T(8,128)S(1)}, u32[]{:S(2)}, u32[]{:S(2)}) %collective-permute-start.4) | collective-permute-done | bytes 192544 | tf_op jit(solution)/shard_map/ppermute | solution.py:35
  74.6 0.0 collective-permute-done.5.east_in
  74.6 0.0 copy-done.3
  74.6 0.0 copy-done.5
  74.6 7.4 %two_steps.1 = (f32[12,17,4,128]{3,2,1,0:T(4,128)}, f32[4,48,128]{2,1,0:T(8,128)S(1)}) custom-call(f32[12,17,4,128]{3,2,1,0:T(4,128)S(1)} %bitcast.28, f32[12,17,4,128]{3,2,1,0:T(4,128)S(1)} %collective-permute-done.west, f32[12,17,4,128]{3,2,1,0:T(4,128)S(1)} %collective-permute-done.1.east, f32[332,128]{1,0:T(8,128)S(1)} %copy-done.3, ...), custom_call_target="tpu_custom_call" | custom-call | tf_op jit(solution)/shard_map/two_steps/pallas_call | solution.py:288
  82.1 7.2 %all_to_all.10 = f32[4,48,128]{2,1,0:T(8,128)S(1)} all-to-all(f32[4,48,128]{2,1,0:T(8,128)S(1)} %get-tuple-element.17), channel_id=1, replica_groups=mesh['grp'=4,'gx'=48,'gy'=4] {'gy'}, dimensions={0} | all-to-all | bytes 196608 | tf_op jit(solution)/shard_map/all_to_all | solution.py:363
  89.3 0.2 reshape.107
  89.5 0.1 copy.29
  89.7 0.7 copy.27
  90.4 0.7 copy.26
  91.1 0.7 copy.25
  91.8 0.7 copy.24
  (22 shorter events, 0.4 us)
Async XLA Ops:
  0.6 27.9 %copy-start = (s32[4,48]{1,0:T(4,128)S(1)}, s32[4,48]{1,0:T(4,128)}, u32[]{:S(2)}) copy-start(s32[4,48]{1,0:T(4,128)} %param.13) | copy-start | bytes 2308
  0.6 54.8 %collective-permute-start.1 = (f32[12,17,4,128]{3,2,1,0:T(4,128)}, f32[12,17,4,128]{3,2,1,0:T(4,128)S(1)}, u32[]{:S(2)}, u32[]{:S(2)}) collective-permute-start(f32[12,17,4,128]{3,2,1,0:T(4,128)} %bitcast.25), channel_id=1, source_target_pairs={{0,188},{4,0},{8,4},{12,8},{16,12},{20,16},{24,20},{28,24},{32,28}... | collective-permute-start | bytes 1253384 | tf_op jit(solution)/shard_map/ppermute | solution.py:35
  19.5 35.9 %collective-permute-start = (f32[12,17,4,128]{3,2,1,0:T(4,128)}, f32[12,17,4,128]{3,2,1,0:T(4,128)S(1)}, u32[]{:S(2)}, u32[]{:S(2)}) collective-permute-start(f32[12,17,4,128]{3,2,1,0:T(4,128)} %bitcast.26), channel_id=1, source_target_pairs={{0,4},{4,8},{8,12},{12,16},{16,20},{20,24},{24,28},{28,32},{32,36}... | collective-permute-start | bytes 1253384 | tf_op jit(solution)/shard_map/ppermute | solution.py:35
  22.6 5.1 %copy-start.1 = (f32[4,12,17,128]{3,0,2,1:T(4,128)S(1)}, f32[4,12,17,128]{3,0,2,1:T(4,128)}, u32[]{:S(2)}) copy-start(f32[4,12,17,128]{3,0,2,1:T(4,128)} %param.11) | copy-start | bytes 1253380
  23.5 19.2 %all-to-all-start = ((f32[4,12,4,128]{3,2,1,0:T(4,128)}), f32[4,12,4,128]{3,2,1,0:T(4,128)S(1)}, u32[]{:S(2)}, u32[]{:S(2)}) async-start(f32[4,12,4,128]{3,2,1,0:T(4,128)} %bitcast.6), calls=%async_computation | async-start | bytes 196608 | tf_op jit(solution)/shard_map/all_to_all | solution.py:340
  27.8 0.7 copy-start.8
  43.8 7.2 %collective-permute-start.2 = (f32[332,128]{1,0:T(8,128)S(1)}, f32[332,128]{1,0:T(8,128)S(1)}, u32[]{:S(2)}, u32[]{:S(2)}) collective-permute-start(f32[332,128]{1,0:T(8,128)S(1)} %pad_maximum_fusion.3), channel_id=1, source_target_pairs={{0,1},{1,2},{2,3},{3,192},{192,193},{193,194},{194,195},{195,384},... | collective-permute-start | bytes 509960 | tf_op jit(solution)/shard_map/ppermute | solution.py:35
  48.7 6.7 %collective-permute-start.3 = (f32[332,128]{1,0:T(8,128)S(1)}, f32[332,128]{1,0:T(8,128)S(1)}, u32[]{:S(2)}, u32[]{:S(2)}) collective-permute-start(f32[332,128]{1,0:T(8,128)S(1)} %pad_maximum_fusion.4), channel_id=1, source_target_pairs={{0,579},{1,0},{2,1},{3,2},{192,3},{193,192},{194,193},{195,194},{3... | collective-permute-start | bytes 509960 | tf_op jit(solution)/shard_map/ppermute | solution.py:35
  51.0 4.4 %copy-start.2 = (f32[332,128]{1,0:T(8,128)}, f32[332,128]{1,0:T(8,128)S(1)}, u32[]{:S(2)}) copy-start(f32[332,128]{1,0:T(8,128)S(1)} %collective-permute-done.2.south_in) | copy-start | bytes 509956
  55.4 0.7 copy-start.4
  56.1 1.2 %slice-start = ((f32[332,128]{1,0:T(8,128)}), f32[272,128]{1,0:T(8,128)S(1)}, s32[]{:S(2)}) async-start(f32[332,128]{1,0:T(8,128)} %copy-done.2), calls=%async_computation.2 | async-start | bytes 278528 | tf_op jit(solution)/shard_map/slice | solution.py:351
  56.1 0.6 copy-start.6
  56.7 0.6 copy-start.7
  57.3 0.9 slice-start.1
  58.3 0.7 slice-start.2
  58.3 0.7 slice-start.3
  59.3 15.3 %copy-start.3 = (f32[332,128]{1,0:T(8,128)S(1)}, f32[332,128]{1,0:T(8,128)}, u32[]{:S(2)}) copy-start(f32[332,128]{1,0:T(8,128)} %copy-done.2) | copy-start | bytes 509956
  59.3 15.3 %copy-start.5 = (f32[332,128]{1,0:T(8,128)S(1)}, f32[332,128]{1,0:T(8,128)}, u32[]{:S(2)}) copy-start(f32[332,128]{1,0:T(8,128)} %copy-done.4) | copy-start | bytes 509956
  59.3 15.3 %collective-permute-start.4 = (f32[376,128]{1,0:T(8,128)S(1)}, f32[376,128]{1,0:T(8,128)S(1)}, u32[]{:S(2)}, u32[]{:S(2)}) collective-permute-start(f32[376,128]{1,0:T(8,128)S(1)} %pad_maximum_fusion.1), channel_id=1, source_target_pairs={{0,4},{4,8},{8,12},{12,16},{16,20},{20,24},{24,28},{28,32},{32,36}... | collective-permute-start | bytes 577544 | tf_op jit(solution)/shard_map/ppermute | solution.py:35
  61.4 13.2 %collective-permute-start.5 = (f32[376,128]{1,0:T(8,128)S(1)}, f32[376,128]{1,0:T(8,128)S(1)}, u32[]{:S(2)}, u32[]{:S(2)}) collective-permute-start(f32[376,128]{1,0:T(8,128)S(1)} %pad_maximum_fusion.2), channel_id=1, source_target_pairs={{0,188},{4,0},{8,4},{12,8},{16,12},{20,16},{24,20},{28,24},{32,28}... | collective-permute-start | bytes 577544 | tf_op jit(solution)/shard_map/ppermute | solution.py:35

commit v4 on v3

--- a/solution.py
+++ b/solution.py
@@ -169,7 +169,7 @@
 
 
 def two_steps(
-    own, west, east, south_in, north_in, west_in, east_in, state,
+    own, east, west, south_in, north_in, state,
     out, mail,
     src, phys, u_west, u_east, v_south, mid, cells, absorb, light,
     u_west2, u_east2, v_south2, mid2, absorb2, light2, fields,
@@ -182,37 +182,35 @@
         src[y + 4, :, 4:8, :] = own[y]
         src[y + 4, :, 8:12, :] = east[y]
         for f in range(5):
-            phys[f, y + 3, 4:8, :] = state[f, y]
+            phys[f, y + 3, 0:10, :] = state[pl.ds((f * ny + y) * 10, 10), :]
         return carry
 
     lax.fori_loop(0, ny, place, 0)
+
+    wing = 4 * ntr * nx
 
     def place_rows(t, carry):
         for j in range(4):
             at = pl.multiple_of((j * ntr + t) * 4, 4)
             src[j, t, 4:8, :] = south_in[pl.ds(at, 4), :]
             src[ny + 4 + j, t, 4:8, :] = north_in[pl.ds(at, 4), :]
-        for k, top in ((0, 2), (1, ny + 4)):
-            for j in range(2):
-                at = ((k * 2 + j) * ntr + t) * 2
-                src[top + j, t, 2:4, :] = west_in[pl.ds(at, 2), :]
-                src[top + j, t, 8:10, :] = east_in[pl.ds(at, 2), :]
+        for j in range(2):
+            at = wing + (j * ntr + t) * 4
+            src[2 + j, t, 2:4, :] = south_in[pl.ds(at, 2), :]
+            src[2 + j, t, 8:10, :] = south_in[pl.ds(at + 2, 2), :]
+            src[ny + 4 + j, t, 2:4, :] = north_in[pl.ds(at, 2), :]
+            src[ny + 4 + j, t, 8:10, :] = north_in[pl.ds(at + 2, 2), :]
         return carry
 
     lax.fori_loop(0, ntr, place_rows, 0)
-    rows_y, rows_x = 16 * ntr, 8 * ntr
     for f in range(5):
         for j in range(3):
-            at = rows_y + (f * 3 + j) * 4
-            phys[f, j, 4:8, :] = south_in[at : at + 4, :]
-            phys[f, ny + 3 + j, 4:8, :] = north_in[at : at + 4, :]
-        for y in range(ry):
-            at = rows_x + (f * ry + y) * 3
-            phys[f, y + 1, 1:4, :] = west_in[at : at + 3, :]
-            phys[f, y + 1, 8:11, :] = east_in[at : at + 3, :]
+            at = wing + wing // 2 + (f * 3 + j) * 10
+            phys[f, j, 0:10, :] = south_in[at : at + 10, :]
+            phys[f, ny + 3 + j, 0:10, :] = north_in[at : at + 10, :]
 
     def get(f, row, shift):
-        return phys[f, row + 1, 2 + shift : 10 + shift, :]
+        return phys[f, row + 1, 1 + shift : 9 + shift, :]
 
     def put(ref):
         def store(row, value):
@@ -241,7 +239,7 @@
         if f < 2:
             return mid[f, row + 2, cut, :]
         if f == 2:
-            return phys[2, row + 3, 4 + shift : 8 + shift, :]
+            return phys[2, row + 3, 3 + shift : 7 + shift, :]
         if f == 3:
             return u_east[row + 2, cut, :]
         return v_south[row + 3, cut, :]
@@ -279,7 +277,7 @@
         mail[g] = packed
 
 
-def run_two_steps(own, west, east, south, north, w_in, e_in, state):
+def run_two_steps(own, west, east, south, north, state):
     ny, ntr, nx, depth = own.shape
     ry = ny + 4
     f32 = jnp.float32
@@ -291,7 +289,7 @@
             jax.ShapeDtypeStruct((ny, ntr, nx, depth), f32),
             jax.ShapeDtypeStruct((4, ny * nx, depth), f32),
         ),
-        in_specs=[whole] * 8,
+        in_specs=[whole] * 6,
         out_specs=(whole, whole),
         scratch_shapes=[
             vmem((ny + 8, ntr, 16, depth), f32),
@@ -313,58 +311,135 @@
         ],
         compiler_params=pltpu.CompilerParams(vmem_limit_bytes=40 * 1024 * 1024),
         name="two_steps",
-    )(own, west, east, south, north, w_in, e_in, state)
-
-
-def flat(*pieces):
-    return jnp.concatenate([p.reshape(-1, p.shape[-1]) for p in pieces], axis=0)
+    )(own, east, west, south, north, state)
+
+
+def call(body, out_shapes, *args, name):
+    whole = pl.BlockSpec(memory_space=pltpu.VMEM)
+    return pl.pallas_call(
+        body,
+        out_shape=tuple(jax.ShapeDtypeStruct(s, jnp.float32) for s in out_shapes),
+        in_specs=[whole] * len(args),
+        out_specs=(whole,) * len(out_shapes),
+        compiler_params=pltpu.CompilerParams(vmem_limit_bytes=16 * 1024 * 1024),
+        name=name,
+    )(*args)
+
+
+def pack_levels(stacked, own, to_east, to_west):
+    span = stacked.shape[1]
+    depth = own.shape[1]
+    nx = own.shape[0] // span
+    for x in range(nx):
+        rows = stacked[x * depth : (x + 1) * depth, :].T
+        own[x * span : (x + 1) * span, :] = rows
+        if x > 0:
+            to_east[(x - 1) * span : x * span, :] = rows
+        if x < nx - 1:
+            to_west[x * span : (x + 1) * span, :] = rows
+    for ref in (to_east, to_west):
+        ref[3 * span : 3 * span + nx, :] = jnp.zeros((nx, depth), jnp.float32)
+        ref[3 * span : 3 * span + nx, 0:span] = stacked[nx * depth :, :]
+
+
+def stage_mail(own, west, east, mail):
+    ny = own.shape[0] // 4
+    for x in range(10):
+        ref, at = (west, x) if x < 3 else (own, x - 3) if x < 7 else (east, x - 7)
+        mail[pl.ds(x, ny, stride=10), :] = ref[at * ny : (at + 1) * ny, :]
+
+
+def open_mail(mail, wet, own, east, west, state, up, down):
+    ny, ntr, nx, depth = own.shape
+    cells = ny * 10
+    group = lax.broadcasted_iota(jnp.int32, (cells, depth), 1) // 32
+    for f, at in ((0, 0), (1, 1), (2, 3), (3, 4)):
+        field = None
+        for s in range(4):
+            turn = ((s - f) * 32) % depth
+            part = mail[s]
+            if turn:
+                part = pltpu.roll(part, turn, 1)
+            field = part if field is None else jnp.where(group == s, part, field)
+        state[at * cells : (at + 1) * cells, :] = field
+    state[2 * cells : 3 * cells, :] = wet[...]
+    for j in range(4):
+        for t in range(ntr):
+            at = (j * ntr + t) * 4
+            up[at : at + 4, :] = own[ny - 4 + j, t]
+            down[at : at + 4, :] = own[j, t]
+    base = 16 * ntr
+    for j in range(2):
+        for t in range(ntr):
+            at = base + (j * ntr + t) * 4
+            up[at : at + 2, :] = west[ny - 2 + j, t, 2:4, :]
+            up[at + 2 : at + 4, :] = east[ny - 2 + j, t, 0:2, :]
+            down[at : at + 2, :] = west[j, t, 2:4, :]
+            down[at + 2 : at + 4, :] = east[j, t, 0:2, :]
+    base = 24 * ntr
+    for f in range(5):
+        up[base + f * 30 : base + f * 30 + 30, :] = state[(f + 1) * cells - 30 : (f + 1) * cells, :]
+        down[base + f * 30 : base + f * 30 + 30, :] = state[f * cells : f * cells + 30, :]
+
+
+def unpack_levels(mail, temp, salt, east, north):
+    nx, share, ny = temp.shape
+    for x in range(nx):
+        tall = mail[pl.ds(x, ny, stride=nx), :].T
+        for f, ref in enumerate((temp, salt, east, north)):
+            ref[x] = tall[f * share : (f + 1) * share]
 
 
 def on_device(temp, salt, east, north, tracer, mask, bottom):
     nx, ny, ntr, levels = tracer.shape
     parts = lax.axis_size("gy")
     share = levels // parts
-    row_start = lax.axis_index("gy") * ny
-    mask_tile = lax.dynamic_slice_in_dim(mask, row_start, ny, 1).T
-    bottom_tile = lax.dynamic_slice_in_dim(bottom, row_start, ny, 1).T
-    column_levels = lax.broadcasted_iota(jnp.int32, (1, 1, levels), 2)
-    wet = ((mask_tile[:, :, None] > 0) & (column_levels < bottom_tile[:, :, None])).astype(
-        jnp.float32
-    )
+    span = parts * ny
     tracer = tracer.transpose(1, 2, 0, 3)
+
+    deep = jnp.where(mask > 0, bottom, 0).astype(jnp.float32)
+    stacked = jnp.stack([f.transpose(0, 2, 1) for f in (temp, salt, east, north)], axis=1)
+    stacked = jnp.concatenate([stacked.reshape(nx * levels, span), deep], axis=0)
+    side = (3 * span + nx, levels)
+    own, to_east, to_west = call(
+        pack_levels, [(nx * span, levels), side, side], stacked, name="pack_levels"
+    )
+    west_p = ring_send(to_east, "gx", 1)
     west_t = ring_send(tracer, "gx", 1)
+    east_p = ring_send(to_west, "gx", -1)
     east_t = ring_send(tracer, "gx", -1)
-
-    packed = jnp.stack([temp, salt, east, north], axis=2)
-    packed = packed.reshape(nx, parts, ny, 4 * share).transpose(1, 2, 0, 3)
-    packed = lax.all_to_all(packed, "gy", split_axis=0, concat_axis=0, tiled=True)
-    packed = packed.reshape(parts, ny, nx, 4, share).transpose(3, 1, 2, 0, 4)
-    packed = packed.reshape(4, ny, nx, levels)
-    state = jnp.concatenate([packed[:2], wet[None], packed[2:]], axis=0)
-
-    south = ring_send(flat(tracer[ny - 4 :], state[:, ny - 3 :]), ROWS, 1)
-    north = ring_send(flat(tracer[:4], state[:, :3]), ROWS, -1)
-    west_t, east_t, south, north, state = lax.optimization_barrier(
-        (west_t, east_t, south, north, state)
-    )
-    rows = 4 * ntr * nx
-    south_t = south[:rows].reshape(4, ntr, nx, levels)
-    north_t = north[:rows].reshape(4, ntr, nx, levels)
-    south_p = south[rows:].reshape(5, 3, nx, levels)
-    north_p = north[rows:].reshape(5, 3, nx, levels)
-    tall = jnp.concatenate([south_p[:, 1:], state, north_p[:, :2]], axis=1)
-
-    def side(lines, cells):
-        return flat(south_t[2:, :, lines], north_t[:2, :, lines], tall[:, :, cells])
-
-    w_in = ring_send(side(slice(nx - 2, nx), slice(nx - 3, nx)), "gx", 1)
-    e_in = ring_send(side(slice(0, 2), slice(0, 3)), "gx", -1)
-    tracer, mail = run_two_steps(tracer, west_t, east_t, south, north, w_in, e_in, state)
+    (mail,) = call(stage_mail, [(10 * span, levels)], own, west_p, east_p, name="stage_mail")
+    mail = lax.all_to_all(
+        mail.reshape(parts, 10 * ny, levels), "gy", split_axis=0, concat_axis=0, tiled=True
+    )
+    deep = jnp.concatenate(
+        [west_p[3 * span + 1 : 3 * span + 4, :span], deep, east_p[3 * span : 3 * span + 3, :span]]
+    )
+    deep = lax.dynamic_slice_in_dim(deep, lax.axis_index("gy") * ny, ny, 1).T
+    level = lax.broadcasted_iota(jnp.int32, (ny, 10, levels), 2).astype(jnp.float32)
+    wet = (level < deep[:, :, None]).astype(jnp.float32).reshape(10 * ny, levels)
+    y_rows = 24 * ntr + 150
+    state, up, down = call(
+        open_mail,
+        [(50 * ny, levels), (y_rows, levels), (y_rows, levels)],
+        mail,
+        wet,
+        tracer,
+        east_t,
+        west_t,
+        name="open_mail",
+    )
+    south = ring_send(up, ROWS, 1)
+    north = ring_send(down, ROWS, -1)
+    tracer, mail = run_two_steps(tracer, west_t, east_t, south, north, state)
     mail = lax.all_to_all(mail, "gy", split_axis=0, concat_axis=0, tiled=True)
-    mail = mail.reshape(parts, ny, nx, 4, share).transpose(3, 2, 0, 1, 4)
-    mail = mail.reshape(4, nx, parts * ny, share)
-    fields = [mail[i] for i in range(4)]
-    return (*fields, tracer.transpose(2, 0, 1, 3))
+    fields = call(
+        unpack_levels,
+        [(nx, share, span)] * 4,
+        mail.reshape(nx * span, levels),
+        name="unpack_levels",
+    )
+    return (*[f.transpose(0, 2, 1) for f in fields], tracer.transpose(2, 0, 1, 3))
 
 
 def solution(mesh):

time: 93.1 us -> 76.7 us (0.82)
  local copies, waits for them, and re-layouts: 10.1 us -> 0.86 us
  waiting for transfers between devices: 24.2 us -> 16.3 us
  Pallas kernels: 7.41 us -> 9.26 us
    all_to_all x1, waiting for transfers between devices: 13.8 us -> 0.95 us  [on_device(): lax.all_to_all(mail.reshape(parts, 10 * ny, levels), 'gy', split_axis=0,...]
    ppermute x6, waiting for transfers between devices: 10.4 us -> 15.3 us  [ring_send(): lax.ppermute(block, axis, [(i, (i + step) % count) for i in range(count)])]
    unnamed x22 -> x6, local copies, waits for them, and re-layouts: 5.43 us -> 0.66 us
    slice x21 -> x2, local copies, waits for them, and re-layouts: 2.42 us -> 0.01 us  [the longest x1 0.01 us: on_device(): west_p[3 * span + 1:3 * span + 4, :span]]
    pallas_call x0 -> x4, Pallas kernels: none -> 1.91 us  [call(): pl.pallas_call(body, out_shape=tuple((jax.ShapeDtypeStruct(s, jnp.float32...]
    reshape x14 -> x0, local copies, waits for them, and re-layouts: 1.69 us -> none  [the longest x1 0.87 us: on_device(): packed = packed.reshape(nx, parts, ny, 4 * share).transpose(1, 2, 0, 3)]
  transfers between devices with their start and end apart: 7 -> 7, of which waited for: 4 -> 4; matrix products, arithmetic and copies ran while one was open for 4% -> 0% of each run, Pallas kernels for 0% -> 1%
where the time goes in v4:
time: 76.7 us; the launch traced here: 76.3 us
  starting transfers between devices  41.3 us (54%)
  waiting for transfers between devices  16.3 us (21%)
  Pallas kernels  9.26 us (12%)
  blocking collectives  6.58 us (9%)
  other arithmetic  1.16 us (2%)
  local copies, waits for them, and re-layouts  0.86 us (1%)
  between operations  0.78 us (1%)
    ppermute x6, starting transfers between devices, ring_send(): lax.ppermute(block, axis, [(i, (i + step) % count) for i in range(count)])  36.5 us
    ppermute x6, waiting for transfers between devices, ring_send(): lax.ppermute(block, axis, [(i, (i + step) % count) for i in range(count)])  15.3 us
    pallas_call x1, Pallas kernels, run_two_steps(): pl.pallas_call(two_steps, out_shape=(jax.ShapeDtypeStruct((ny, ntr, nx, d...  7.35 us
    all_to_all x1, blocking collectives, on_device(): mail = lax.all_to_all(mail, 'gy', split_axis=0, concat_axis=0, tiled=True)  6.58 us
    all_to_all x1, starting transfers between devices, on_device(): lax.all_to_all(mail.reshape(parts, 10 * ny, levels), 'gy', split_axis=0,...  4.88 us
    pallas_call x4, Pallas kernels, call(): pl.pallas_call(body, out_shape=tuple((jax.ShapeDtypeStruct(s, jnp.float32...  1.91 us
  transfers between devices with their start and end apart: 7, of which 4 were waited for; matrix products, arithmetic and copies ran while one was open for 0% of the time, Pallas kernels for 1%

profile of v4, /device:TPU:1, one launch (start us, length us, event | category | flops | bytes accessed | tf_op | source)
XLA Modules:
  0.0 76.3 jit_solution(5686441714028603454)
XLA Ops:
  0.6 1.0 %pad_maximum_fusion.1 = f32[4,4,32,48]{3,2,0,1:T(8,128)S(1)} fusion(f32[4,1,32,48]{3,2,0,1:T(8,128)} %bitcast.29, f32[4,1,32,48]{3,2,0,1:T(8,128)} %bitcast.30, f32[4,1,32,48]{3,2,0,1:T(8,128)} %bitcast.31, f32[4,1,32,48]{3,2,0,1:T(8,128)} %bitcast.32), kind=kLoop, calls=%fused_computation.1 | loop fusion | flops 73728 | bytes 196608 | tf_op jit(solution)/shard_map/stack | solution.py:401
  1.6 0.0 copy-start.1
  1.6 0.0 copy-start.2
  1.6 0.6 copy-done.1
  2.3 0.0 copy-done.2
  2.3 0.0 copy-start
  2.3 0.1 pack_levels.1
  2.4 4.8 %collective-permute-start.2 = (f32[148,128]{1,0:T(8,128)S(1)}, f32[148,128]{1,0:T(8,128)S(1)}, u32[]{:S(2)}, u32[]{:S(2)}) collective-permute-start(f32[148,128]{1,0:T(8,128)S(1)} %get-tuple-element.18), channel_id=1, source_target_pairs={{0,4},{4,8},{8,12},{12,16},{16,20},{20,24},{24,28},{28,32},{32,36}... | collective-permute-start | bytes 227336 | tf_op jit(solution)/shard_map/ppermute | solution.py:35
  7.3 15.9 %collective-permute-start.3 = (f32[148,128]{1,0:T(8,128)S(1)}, f32[148,128]{1,0:T(8,128)S(1)}, u32[]{:S(2)}, u32[]{:S(2)}) collective-permute-start(f32[148,128]{1,0:T(8,128)S(1)} %get-tuple-element.19), channel_id=1, source_target_pairs={{0,188},{4,0},{8,4},{12,8},{16,12},{20,16},{24,20},{28,24},{32,28}... | collective-permute-start | bytes 227336 | tf_op jit(solution)/shard_map/ppermute | solution.py:35
  23.2 0.0 copy-done
  23.2 1.9 %collective-permute-start.1 = (f32[12,17,4,128]{3,2,1,0:T(4,128)S(1)}, f32[12,17,4,128]{3,2,1,0:T(4,128)S(1)}, u32[]{:S(2)}, u32[]{:S(2)}) collective-permute-start(f32[12,17,4,128]{3,2,1,0:T(4,128)S(1)} %bitcast.23), channel_id=1, source_target_pairs={{0,4},{4,8},{8,12},{12,16},{16,20},{20,24},{24,28},{28,32},{32,36}... | collective-permute-start | bytes 1253384 | tf_op jit(solution)/shard_map/ppermute | solution.py:35
  25.1 7.6 %collective-permute-start = (f32[12,17,4,128]{3,2,1,0:T(4,128)S(1)}, f32[12,17,4,128]{3,2,1,0:T(4,128)S(1)}, u32[]{:S(2)}, u32[]{:S(2)}) collective-permute-start(f32[12,17,4,128]{3,2,1,0:T(4,128)S(1)} %bitcast.24), channel_id=1, source_target_pairs={{0,188},{4,0},{8,4},{12,8},{16,12},{20,16},{24,20},{28,24},{32,28}... | collective-permute-start | bytes 1253384 | tf_op jit(solution)/shard_map/ppermute | solution.py:35
  32.7 0.0 collective-permute-done.2.west
  32.7 0.0 collective-permute-done.3.east
  32.8 0.7 stage_mail.1
  33.5 4.9 %all-to-all-start = ((f32[4,120,128]{2,1,0:T(8,128)}), f32[4,120,128]{2,1,0:T(8,128)S(1)}, u32[]{:S(2)}, u32[]{:S(2)}) async-start(f32[4,120,128]{2,1,0:T(8,128)} %bitcast.10), calls=%async_computation | async-start | bytes 491520 | tf_op jit(solution)/shard_map/all_to_all | solution.py:412
  38.4 0.1 fusion
  38.4 0.1 copy.38
  38.5 0.1 lt.15
  38.6 0.1 compare_convert_fusion.wet
  38.7 8.7 %collective-permute-done.1.west = f32[12,17,4,128]{3,2,1,0:T(4,128)S(1)} collective-permute-done((f32[12,17,4,128]{3,2,1,0:T(4,128)S(1)}, f32[12,17,4,128]{3,2,1,0:T(4,128)S(1)}, u32[]{:S(2)}, u32[]{:S(2)}) %collective-permute-start.1) | collective-permute-done | bytes 417824 | tf_op jit(solution)/shard_map/ppermute | solution.py:35
  47.4 0.0 collective-permute-done.east
  47.4 1.0 %all-to-all-done.mail = f32[4,120,128]{2,1,0:T(8,128)S(1)} async-done(((f32[4,120,128]{2,1,0:T(8,128)}), f32[4,120,128]{2,1,0:T(8,128)S(1)}, u32[]{:S(2)}, u32[]{:S(2)}) %all-to-all-start) | async-done | bytes 245792 | tf_op jit(solution)/shard_map/all_to_all | solution.py:412
  48.4 0.3 open_mail.1
  48.6 4.3 %collective-permute-start.4 = (f32[558,128]{1,0:T(8,128)S(1)}, f32[558,128]{1,0:T(8,128)S(1)}, u32[]{:S(2)}, u32[]{:S(2)}) collective-permute-start(f32[558,128]{1,0:T(8,128)S(1)} %get-tuple-element.20), channel_id=1, source_target_pairs={{0,1},{1,2},{2,3},{3,192},{192,193},{193,194},{194,195},{195,384},... | collective-permute-start | bytes 857096 | tf_op jit(solution)/shard_map/ppermute | solution.py:35
  53.0 1.9 %collective-permute-start.5 = (f32[558,128]{1,0:T(8,128)S(1)}, f32[558,128]{1,0:T(8,128)S(1)}, u32[]{:S(2)}, u32[]{:S(2)}) collective-permute-start(f32[558,128]{1,0:T(8,128)S(1)} %get-tuple-element.21), channel_id=1, source_target_pairs={{0,579},{1,0},{2,1},{3,2},{192,3},{193,192},{194,193},{195,194},{3... | collective-permute-start | bytes 857096 | tf_op jit(solution)/shard_map/ppermute | solution.py:35
  54.9 1.6 %collective-permute-done.4.south_in = f32[558,128]{1,0:T(8,128)S(1)} collective-permute-done((f32[558,128]{1,0:T(8,128)S(1)}, f32[558,128]{1,0:T(8,128)S(1)}, u32[]{:S(2)}, u32[]{:S(2)}) %collective-permute-start.4) | collective-permute-done | bytes 285728 | tf_op jit(solution)/shard_map/ppermute | solution.py:35
  56.5 5.0 %collective-permute-done.5.north_in = f32[558,128]{1,0:T(8,128)S(1)} collective-permute-done((f32[558,128]{1,0:T(8,128)S(1)}, f32[558,128]{1,0:T(8,128)S(1)}, u32[]{:S(2)}, u32[]{:S(2)}) %collective-permute-start.5) | collective-permute-done | bytes 285728 | tf_op jit(solution)/shard_map/ppermute | solution.py:35
  61.5 7.4 %two_steps.1 = (f32[12,17,4,128]{3,2,1,0:T(4,128)}, f32[4,48,128]{2,1,0:T(8,128)S(1)}) custom-call(f32[12,17,4,128]{3,2,1,0:T(4,128)S(1)} %bitcast.26, f32[12,17,4,128]{3,2,1,0:T(4,128)S(1)} %collective-permute-done.east, f32[12,17,4,128]{3,2,1,0:T(4,128)S(1)} %collective-permute-done.1.west, f32[558,128]{1,0:T(8,128)S(1)} %collective-permute-done.4.south_in, ...), custom_call_target="tpu_custom_call" | custom-call | tf_op jit(solution)/shard_map/two_steps/pallas_call | solution.py:286
  68.9 6.6 %all_to_all.10 = f32[4,48,128]{2,1,0:T(8,128)S(1)} all-to-all(f32[4,48,128]{2,1,0:T(8,128)S(1)} %get-tuple-element.23), channel_id=1, replica_groups=mesh['grp'=4,'gx'=48,'gy'=4] {'gy'}, dimensions={0} | all-to-all | bytes 196608 | tf_op jit(solution)/shard_map/all_to_all | solution.py:435
  75.5 0.8 %unpack_levels.1 = (f32[4,32,48]{2,1,0:T(8,128)}, f32[4,32,48]{2,1,0:T(8,128)}, f32[4,32,48]{2,1,0:T(8,128)}, f32[4,32,48]{2,1,0:T(8,128)}) custom-call(f32[192,128]{1,0:T(8,128)S(1)} %bitcast.27), custom_call_target="tpu_custom_call" | custom-call | tf_op jit(solution)/shard_map/unpack_levels/pallas_call | solution.py:319
  (6 shorter events, 0.1 us)
Async XLA Ops:
  1.6 0.7 copy-start.1
  1.6 0.7 copy-start.2
  2.3 20.9 %copy-start = (f32[4,12,17,128]{3,0,2,1:T(4,128)S(1)}, f32[4,12,17,128]{3,0,2,1:T(4,128)}, u32[]{:S(2)}) copy-start(f32[4,12,17,128]{3,0,2,1:T(4,128)} %param.11) | copy-start | bytes 1253380
  2.4 30.3 %collective-permute-start.2 = (f32[148,128]{1,0:T(8,128)S(1)}, f32[148,128]{1,0:T(8,128)S(1)}, u32[]{:S(2)}, u32[]{:S(2)}) collective-permute-start(f32[148,128]{1,0:T(8,128)S(1)} %get-tuple-element.18), channel_id=1, source_target_pairs={{0,4},{4,8},{8,12},{12,16},{16,20},{20,24},{24,28},{28,32},{32,36}... | collective-permute-start | bytes 227336 | tf_op jit(solution)/shard_map/ppermute | solution.py:35
  7.3 25.5 %collective-permute-start.3 = (f32[148,128]{1,0:T(8,128)S(1)}, f32[148,128]{1,0:T(8,128)S(1)}, u32[]{:S(2)}, u32[]{:S(2)}) collective-permute-start(f32[148,128]{1,0:T(8,128)S(1)} %get-tuple-element.19), channel_id=1, source_target_pairs={{0,188},{4,0},{8,4},{12,8},{16,12},{20,16},{24,20},{28,24},{32,28}... | collective-permute-start | bytes 227336 | tf_op jit(solution)/shard_map/ppermute | solution.py:35
  23.2 24.2 %collective-permute-start.1 = (f32[12,17,4,128]{3,2,1,0:T(4,128)S(1)}, f32[12,17,4,128]{3,2,1,0:T(4,128)S(1)}, u32[]{:S(2)}, u32[]{:S(2)}) collective-permute-start(f32[12,17,4,128]{3,2,1,0:T(4,128)S(1)} %bitcast.23), channel_id=1, source_target_pairs={{0,4},{4,8},{8,12},{12,16},{16,20},{20,24},{24,28},{28,32},{32,36}... | collective-permute-start | bytes 1253384 | tf_op jit(solution)/shard_map/ppermute | solution.py:35
  25.1 22.3 %collective-permute-start = (f32[12,17,4,128]{3,2,1,0:T(4,128)S(1)}, f32[12,17,4,128]{3,2,1,0:T(4,128)S(1)}, u32[]{:S(2)}, u32[]{:S(2)}) collective-permute-start(f32[12,17,4,128]{3,2,1,0:T(4,128)S(1)} %bitcast.24), channel_id=1, source_target_pairs={{0,188},{4,0},{8,4},{12,8},{16,12},{20,16},{24,20},{28,24},{32,28}... | collective-permute-start | bytes 1253384 | tf_op jit(solution)/shard_map/ppermute | solution.py:35
  33.5 14.9 %all-to-all-start = ((f32[4,120,128]{2,1,0:T(8,128)}), f32[4,120,128]{2,1,0:T(8,128)S(1)}, u32[]{:S(2)}, u32[]{:S(2)}) async-start(f32[4,120,128]{2,1,0:T(8,128)} %bitcast.10), calls=%async_computation | async-start | bytes 491520 | tf_op jit(solution)/shard_map/all_to_all | solution.py:412
  48.6 7.9 %collective-permute-start.4 = (f32[558,128]{1,0:T(8,128)S(1)}, f32[558,128]{1,0:T(8,128)S(1)}, u32[]{:S(2)}, u32[]{:S(2)}) collective-permute-start(f32[558,128]{1,0:T(8,128)S(1)} %get-tuple-element.20), channel_id=1, source_target_pairs={{0,1},{1,2},{2,3},{3,192},{192,193},{193,194},{194,195},{195,384},... | collective-permute-start | bytes 857096 | tf_op jit(solution)/shard_map/ppermute | solution.py:35
  53.0 8.6 %collective-permute-start.5 = (f32[558,128]{1,0:T(8,128)S(1)}, f32[558,128]{1,0:T(8,128)S(1)}, u32[]{:S(2)}, u32[]{:S(2)}) collective-permute-start(f32[558,128]{1,0:T(8,128)S(1)} %get-tuple-element.21), channel_id=1, source_target_pairs={{0,579},{1,0},{2,1},{3,2},{192,3},{193,192},{194,193},{195,194},{3... | collective-permute-start | bytes 857096 | tf_op jit(solution)/shard_map/ppermute | solution.py:35

commit v5 on v4

--- a/solution.py
+++ b/solution.py
@@ -81,10 +81,10 @@
     put_south(rows, face_y(rows - 1))
 
 
-def advect_all(src, dst, width, rows, west, east, south):
+def advect_all(read, dst, width, rows, west, east, south):
     def body(t, carry):
         def cell(e, shift=0):
-            return src[e, t, 2 + shift : 2 + shift + width, :]
+            return read(e, t, 2 + shift)
 
         below, here = cell(1), cell(2)
         d_low = here - below
@@ -168,82 +168,165 @@
     lax.fori_loop(0, rows, body, 0)
 
 
-def two_steps(
-    own, east, west, south_in, north_in, state,
+def store_rows(ref):
+    def put(row, value):
+        ref[row] = value
+
+    return put
+
+
+def inner_rows(
+    own, east, west, state,
+    cells, u_east, v_south, mid,
+    src, u_west, absorb, light,
+):
+    ny, ntr, nx, depth = own.shape
+    rows = ny - 4
+
+    def place(y, carry):
+        src[y, :, 0:4, :] = west[y]
+        src[y, :, 4:8, :] = own[y]
+        src[y, :, 8:12, :] = east[y]
+        return carry
+
+    lax.fori_loop(0, ny, place, 0)
+
+    def get(f, row, shift):
+        return state[pl.ds((f * ny + row + 2) * 10 + 1 + shift, 8), :]
+
+    def put_mid(row, temp, salt):
+        mid[0, row] = temp
+        mid[1, row] = salt
+
+    def put_temp(row, value):
+        mid[0, row] = value
+
+    physics_rows(
+        get, rows, store_rows(u_west), store_rows(u_east), store_rows(v_south), put_mid
+    )
+    advect_all(lambda e, t, x: src[e, t, x : x + 8, :], cells, 8, rows, u_west, u_east, v_south)
+    absorb_rows(cells, 8, rows, absorb)
+    dim_light(absorb, light, rows, 8)
+    react_rows(
+        cells, 8, rows, absorb, light, lambda row: mid[0, row], lambda row: get(2, row, 0), put_temp
+    )
+
+
+def outer_rows(
+    own, east, west, south_in, north_in, state, cells_in, u_in, v_in, mid_in,
     out, mail,
-    src, phys, u_west, u_east, v_south, mid, cells, absorb, light,
+    src, phys, wets, u_west, u_east, v_south, mid, edge, absorb, light,
     u_west2, u_east2, v_south2, mid2, absorb2, light2, fields,
 ):
     ny, ntr, nx, depth = own.shape
-    ry = ny + 4
+    inner = ny - 4
 
     def place(y, carry):
-        src[y + 4, :, 0:4, :] = west[y]
-        src[y + 4, :, 4:8, :] = own[y]
-        src[y + 4, :, 8:12, :] = east[y]
-        for f in range(5):
-            phys[f, y + 3, 0:10, :] = state[pl.ds((f * ny + y) * 10, 10), :]
-        return carry
-
-    lax.fori_loop(0, ny, place, 0)
-
+        for k, top, at in ((0, 0, 4), (1, ny - 4, 0)):
+            src[k, y + at, :, 0:4, :] = west[top + y]
+            src[k, y + at, :, 4:8, :] = own[top + y]
+            src[k, y + at, :, 8:12, :] = east[top + y]
+        return carry
+
+    lax.fori_loop(0, 4, place, 0)
     wing = 4 * ntr * nx
 
     def place_rows(t, carry):
         for j in range(4):
             at = pl.multiple_of((j * ntr + t) * 4, 4)
-            src[j, t, 4:8, :] = south_in[pl.ds(at, 4), :]
-            src[ny + 4 + j, t, 4:8, :] = north_in[pl.ds(at, 4), :]
+            src[0, j, t, 4:8, :] = south_in[pl.ds(at, 4), :]
+            src[1, 4 + j, t, 4:8, :] = north_in[pl.ds(at, 4), :]
         for j in range(2):
             at = wing + (j * ntr + t) * 4
-            src[2 + j, t, 2:4, :] = south_in[pl.ds(at, 2), :]
-            src[2 + j, t, 8:10, :] = south_in[pl.ds(at + 2, 2), :]
-            src[ny + 4 + j, t, 2:4, :] = north_in[pl.ds(at, 2), :]
-            src[ny + 4 + j, t, 8:10, :] = north_in[pl.ds(at + 2, 2), :]
+            src[0, 2 + j, t, 2:4, :] = south_in[pl.ds(at, 2), :]
+            src[0, 2 + j, t, 8:10, :] = south_in[pl.ds(at + 2, 2), :]
+            src[1, 4 + j, t, 2:4, :] = north_in[pl.ds(at, 2), :]
+            src[1, 4 + j, t, 8:10, :] = north_in[pl.ds(at + 2, 2), :]
         return carry
 
     lax.fori_loop(0, ntr, place_rows, 0)
     for f in range(5):
         for j in range(3):
             at = wing + wing // 2 + (f * 3 + j) * 10
-            phys[f, j, 0:10, :] = south_in[at : at + 10, :]
-            phys[f, ny + 3 + j, 0:10, :] = north_in[at : at + 10, :]
-
-    def get(f, row, shift):
-        return phys[f, row + 1, 1 + shift : 9 + shift, :]
-
-    def put(ref):
-        def store(row, value):
-            ref[row] = value
-
-        return store
-
-    def put_mid(row, temp, salt):
-        mid[0, row] = temp
-        mid[1, row] = salt
-
-    physics_rows(get, ry, put(u_west), put(u_east), put(v_south), put_mid)
-    advect_all(src, cells, 8, ry, u_west, u_east, v_south)
-    absorb_rows(cells, 8, ry, absorb)
-    dim_light(absorb, light, ry, 8)
-
-    def put_temp(row, value):
-        mid[0, row] = value
-
-    react_rows(
-        cells, 8, ry, absorb, light, lambda row: mid[0, row], lambda row: get(2, row, 0), put_temp
-    )
+            low, high = (f * ny + j) * 10, (f * ny + ny - 3 + j) * 10
+            phys[0, f, j, 0:10, :] = south_in[at : at + 10, :]
+            phys[0, f, 3 + j, 0:10, :] = state[low : low + 10, :]
+            phys[1, f, j, 0:10, :] = state[high : high + 10, :]
+            phys[1, f, 3 + j, 0:10, :] = north_in[at : at + 10, :]
+    wets[0] = phys[0, 2, 2]
+    wets[ny + 1] = phys[1, 2, 3]
+    for y in range(ny):
+        at = (2 * ny + y) * 10
+        wets[y + 1, 0:10, :] = state[at : at + 10, :]
+    for y in range(inner):
+        mid[0, 4 + y] = mid_in[0, y]
+        mid[1, 4 + y] = mid_in[1, y]
+        u_east[4 + y] = u_in[y]
+        v_south[4 + y] = v_in[y]
+
+    for k, at in ((0, 0), (1, inner + 4)):
+
+        def get(f, row, shift):
+            return phys[k, f, row + 1, 1 + shift : 9 + shift, :]
+
+        def put_mid(row, temp, salt):
+            mid[0, at + row] = temp
+            mid[1, at + row] = salt
+
+        here = pl.ds(at, 4)
+        faces = v_south.at[pl.ds(at, 5)]
+        physics_rows(
+            get,
+            4,
+            store_rows(u_west.at[pl.ds(4 * k, 4)]),
+            store_rows(u_east.at[here]),
+            store_rows(faces),
+            put_mid,
+        )
+        advect_all(
+            lambda e, t, x: src[k, e, t, x : x + 8, :],
+            edge.at[k],
+            8,
+            4,
+            u_west.at[pl.ds(4 * k, 4)],
+            u_east.at[here],
+            faces,
+        )
+        absorb_rows(edge.at[k], 8, 4, absorb.at[pl.ds(4 * k, 4)])
+    dim_light(absorb, light, 8, 8)
+    for k, at in ((0, 0), (1, inner + 4)):
+
+        def put_temp(row, value):
+            mid[0, at + row] = value
+
+        react_rows(
+            edge.at[k],
+            8,
+            4,
+            absorb.at[pl.ds(4 * k, 4)],
+            light.at[pl.ds(4 * k, 4)],
+            lambda row: mid[0, at + row],
+            lambda row: phys[k, 2, row + 1, 1:9, :],
+            put_temp,
+        )
 
     def get2(f, row, shift):
         cut = slice(2 + shift, 6 + shift)
         if f < 2:
             return mid[f, row + 2, cut, :]
         if f == 2:
-            return phys[2, row + 3, 3 + shift : 7 + shift, :]
+            return wets[row + 1, 3 + shift : 7 + shift, :]
         if f == 3:
             return u_east[row + 2, cut, :]
         return v_south[row + 3, cut, :]
 
+    def read2(e, t, x):
+        if e < 4:
+            return edge[0, e, t, x : x + 4, :]
+        if e < inner + 4:
+            return cells_in[e - 4, t, x : x + 4, :]
+        return edge[1, e - inner - 4, t, x : x + 4, :]
+
     def put_mid2(row, temp, salt):
         mid2[row] = temp
         fields[1, pl.ds(row * 4, 4), :] = salt
@@ -252,8 +335,8 @@
         u_east2[row] = value
         fields[2, pl.ds(row * 4, 4), :] = value
 
-    physics_rows(get2, ny, put(u_west2), put_east2, put(v_south2), put_mid2)
-    advect_all(cells, out, 4, ny, u_west2, u_east2, v_south2)
+    physics_rows(get2, ny, store_rows(u_west2), put_east2, store_rows(v_south2), put_mid2)
+    advect_all(read2, out, 4, ny, u_west2, u_east2, v_south2)
     absorb_rows(out, 4, ny, absorb2)
     dim_light(absorb2, light2, ny, 4)
 
@@ -277,51 +360,71 @@
         mail[g] = packed
 
 
-def run_two_steps(own, west, east, south, north, state):
+def run_inner(own, east, west, state):
+    ny, ntr, nx, depth = own.shape
+    rows = ny - 4
+    return call(
+        inner_rows,
+        [(rows, ntr, 8, depth), (rows, 8, depth), (rows + 1, 8, depth), (2, rows, 8, depth)],
+        own,
+        east,
+        west,
+        state,
+        name="inner_rows",
+        scratch=[
+            (ny, ntr, 16, depth),
+            (rows, 8, depth),
+            (rows, 8, depth),
+            (rows, 8, depth),
+        ],
+    )
+
+
+def run_outer(own, east, west, south, north, state, *inner):
     ny, ntr, nx, depth = own.shape
     ry = ny + 4
-    f32 = jnp.float32
-    vmem = pltpu.VMEM
-    whole = pl.BlockSpec(memory_space=pltpu.VMEM)
-    return pl.pallas_call(
-        two_steps,
-        out_shape=(
-            jax.ShapeDtypeStruct((ny, ntr, nx, depth), f32),
-            jax.ShapeDtypeStruct((4, ny * nx, depth), f32),
-        ),
-        in_specs=[whole] * 6,
-        out_specs=(whole, whole),
-        scratch_shapes=[
-            vmem((ny + 8, ntr, 16, depth), f32),
-            vmem((5, ny + 6, 16, depth), f32),
-            vmem((ry, 8, depth), f32),
-            vmem((ry, 8, depth), f32),
-            vmem((ry + 1, 8, depth), f32),
-            vmem((2, ry, 8, depth), f32),
-            vmem((ry, ntr, 8, depth), f32),
-            vmem((ry, 8, depth), f32),
-            vmem((ry, 8, depth), f32),
-            vmem((ny, nx, depth), f32),
-            vmem((ny, nx, depth), f32),
-            vmem((ny + 1, nx, depth), f32),
-            vmem((ny, nx, depth), f32),
-            vmem((ny, nx, depth), f32),
-            vmem((ny, nx, depth), f32),
-            vmem((4, ny * nx, depth), f32),
+    return call(
+        outer_rows,
+        [(ny, ntr, nx, depth), (4, ny * nx, depth)],
+        own,
+        east,
+        west,
+        south,
+        north,
+        state,
+        *inner,
+        name="outer_rows",
+        scratch=[
+            (2, 8, ntr, 16, depth),
+            (2, 5, 6, 16, depth),
+            (ny + 2, 16, depth),
+            (8, 8, depth),
+            (ry, 8, depth),
+            (ry + 1, 8, depth),
+            (2, ry, 8, depth),
+            (2, 4, ntr, 8, depth),
+            (8, 8, depth),
+            (8, 8, depth),
+            (ny, nx, depth),
+            (ny, nx, depth),
+            (ny + 1, nx, depth),
+            (ny, nx, depth),
+            (ny, nx, depth),
+            (ny, nx, depth),
+            (4, ny * nx, depth),
         ],
-        compiler_params=pltpu.CompilerParams(vmem_limit_bytes=40 * 1024 * 1024),
-        name="two_steps",
-    )(own, east, west, south, north, state)
-
-
-def call(body, out_shapes, *args, name):
+    )
+
+
+def call(body, out_shapes, *args, name, scratch=()):
     whole = pl.BlockSpec(memory_space=pltpu.VMEM)
     return pl.pallas_call(
         body,
         out_shape=tuple(jax.ShapeDtypeStruct(s, jnp.float32) for s in out_shapes),
         in_specs=[whole] * len(args),
         out_specs=(whole,) * len(out_shapes),
-        compiler_params=pltpu.CompilerParams(vmem_limit_bytes=16 * 1024 * 1024),
+        scratch_shapes=[pltpu.VMEM(shape, jnp.float32) for shape in scratch],
+        compiler_params=pltpu.CompilerParams(vmem_limit_bytes=40 * 1024 * 1024),
         name=name,
     )(*args)
 
@@ -431,7 +534,8 @@
     )
     south = ring_send(up, ROWS, 1)
     north = ring_send(down, ROWS, -1)
-    tracer, mail = run_two_steps(tracer, west_t, east_t, south, north, state)
+    inner = run_inner(tracer, east_t, west_t, state)
+    tracer, mail = run_outer(tracer, east_t, west_t, south, north, state, *inner)
     mail = lax.all_to_all(mail, "gy", split_axis=0, concat_axis=0, tiled=True)
     fields = call(
         unpack_levels,

time: 76.7 us -> 75.3 us (0.982)
  waiting for transfers between devices: 16.3 us -> 14.1 us
    pallas_call x4 -> x6, Pallas kernels: 1.91 us -> 9.93 us  [call(): pl.pallas_call(body, out_shape=tuple((jax.ShapeDtypeStruct(s, jnp.float32...]
    pallas_call x1 -> x0, Pallas kernels: 7.35 us -> none  [run_two_steps(): pl.pallas_call(two_steps, out_shape=(jax.ShapeDtypeStruct((ny, ntr, nx, d...]
    ppermute x6, waiting for transfers between devices: 15.3 us -> 13.2 us  [ring_send(): lax.ppermute(block, axis, [(i, (i + step) % count) for i in range(count)])]
  transfers between devices with their start and end apart: 7 -> 7, of which waited for: 4 -> 3; matrix products, arithmetic and copies ran while one was open for 0% -> 0% of each run, Pallas kernels for 1% -> 4%
where the time goes in v5:
time: 75.3 us; the launch traced here: 74.8 us
  starting transfers between devices  41.3 us (55%)
  waiting for transfers between devices  14.1 us (19%)
  Pallas kernels  9.93 us (13%)
  blocking collectives  6.58 us (9%)
  other arithmetic  1.16 us (2%)
  local copies, waits for them, and re-layouts  0.86 us (1%)
  between operations  0.79 us (1%)
    ppermute x6, starting transfers between devices, ring_send(): lax.ppermute(block, axis, [(i, (i + step) % count) for i in range(count)])  36.5 us
    ppermute x6, waiting for transfers between devices, ring_send(): lax.ppermute(block, axis, [(i, (i + step) % count) for i in range(count)])  13.2 us
    pallas_call x6, Pallas kernels, call(): pl.pallas_call(body, out_shape=tuple((jax.ShapeDtypeStruct(s, jnp.float32...  9.93 us
    all_to_all x1, blocking collectives, on_device(): mail = lax.all_to_all(mail, 'gy', split_axis=0, concat_axis=0, tiled=True)  6.58 us
    all_to_all x1, starting transfers between devices, on_device(): lax.all_to_all(mail.reshape(parts, 10 * ny, levels), 'gy', split_axis=0,...  4.88 us
  transfers between devices with their start and end apart: 7, of which 3 were waited for; matrix products, arithmetic and copies ran while one was open for 0% of the time, Pallas kernels for 4%

profile of v5, /device:TPU:1, one launch (start us, length us, event | category | flops | bytes accessed | tf_op | source)
XLA Modules:
  0.0 74.8 jit_solution(17911139867677140862)
XLA Ops:
  0.6 1.0 %pad_maximum_fusion.1 = f32[4,4,32,48]{3,2,0,1:T(8,128)S(1)} fusion(f32[4,1,32,48]{3,2,0,1:T(8,128)} %bitcast.30, f32[4,1,32,48]{3,2,0,1:T(8,128)} %bitcast.31, f32[4,1,32,48]{3,2,0,1:T(8,128)} %bitcast.32, f32[4,1,32,48]{3,2,0,1:T(8,128)} %bitcast.33), kind=kLoop, calls=%fused_computation.1 | loop fusion | flops 73728 | bytes 196608 | tf_op jit(solution)/shard_map/stack | solution.py:504
  1.6 0.0 copy-start.1
  1.6 0.0 copy-start.2
  1.6 0.6 copy-done.1
  2.3 0.0 copy-done.2
  2.3 0.0 copy-start
  2.3 0.1 pack_levels.1
  2.4 4.8 %collective-permute-start.2 = (f32[148,128]{1,0:T(8,128)S(1)}, f32[148,128]{1,0:T(8,128)S(1)}, u32[]{:S(2)}, u32[]{:S(2)}) collective-permute-start(f32[148,128]{1,0:T(8,128)S(1)} %get-tuple-element.22), channel_id=1, source_target_pairs={{0,4},{4,8},{8,12},{12,16},{16,20},{20,24},{24,28},{28,32},{32,36}... | collective-permute-start | bytes 227336 | tf_op jit(solution)/shard_map/ppermute | solution.py:35
  7.3 15.9 %collective-permute-start.3 = (f32[148,128]{1,0:T(8,128)S(1)}, f32[148,128]{1,0:T(8,128)S(1)}, u32[]{:S(2)}, u32[]{:S(2)}) collective-permute-start(f32[148,128]{1,0:T(8,128)S(1)} %get-tuple-element.23), channel_id=1, source_target_pairs={{0,188},{4,0},{8,4},{12,8},{16,12},{20,16},{24,20},{28,24},{32,28}... | collective-permute-start | bytes 227336 | tf_op jit(solution)/shard_map/ppermute | solution.py:35
  23.2 0.0 copy-done
  23.2 1.9 %collective-permute-start.1 = (f32[12,17,4,128]{3,2,1,0:T(4,128)S(1)}, f32[12,17,4,128]{3,2,1,0:T(4,128)S(1)}, u32[]{:S(2)}, u32[]{:S(2)}) collective-permute-start(f32[12,17,4,128]{3,2,1,0:T(4,128)S(1)} %bitcast.23), channel_id=1, source_target_pairs={{0,4},{4,8},{8,12},{12,16},{16,20},{20,24},{24,28},{28,32},{32,36}... | collective-permute-start | bytes 1253384 | tf_op jit(solution)/shard_map/ppermute | solution.py:35
  25.1 7.6 %collective-permute-start = (f32[12,17,4,128]{3,2,1,0:T(4,128)S(1)}, f32[12,17,4,128]{3,2,1,0:T(4,128)S(1)}, u32[]{:S(2)}, u32[]{:S(2)}) collective-permute-start(f32[12,17,4,128]{3,2,1,0:T(4,128)S(1)} %bitcast.24), channel_id=1, source_target_pairs={{0,188},{4,0},{8,4},{12,8},{16,12},{20,16},{24,20},{28,24},{32,28}... | collective-permute-start | bytes 1253384 | tf_op jit(solution)/shard_map/ppermute | solution.py:35
  32.7 0.0 collective-permute-done.2.west
  32.7 0.0 collective-permute-done.3.east
  32.8 0.7 stage_mail.1
  33.5 4.9 %all-to-all-start = ((f32[4,120,128]{2,1,0:T(8,128)}), f32[4,120,128]{2,1,0:T(8,128)S(1)}, u32[]{:S(2)}, u32[]{:S(2)}) async-start(f32[4,120,128]{2,1,0:T(8,128)} %bitcast.10), calls=%async_computation | async-start | bytes 491520 | tf_op jit(solution)/shard_map/all_to_all | solution.py:515
  38.4 0.1 fusion
  38.4 0.1 copy.38
  38.5 0.1 lt.15
  38.6 0.1 compare_convert_fusion.wet
  38.7 8.7 %collective-permute-done.1.west = f32[12,17,4,128]{3,2,1,0:T(4,128)S(1)} collective-permute-done((f32[12,17,4,128]{3,2,1,0:T(4,128)S(1)}, f32[12,17,4,128]{3,2,1,0:T(4,128)S(1)}, u32[]{:S(2)}, u32[]{:S(2)}) %collective-permute-start.1) | collective-permute-done | bytes 417824 | tf_op jit(solution)/shard_map/ppermute | solution.py:35
  47.4 0.0 collective-permute-done.east
  47.4 1.0 %all-to-all-done.mail = f32[4,120,128]{2,1,0:T(8,128)S(1)} async-done(((f32[4,120,128]{2,1,0:T(8,128)}), f32[4,120,128]{2,1,0:T(8,128)S(1)}, u32[]{:S(2)}, u32[]{:S(2)}) %all-to-all-start) | async-done | bytes 245792 | tf_op jit(solution)/shard_map/all_to_all | solution.py:515
  48.4 0.3 open_mail.1
  48.6 4.3 %collective-permute-start.4 = (f32[558,128]{1,0:T(8,128)S(1)}, f32[558,128]{1,0:T(8,128)S(1)}, u32[]{:S(2)}, u32[]{:S(2)}) collective-permute-start(f32[558,128]{1,0:T(8,128)S(1)} %get-tuple-element.24), channel_id=1, source_target_pairs={{0,1},{1,2},{2,3},{3,192},{192,193},{193,194},{194,195},{195,384},... | collective-permute-start | bytes 857096 | tf_op jit(solution)/shard_map/ppermute | solution.py:35
  53.0 1.9 %collective-permute-start.5 = (f32[558,128]{1,0:T(8,128)S(1)}, f32[558,128]{1,0:T(8,128)S(1)}, u32[]{:S(2)}, u32[]{:S(2)}) collective-permute-start(f32[558,128]{1,0:T(8,128)S(1)} %get-tuple-element.25), channel_id=1, source_target_pairs={{0,579},{1,0},{2,1},{3,2},{192,3},{193,192},{194,193},{195,194},{3... | collective-permute-start | bytes 857096 | tf_op jit(solution)/shard_map/ppermute | solution.py:35
  54.9 2.2 %inner_rows.1 = (f32[8,17,8,128]{3,2,1,0:T(8,128)S(1)}, f32[8,8,128]{2,1,0:T(8,128)S(1)}, f32[9,8,128]{2,1,0:T(8,128)S(1)}, f32[2,8,8,128]{3,2,1,0:T(8,128)S(1)}) custom-call(f32[12,17,4,128]{3,2,1,0:T(4,128)S(1)} %bitcast.26, f32[12,17,4,128]{3,2,1,0:T(4,128)S(1)} %collective-permute-done.east, f32[12,17,4,128]{3,2,1,0:T(4,128)S(1)} %collective-permute-done.1.west, ...), custom_call_target="tpu_custom_call" | custom-call | tf_op jit(solution)/shard_map/inner_rows/pallas_call | solution.py:421
  57.0 0.0 collective-permute-done.4.south_in
  57.0 4.5 %collective-permute-done.5.north_in = f32[558,128]{1,0:T(8,128)S(1)} collective-permute-done((f32[558,128]{1,0:T(8,128)S(1)}, f32[558,128]{1,0:T(8,128)S(1)}, u32[]{:S(2)}, u32[]{:S(2)}) %collective-permute-start.5) | collective-permute-done | bytes 285728 | tf_op jit(solution)/shard_map/ppermute | solution.py:35
  61.5 5.9 %outer_rows.1 = (f32[12,17,4,128]{3,2,1,0:T(4,128)}, f32[4,48,128]{2,1,0:T(8,128)S(1)}) custom-call(f32[12,17,4,128]{3,2,1,0:T(4,128)S(1)} %bitcast.27, f32[12,17,4,128]{3,2,1,0:T(4,128)S(1)} %collective-permute-done.east, f32[12,17,4,128]{3,2,1,0:T(4,128)S(1)} %collective-permute-done.1.west, f32[558,128]{1,0:T(8,128)S(1)} %collective-permute-done.4.south_in, ...), custom_call_target="tpu_custom_call" | custom-call | tf_op jit(solution)/shard_map/outer_rows/pallas_call | solution.py:421
  67.4 6.6 %all_to_all.10 = f32[4,48,128]{2,1,0:T(8,128)S(1)} all-to-all(f32[4,48,128]{2,1,0:T(8,128)S(1)} %get-tuple-element.31), channel_id=1, replica_groups=mesh['grp'=4,'gx'=48,'gy'=4] {'gy'}, dimensions={0} | all-to-all | bytes 196608 | tf_op jit(solution)/shard_map/all_to_all | solution.py:539
  74.0 0.8 %unpack_levels.1 = (f32[4,32,48]{2,1,0:T(8,128)}, f32[4,32,48]{2,1,0:T(8,128)}, f32[4,32,48]{2,1,0:T(8,128)}, f32[4,32,48]{2,1,0:T(8,128)}) custom-call(f32[192,128]{1,0:T(8,128)S(1)} %bitcast.28), custom_call_target="tpu_custom_call" | custom-call | tf_op jit(solution)/shard_map/unpack_levels/pallas_call | solution.py:421
  (6 shorter events, 0.1 us)
Async XLA Ops:
  1.6 0.7 copy-start.1
  1.6 0.7 copy-start.2
  2.3 20.9 %copy-start = (f32[4,12,17,128]{3,0,2,1:T(4,128)S(1)}, f32[4,12,17,128]{3,0,2,1:T(4,128)}, u32[]{:S(2)}) copy-start(f32[4,12,17,128]{3,0,2,1:T(4,128)} %param.11) | copy-start | bytes 1253380
  2.4 30.3 %collective-permute-start.2 = (f32[148,128]{1,0:T(8,128)S(1)}, f32[148,128]{1,0:T(8,128)S(1)}, u32[]{:S(2)}, u32[]{:S(2)}) collective-permute-start(f32[148,128]{1,0:T(8,128)S(1)} %get-tuple-element.22), channel_id=1, source_target_pairs={{0,4},{4,8},{8,12},{12,16},{16,20},{20,24},{24,28},{28,32},{32,36}... | collective-permute-start | bytes 227336 | tf_op jit(solution)/shard_map/ppermute | solution.py:35
  7.3 25.5 %collective-permute-start.3 = (f32[148,128]{1,0:T(8,128)S(1)}, f32[148,128]{1,0:T(8,128)S(1)}, u32[]{:S(2)}, u32[]{:S(2)}) collective-permute-start(f32[148,128]{1,0:T(8,128)S(1)} %get-tuple-element.23), channel_id=1, source_target_pairs={{0,188},{4,0},{8,4},{12,8},{16,12},{20,16},{24,20},{28,24},{32,28}... | collective-permute-start | bytes 227336 | tf_op jit(solution)/shard_map/ppermute | solution.py:35
  23.2 24.2 %collective-permute-start.1 = (f32[12,17,4,128]{3,2,1,0:T(4,128)S(1)}, f32[12,17,4,128]{3,2,1,0:T(4,128)S(1)}, u32[]{:S(2)}, u32[]{:S(2)}) collective-permute-start(f32[12,17,4,128]{3,2,1,0:T(4,128)S(1)} %bitcast.23), channel_id=1, source_target_pairs={{0,4},{4,8},{8,12},{12,16},{16,20},{20,24},{24,28},{28,32},{32,36}... | collective-permute-start | bytes 1253384 | tf_op jit(solution)/shard_map/ppermute | solution.py:35
  25.1 22.3 %collective-permute-start = (f32[12,17,4,128]{3,2,1,0:T(4,128)S(1)}, f32[12,17,4,128]{3,2,1,0:T(4,128)S(1)}, u32[]{:S(2)}, u32[]{:S(2)}) collective-permute-start(f32[12,17,4,128]{3,2,1,0:T(4,128)S(1)} %bitcast.24), channel_id=1, source_target_pairs={{0,188},{4,0},{8,4},{12,8},{16,12},{20,16},{24,20},{28,24},{32,28}... | collective-permute-start | bytes 1253384 | tf_op jit(solution)/shard_map/ppermute | solution.py:35
  33.5 14.9 %all-to-all-start = ((f32[4,120,128]{2,1,0:T(8,128)}), f32[4,120,128]{2,1,0:T(8,128)S(1)}, u32[]{:S(2)}, u32[]{:S(2)}) async-start(f32[4,120,128]{2,1,0:T(8,128)} %bitcast.10), calls=%async_computation | async-start | bytes 491520 | tf_op jit(solution)/shard_map/all_to_all | solution.py:515
  48.6 8.4 %collective-permute-start.4 = (f32[558,128]{1,0:T(8,128)S(1)}, f32[558,128]{1,0:T(8,128)S(1)}, u32[]{:S(2)}, u32[]{:S(2)}) collective-permute-start(f32[558,128]{1,0:T(8,128)S(1)} %get-tuple-element.24), channel_id=1, source_target_pairs={{0,1},{1,2},{2,3},{3,192},{192,193},{193,194},{194,195},{195,384},... | collective-permute-start | bytes 857096 | tf_op jit(solution)/shard_map/ppermute | solution.py:35
  53.0 8.6 %collective-permute-start.5 = (f32[558,128]{1,0:T(8,128)S(1)}, f32[558,128]{1,0:T(8,128)S(1)}, u32[]{:S(2)}, u32[]{:S(2)}) collective-permute-start(f32[558,128]{1,0:T(8,128)S(1)} %get-tuple-element.25), channel_id=1, source_target_pairs={{0,579},{1,0},{2,1},{3,2},{192,3},{193,192},{194,193},{195,194},{3... | collective-permute-start | bytes 857096 | tf_op jit(solution)/shard_map/ppermute | solution.py:35

commit v6 on v5

--- a/solution.py
+++ b/solution.py
@@ -429,7 +429,7 @@
     )(*args)
 
 
-def pack_levels(stacked, own, to_east, to_west):
+def pack_levels(stacked, tracer, own, to_east, to_west):
     span = stacked.shape[1]
     depth = own.shape[1]
     nx = own.shape[0] // span
@@ -443,6 +443,13 @@
     for ref in (to_east, to_west):
         ref[3 * span : 3 * span + nx, :] = jnp.zeros((nx, depth), jnp.float32)
         ref[3 * span : 3 * span + nx, 0:span] = stacked[nx * depth :, :]
+    ny, ntr = tracer.shape[:2]
+    base = 3 * span + nx
+    for k, line in enumerate((0, 1, ny - 2, ny - 1)):
+        for t in range(ntr):
+            at = base + (k * ntr + t) * 2
+            to_east[at : at + 2, :] = tracer[line, t, nx - 2 :, :]
+            to_west[at : at + 2, :] = tracer[line, t, :2, :]
 
 
 def stage_mail(own, west, east, mail):
@@ -472,13 +479,16 @@
             up[at : at + 4, :] = own[ny - 4 + j, t]
             down[at : at + 4, :] = own[j, t]
     base = 16 * ntr
+    first = west.shape[0] - 8 * ntr
     for j in range(2):
         for t in range(ntr):
             at = base + (j * ntr + t) * 4
-            up[at : at + 2, :] = west[ny - 2 + j, t, 2:4, :]
-            up[at + 2 : at + 4, :] = east[ny - 2 + j, t, 0:2, :]
-            down[at : at + 2, :] = west[j, t, 2:4, :]
-            down[at + 2 : at + 4, :] = east[j, t, 0:2, :]
+            low = first + (j * ntr + t) * 2
+            high = low + 4 * ntr
+            up[at : at + 2, :] = west[high : high + 2, :]
+            up[at + 2 : at + 4, :] = east[high : high + 2, :]
+            down[at : at + 2, :] = west[low : low + 2, :]
+            down[at + 2 : at + 4, :] = east[low : low + 2, :]
     base = 24 * ntr
     for f in range(5):
         up[base + f * 30 : base + f * 30 + 30, :] = state[(f + 1) * cells - 30 : (f + 1) * cells, :]
@@ -503,9 +513,9 @@
     deep = jnp.where(mask > 0, bottom, 0).astype(jnp.float32)
     stacked = jnp.stack([f.transpose(0, 2, 1) for f in (temp, salt, east, north)], axis=1)
     stacked = jnp.concatenate([stacked.reshape(nx * levels, span), deep], axis=0)
-    side = (3 * span + nx, levels)
+    side = (3 * span + nx + 8 * ntr, levels)
     own, to_east, to_west = call(
-        pack_levels, [(nx * span, levels), side, side], stacked, name="pack_levels"
+        pack_levels, [(nx * span, levels), side, side], stacked, tracer, name="pack_levels"
     )
     west_p = ring_send(to_east, "gx", 1)
     west_t = ring_send(tracer, "gx", 1)
@@ -528,8 +538,8 @@
         mail,
         wet,
         tracer,
-        east_t,
-        west_t,
+        east_p,
+        west_p,
         name="open_mail",
     )
     south = ring_send(up, ROWS, 1)

time: 75.3 us -> 74.7 us (level)
    ppermute x6, waiting for transfers between devices: 13.2 us -> 3.85 us  [ring_send(): lax.ppermute(block, axis, [(i, (i + step) % count) for i in range(count)])]
    all_to_all x1, waiting for transfers between devices: 0.95 us -> 9.63 us  [on_device(): lax.all_to_all(mail.reshape(parts, 10 * ny, levels), 'gy', split_axis=0,...]
  transfers between devices with their start and end apart: 7 -> 7, of which waited for: 3 -> 2; matrix products, arithmetic and copies ran while one was open for 0% -> 0% of each run, Pallas kernels for 4% -> 4%
where the time goes in v6:
time: 74.7 us; the launch traced here: 74.2 us
  starting transfers between devices  41.3 us (55%)
  waiting for transfers between devices  13.5 us (18%)
  Pallas kernels  9.95 us (13%)
  blocking collectives  6.31 us (8%)
  other arithmetic  1.16 us (2%)
  local copies, waits for them, and re-layouts  1.16 us (2%)
  between operations  0.8 us (1%)
    ppermute x6, starting transfers between devices, ring_send(): lax.ppermute(block, axis, [(i, (i + step) % count) for i in range(count)])  36.5 us
    pallas_call x6, Pallas kernels, call(): pl.pallas_call(body, out_shape=tuple((jax.ShapeDtypeStruct(s, jnp.float32...  9.95 us
    all_to_all x1, waiting for transfers between devices, on_device(): lax.all_to_all(mail.reshape(parts, 10 * ny, levels), 'gy', split_axis=0,...  9.63 us
    all_to_all x1, blocking collectives, on_device(): mail = lax.all_to_all(mail, 'gy', split_axis=0, concat_axis=0, tiled=True)  6.31 us
    all_to_all x1, starting transfers between devices, on_device(): lax.all_to_all(mail.reshape(parts, 10 * ny, levels), 'gy', split_axis=0,...  4.88 us
    ppermute x6, waiting for transfers between devices, ring_send(): lax.ppermute(block, axis, [(i, (i + step) % count) for i in range(count)])  3.85 us
  transfers between devices with their start and end apart: 7, of which 2 were waited for; matrix products, arithmetic and copies ran while one was open for 0% of the time, Pallas kernels for 4%

profile of v6, /device:TPU:1, one launch (start us, length us, event | category | flops | bytes accessed | tf_op | source)
XLA Modules:
  0.0 74.2 jit_solution(5641169382641584460)
XLA Ops:
  0.6 1.0 %pad_maximum_fusion.1 = f32[4,4,32,48]{3,2,0,1:T(8,128)S(1)} fusion(f32[4,1,32,48]{3,2,0,1:T(8,128)} %bitcast.31, f32[4,1,32,48]{3,2,0,1:T(8,128)} %bitcast.32, f32[4,1,32,48]{3,2,0,1:T(8,128)} %bitcast.33, f32[4,1,32,48]{3,2,0,1:T(8,128)} %bitcast.34), kind=kLoop, calls=%fused_computation.1 | loop fusion | flops 73728 | bytes 196608 | tf_op jit(solution)/shard_map/stack | solution.py:514
  1.6 0.0 copy-start.1
  1.6 0.0 copy-start.2
  1.6 0.0 copy-start
  1.7 0.6 copy-done.1
  2.3 0.0 copy-done.2
  2.3 0.3 copy-done
  2.6 0.1 pack_levels.1
  2.8 4.8 %collective-permute-start.2 = (f32[284,128]{1,0:T(8,128)S(1)}, f32[284,128]{1,0:T(8,128)S(1)}, u32[]{:S(2)}, u32[]{:S(2)}) collective-permute-start(f32[284,128]{1,0:T(8,128)S(1)} %get-tuple-element.22), channel_id=1, source_target_pairs={{0,4},{4,8},{8,12},{12,16},{16,20},{20,24},{24,28},{28,32},{32,36}... | collective-permute-start | bytes 436232 | tf_op jit(solution)/shard_map/ppermute | solution.py:35
  7.6 15.9 %collective-permute-start.3 = (f32[284,128]{1,0:T(8,128)S(1)}, f32[284,128]{1,0:T(8,128)S(1)}, u32[]{:S(2)}, u32[]{:S(2)}) collective-permute-start(f32[284,128]{1,0:T(8,128)S(1)} %get-tuple-element.23), channel_id=1, source_target_pairs={{0,188},{4,0},{8,4},{12,8},{16,12},{20,16},{24,20},{28,24},{32,28}... | collective-permute-start | bytes 436232 | tf_op jit(solution)/shard_map/ppermute | solution.py:35
  23.5 1.9 %collective-permute-start.1 = (f32[12,17,4,128]{3,2,1,0:T(4,128)S(1)}, f32[12,17,4,128]{3,2,1,0:T(4,128)S(1)}, u32[]{:S(2)}, u32[]{:S(2)}) collective-permute-start(f32[12,17,4,128]{3,2,1,0:T(4,128)S(1)} %bitcast.24), channel_id=1, source_target_pairs={{0,4},{4,8},{8,12},{12,16},{16,20},{20,24},{24,28},{28,32},{32,36}... | collective-permute-start | bytes 1253384 | tf_op jit(solution)/shard_map/ppermute | solution.py:35
  25.5 7.6 %collective-permute-start = (f32[12,17,4,128]{3,2,1,0:T(4,128)S(1)}, f32[12,17,4,128]{3,2,1,0:T(4,128)S(1)}, u32[]{:S(2)}, u32[]{:S(2)}) collective-permute-start(f32[12,17,4,128]{3,2,1,0:T(4,128)S(1)} %bitcast.25), channel_id=1, source_target_pairs={{0,188},{4,0},{8,4},{12,8},{16,12},{20,16},{24,20},{28,24},{32,28}... | collective-permute-start | bytes 1253384 | tf_op jit(solution)/shard_map/ppermute | solution.py:35
  33.1 0.0 collective-permute-done.2.west
  33.1 0.0 collective-permute-done.3.east
  33.1 0.7 stage_mail.1
  33.8 4.9 %all-to-all-start = ((f32[4,120,128]{2,1,0:T(8,128)}), f32[4,120,128]{2,1,0:T(8,128)S(1)}, u32[]{:S(2)}, u32[]{:S(2)}) async-start(f32[4,120,128]{2,1,0:T(8,128)} %bitcast.10), calls=%async_computation | async-start | bytes 491520 | tf_op jit(solution)/shard_map/all_to_all | solution.py:525
  38.7 0.1 fusion
  38.8 0.1 copy.38
  38.9 0.1 lt.15
  38.9 0.1 compare_convert_fusion.wet
  39.0 9.6 %all-to-all-done.mail = f32[4,120,128]{2,1,0:T(8,128)S(1)} async-done(((f32[4,120,128]{2,1,0:T(8,128)}), f32[4,120,128]{2,1,0:T(8,128)S(1)}, u32[]{:S(2)}, u32[]{:S(2)}) %all-to-all-start) | async-done | bytes 245792 | tf_op jit(solution)/shard_map/all_to_all | solution.py:525
  48.7 0.3 open_mail.1
  49.0 4.3 %collective-permute-start.4 = (f32[558,128]{1,0:T(8,128)S(1)}, f32[558,128]{1,0:T(8,128)S(1)}, u32[]{:S(2)}, u32[]{:S(2)}) collective-permute-start(f32[558,128]{1,0:T(8,128)S(1)} %get-tuple-element.24), channel_id=1, source_target_pairs={{0,1},{1,2},{2,3},{3,192},{192,193},{193,194},{194,195},{195,384},... | collective-permute-start | bytes 857096 | tf_op jit(solution)/shard_map/ppermute | solution.py:35
  53.3 1.9 %collective-permute-start.5 = (f32[558,128]{1,0:T(8,128)S(1)}, f32[558,128]{1,0:T(8,128)S(1)}, u32[]{:S(2)}, u32[]{:S(2)}) collective-permute-start(f32[558,128]{1,0:T(8,128)S(1)} %get-tuple-element.25), channel_id=1, source_target_pairs={{0,579},{1,0},{2,1},{3,2},{192,3},{193,192},{194,193},{195,194},{3... | collective-permute-start | bytes 857096 | tf_op jit(solution)/shard_map/ppermute | solution.py:35
  55.2 0.0 collective-permute-done.1.west
  55.2 0.0 collective-permute-done.east
  55.2 2.2 %inner_rows.1 = (f32[8,17,8,128]{3,2,1,0:T(8,128)S(1)}, f32[8,8,128]{2,1,0:T(8,128)S(1)}, f32[9,8,128]{2,1,0:T(8,128)S(1)}, f32[2,8,8,128]{3,2,1,0:T(8,128)S(1)}) custom-call(f32[12,17,4,128]{3,2,1,0:T(4,128)S(1)} %bitcast.27, f32[12,17,4,128]{3,2,1,0:T(4,128)S(1)} %collective-permute-done.east, f32[12,17,4,128]{3,2,1,0:T(4,128)S(1)} %collective-permute-done.1.west, ...), custom_call_target="tpu_custom_call" | custom-call | tf_op jit(solution)/shard_map/inner_rows/pallas_call | solution.py:421
  57.4 0.0 collective-permute-done.4.south_in
  57.4 3.8 %collective-permute-done.5.north_in = f32[558,128]{1,0:T(8,128)S(1)} collective-permute-done((f32[558,128]{1,0:T(8,128)S(1)}, f32[558,128]{1,0:T(8,128)S(1)}, u32[]{:S(2)}, u32[]{:S(2)}) %collective-permute-start.5) | collective-permute-done | bytes 285728 | tf_op jit(solution)/shard_map/ppermute | solution.py:35
  61.2 5.9 %outer_rows.1 = (f32[12,17,4,128]{3,2,1,0:T(4,128)}, f32[4,48,128]{2,1,0:T(8,128)S(1)}) custom-call(f32[12,17,4,128]{3,2,1,0:T(4,128)S(1)} %bitcast.28, f32[12,17,4,128]{3,2,1,0:T(4,128)S(1)} %collective-permute-done.east, f32[12,17,4,128]{3,2,1,0:T(4,128)S(1)} %collective-permute-done.1.west, f32[558,128]{1,0:T(8,128)S(1)} %collective-permute-done.4.south_in, ...), custom_call_target="tpu_custom_call" | custom-call | tf_op jit(solution)/shard_map/outer_rows/pallas_call | solution.py:421
  67.1 6.3 %all_to_all.10 = f32[4,48,128]{2,1,0:T(8,128)S(1)} all-to-all(f32[4,48,128]{2,1,0:T(8,128)S(1)} %get-tuple-element.31), channel_id=1, replica_groups=mesh['grp'=4,'gx'=48,'gy'=4] {'gy'}, dimensions={0} | all-to-all | bytes 196608 | tf_op jit(solution)/shard_map/all_to_all | solution.py:549
  73.4 0.8 %unpack_levels.1 = (f32[4,32,48]{2,1,0:T(8,128)}, f32[4,32,48]{2,1,0:T(8,128)}, f32[4,32,48]{2,1,0:T(8,128)}, f32[4,32,48]{2,1,0:T(8,128)}) custom-call(f32[192,128]{1,0:T(8,128)S(1)} %bitcast.29), custom_call_target="tpu_custom_call" | custom-call | tf_op jit(solution)/shard_map/unpack_levels/pallas_call | solution.py:421
  (6 shorter events, 0.1 us)
Async XLA Ops:
  1.6 0.7 copy-start.1
  1.6 0.7 copy-start.2
  1.6 1.0 %copy-start = (f32[4,12,17,128]{3,0,2,1:T(4,128)S(1)}, f32[4,12,17,128]{3,0,2,1:T(4,128)}, u32[]{:S(2)}) copy-start(f32[4,12,17,128]{3,0,2,1:T(4,128)} %param.11) | copy-start | bytes 1253380
  2.8 30.3 %collective-permute-start.2 = (f32[284,128]{1,0:T(8,128)S(1)}, f32[284,128]{1,0:T(8,128)S(1)}, u32[]{:S(2)}, u32[]{:S(2)}) collective-permute-start(f32[284,128]{1,0:T(8,128)S(1)} %get-tuple-element.22), channel_id=1, source_target_pairs={{0,4},{4,8},{8,12},{12,16},{16,20},{20,24},{24,28},{28,32},{32,36}... | collective-permute-start | bytes 436232 | tf_op jit(solution)/shard_map/ppermute | solution.py:35
  7.6 25.5 %collective-permute-start.3 = (f32[284,128]{1,0:T(8,128)S(1)}, f32[284,128]{1,0:T(8,128)S(1)}, u32[]{:S(2)}, u32[]{:S(2)}) collective-permute-start(f32[284,128]{1,0:T(8,128)S(1)} %get-tuple-element.23), channel_id=1, source_target_pairs={{0,188},{4,0},{8,4},{12,8},{16,12},{20,16},{24,20},{28,24},{32,28}... | collective-permute-start | bytes 436232 | tf_op jit(solution)/shard_map/ppermute | solution.py:35
  23.5 31.7 %collective-permute-start.1 = (f32[12,17,4,128]{3,2,1,0:T(4,128)S(1)}, f32[12,17,4,128]{3,2,1,0:T(4,128)S(1)}, u32[]{:S(2)}, u32[]{:S(2)}) collective-permute-start(f32[12,17,4,128]{3,2,1,0:T(4,128)S(1)} %bitcast.24), channel_id=1, source_target_pairs={{0,4},{4,8},{8,12},{12,16},{16,20},{20,24},{24,28},{28,32},{32,36}... | collective-permute-start | bytes 1253384 | tf_op jit(solution)/shard_map/ppermute | solution.py:35
  25.5 29.7 %collective-permute-start = (f32[12,17,4,128]{3,2,1,0:T(4,128)S(1)}, f32[12,17,4,128]{3,2,1,0:T(4,128)S(1)}, u32[]{:S(2)}, u32[]{:S(2)}) collective-permute-start(f32[12,17,4,128]{3,2,1,0:T(4,128)S(1)} %bitcast.25), channel_id=1, source_target_pairs={{0,188},{4,0},{8,4},{12,8},{16,12},{20,16},{24,20},{28,24},{32,28}... | collective-permute-start | bytes 1253384 | tf_op jit(solution)/shard_map/ppermute | solution.py:35
  33.8 14.9 %all-to-all-start = ((f32[4,120,128]{2,1,0:T(8,128)}), f32[4,120,128]{2,1,0:T(8,128)S(1)}, u32[]{:S(2)}, u32[]{:S(2)}) async-start(f32[4,120,128]{2,1,0:T(8,128)} %bitcast.10), calls=%async_computation | async-start | bytes 491520 | tf_op jit(solution)/shard_map/all_to_all | solution.py:525
  49.0 8.4 %collective-permute-start.4 = (f32[558,128]{1,0:T(8,128)S(1)}, f32[558,128]{1,0:T(8,128)S(1)}, u32[]{:S(2)}, u32[]{:S(2)}) collective-permute-start(f32[558,128]{1,0:T(8,128)S(1)} %get-tuple-element.24), channel_id=1, source_target_pairs={{0,1},{1,2},{2,3},{3,192},{192,193},{193,194},{194,195},{195,384},... | collective-permute-start | bytes 857096 | tf_op jit(solution)/shard_map/ppermute | solution.py:35
  53.3 8.0 %collective-permute-start.5 = (f32[558,128]{1,0:T(8,128)S(1)}, f32[558,128]{1,0:T(8,128)S(1)}, u32[]{:S(2)}, u32[]{:S(2)}) collective-permute-start(f32[558,128]{1,0:T(8,128)S(1)} %get-tuple-element.25), channel_id=1, source_target_pairs={{0,579},{1,0},{2,1},{3,2},{192,3},{193,192},{194,193},{195,194},{3... | collective-permute-start | bytes 857096 | tf_op jit(solution)/shard_map/ppermute | solution.py:35

commit v7 on v6

--- a/solution.py
+++ b/solution.py
@@ -77,7 +77,7 @@
         put_mid(row, *fresh)
         return carry
 
-    lax.fori_loop(0, rows, body, 0)
+    lax.fori_loop(0, rows, body, 0, unroll=True)
     put_south(rows, face_y(rows - 1))
 
 
@@ -122,7 +122,7 @@
         absorb[row, :, :] = WATER_ATT + CHLORO_ATT * jnp.abs(chloro)
         return carry
 
-    lax.fori_loop(0, rows, body, 0)
+    lax.fori_loop(0, rows, body, 0, unroll=True)
 
 
 def dim_light(absorb, light, rows, width):
@@ -165,7 +165,7 @@
         put_temp(row, mid + HEATING * absorb[row] * lit * wet)
         return carry
 
-    lax.fori_loop(0, rows, body, 0)
+    lax.fori_loop(0, rows, body, 0, unroll=True)
 
 
 def store_rows(ref):

time: 74.7 us -> 74 us (level)
  Pallas kernels: 9.95 us -> 9.02 us
    pallas_call x6, Pallas kernels: 9.95 us -> 9.02 us  [call(): pl.pallas_call(body, out_shape=tuple((jax.ShapeDtypeStruct(s, jnp.float32...]
where the time goes in v7:
time: 74 us; the launch traced here: 73.6 us
  starting transfers between devices  41.3 us (56%)
  waiting for transfers between devices  13.8 us (19%)
  Pallas kernels  9.02 us (12%)
  blocking collectives  6.31 us (9%)
  other arithmetic  1.16 us (2%)
  local copies, waits for them, and re-layouts  1.16 us (2%)
  between operations  0.8 us (1%)
    ppermute x6, starting transfers between devices, ring_send(): lax.ppermute(block, axis, [(i, (i + step) % count) for i in range(count)])  36.5 us
    all_to_all x1, waiting for transfers between devices, on_device(): lax.all_to_all(mail.reshape(parts, 10 * ny, levels), 'gy', split_axis=0,...  9.63 us
    pallas_call x6, Pallas kernels, call(): pl.pallas_call(body, out_shape=tuple((jax.ShapeDtypeStruct(s, jnp.float32...  9.02 us
    all_to_all x1, blocking collectives, on_device(): mail = lax.all_to_all(mail, 'gy', split_axis=0, concat_axis=0, tiled=True)  6.31 us
    all_to_all x1, starting transfers between devices, on_device(): lax.all_to_all(mail.reshape(parts, 10 * ny, levels), 'gy', split_axis=0,...  4.88 us
    ppermute x6, waiting for transfers between devices, ring_send(): lax.ppermute(block, axis, [(i, (i + step) % count) for i in range(count)])  4.17 us
  transfers between devices with their start and end apart: 7, of which 2 were waited for; matrix products, arithmetic and copies ran while one was open for 0% of the time, Pallas kernels for 4%

profile of v7, /device:TPU:1, one launch (start us, length us, event | category | flops | bytes accessed | tf_op | source)
XLA Modules:
  0.0 73.6 jit_solution(13870975210674286748)
XLA Ops:
  0.6 1.0 %pad_maximum_fusion.1 = f32[4,4,32,48]{3,2,0,1:T(8,128)S(1)} fusion(f32[4,1,32,48]{3,2,0,1:T(8,128)} %bitcast.31, f32[4,1,32,48]{3,2,0,1:T(8,128)} %bitcast.32, f32[4,1,32,48]{3,2,0,1:T(8,128)} %bitcast.33, f32[4,1,32,48]{3,2,0,1:T(8,128)} %bitcast.34), kind=kLoop, calls=%fused_computation.1 | loop fusion | flops 73728 | bytes 196608 | tf_op jit(solution)/shard_map/stack | solution.py:514
  1.6 0.0 copy-start.1
  1.6 0.0 copy-start.2
  1.6 0.0 copy-start
  1.7 0.6 copy-done.1
  2.3 0.0 copy-done.2
  2.3 0.3 copy-done
  2.6 0.1 pack_levels.1
  2.8 4.8 %collective-permute-start.2 = (f32[284,128]{1,0:T(8,128)S(1)}, f32[284,128]{1,0:T(8,128)S(1)}, u32[]{:S(2)}, u32[]{:S(2)}) collective-permute-start(f32[284,128]{1,0:T(8,128)S(1)} %get-tuple-element.22), channel_id=1, source_target_pairs={{0,4},{4,8},{8,12},{12,16},{16,20},{20,24},{24,28},{28,32},{32,36}... | collective-permute-start | bytes 436232 | tf_op jit(solution)/shard_map/ppermute | solution.py:35
  7.6 15.9 %collective-permute-start.3 = (f32[284,128]{1,0:T(8,128)S(1)}, f32[284,128]{1,0:T(8,128)S(1)}, u32[]{:S(2)}, u32[]{:S(2)}) collective-permute-start(f32[284,128]{1,0:T(8,128)S(1)} %get-tuple-element.23), channel_id=1, source_target_pairs={{0,188},{4,0},{8,4},{12,8},{16,12},{20,16},{24,20},{28,24},{32,28}... | collective-permute-start | bytes 436232 | tf_op jit(solution)/shard_map/ppermute | solution.py:35
  23.5 1.9 %collective-permute-start.1 = (f32[12,17,4,128]{3,2,1,0:T(4,128)S(1)}, f32[12,17,4,128]{3,2,1,0:T(4,128)S(1)}, u32[]{:S(2)}, u32[]{:S(2)}) collective-permute-start(f32[12,17,4,128]{3,2,1,0:T(4,128)S(1)} %bitcast.24), channel_id=1, source_target_pairs={{0,4},{4,8},{8,12},{12,16},{16,20},{20,24},{24,28},{28,32},{32,36}... | collective-permute-start | bytes 1253384 | tf_op jit(solution)/shard_map/ppermute | solution.py:35
  25.5 7.6 %collective-permute-start = (f32[12,17,4,128]{3,2,1,0:T(4,128)S(1)}, f32[12,17,4,128]{3,2,1,0:T(4,128)S(1)}, u32[]{:S(2)}, u32[]{:S(2)}) collective-permute-start(f32[12,17,4,128]{3,2,1,0:T(4,128)S(1)} %bitcast.25), channel_id=1, source_target_pairs={{0,188},{4,0},{8,4},{12,8},{16,12},{20,16},{24,20},{28,24},{32,28}... | collective-permute-start | bytes 1253384 | tf_op jit(solution)/shard_map/ppermute | solution.py:35
  33.1 0.0 collective-permute-done.2.west
  33.1 0.0 collective-permute-done.3.east
  33.1 0.7 stage_mail.1
  33.8 4.9 %all-to-all-start = ((f32[4,120,128]{2,1,0:T(8,128)}), f32[4,120,128]{2,1,0:T(8,128)S(1)}, u32[]{:S(2)}, u32[]{:S(2)}) async-start(f32[4,120,128]{2,1,0:T(8,128)} %bitcast.10), calls=%async_computation | async-start | bytes 491520 | tf_op jit(solution)/shard_map/all_to_all | solution.py:525
  38.7 0.1 fusion
  38.8 0.1 copy.38
  38.9 0.1 lt.15
  38.9 0.1 compare_convert_fusion.wet
  39.0 9.6 %all-to-all-done.mail = f32[4,120,128]{2,1,0:T(8,128)S(1)} async-done(((f32[4,120,128]{2,1,0:T(8,128)}), f32[4,120,128]{2,1,0:T(8,128)S(1)}, u32[]{:S(2)}, u32[]{:S(2)}) %all-to-all-start) | async-done | bytes 245792 | tf_op jit(solution)/shard_map/all_to_all | solution.py:525
  48.7 0.3 open_mail.1
  49.0 4.3 %collective-permute-start.4 = (f32[558,128]{1,0:T(8,128)S(1)}, f32[558,128]{1,0:T(8,128)S(1)}, u32[]{:S(2)}, u32[]{:S(2)}) collective-permute-start(f32[558,128]{1,0:T(8,128)S(1)} %get-tuple-element.24), channel_id=1, source_target_pairs={{0,1},{1,2},{2,3},{3,192},{192,193},{193,194},{194,195},{195,384},... | collective-permute-start | bytes 857096 | tf_op jit(solution)/shard_map/ppermute | solution.py:35
  53.3 1.9 %collective-permute-start.5 = (f32[558,128]{1,0:T(8,128)S(1)}, f32[558,128]{1,0:T(8,128)S(1)}, u32[]{:S(2)}, u32[]{:S(2)}) collective-permute-start(f32[558,128]{1,0:T(8,128)S(1)} %get-tuple-element.25), channel_id=1, source_target_pairs={{0,579},{1,0},{2,1},{3,2},{192,3},{193,192},{194,193},{195,194},{3... | collective-permute-start | bytes 857096 | tf_op jit(solution)/shard_map/ppermute | solution.py:35
  55.2 0.0 collective-permute-done.1.west
  55.2 0.0 collective-permute-done.east
  55.2 1.8 %inner_rows.1 = (f32[8,17,8,128]{3,2,1,0:T(8,128)S(1)}, f32[8,8,128]{2,1,0:T(8,128)S(1)}, f32[9,8,128]{2,1,0:T(8,128)S(1)}, f32[2,8,8,128]{3,2,1,0:T(8,128)S(1)}) custom-call(f32[12,17,4,128]{3,2,1,0:T(4,128)S(1)} %bitcast.27, f32[12,17,4,128]{3,2,1,0:T(4,128)S(1)} %collective-permute-done.east, f32[12,17,4,128]{3,2,1,0:T(4,128)S(1)} %collective-permute-done.1.west, ...), custom_call_target="tpu_custom_call" | custom-call | tf_op jit(solution)/shard_map/inner_rows/pallas_call | solution.py:421
  57.1 0.0 collective-permute-done.4.south_in
  57.1 4.2 %collective-permute-done.5.north_in = f32[558,128]{1,0:T(8,128)S(1)} collective-permute-done((f32[558,128]{1,0:T(8,128)S(1)}, f32[558,128]{1,0:T(8,128)S(1)}, u32[]{:S(2)}, u32[]{:S(2)}) %collective-permute-start.5) | collective-permute-done | bytes 285728 | tf_op jit(solution)/shard_map/ppermute | solution.py:35
  61.2 5.3 %outer_rows.1 = (f32[12,17,4,128]{3,2,1,0:T(4,128)}, f32[4,48,128]{2,1,0:T(8,128)S(1)}) custom-call(f32[12,17,4,128]{3,2,1,0:T(4,128)S(1)} %bitcast.28, f32[12,17,4,128]{3,2,1,0:T(4,128)S(1)} %collective-permute-done.east, f32[12,17,4,128]{3,2,1,0:T(4,128)S(1)} %collective-permute-done.1.west, f32[558,128]{1,0:T(8,128)S(1)} %collective-permute-done.4.south_in, ...), custom_call_target="tpu_custom_call" | custom-call | tf_op jit(solution)/shard_map/outer_rows/pallas_call | solution.py:421
  66.5 6.3 %all_to_all.10 = f32[4,48,128]{2,1,0:T(8,128)S(1)} all-to-all(f32[4,48,128]{2,1,0:T(8,128)S(1)} %get-tuple-element.31), channel_id=1, replica_groups=mesh['grp'=4,'gx'=48,'gy'=4] {'gy'}, dimensions={0} | all-to-all | bytes 196608 | tf_op jit(solution)/shard_map/all_to_all | solution.py:549
  72.8 0.8 %unpack_levels.1 = (f32[4,32,48]{2,1,0:T(8,128)}, f32[4,32,48]{2,1,0:T(8,128)}, f32[4,32,48]{2,1,0:T(8,128)}, f32[4,32,48]{2,1,0:T(8,128)}) custom-call(f32[192,128]{1,0:T(8,128)S(1)} %bitcast.29), custom_call_target="tpu_custom_call" | custom-call | tf_op jit(solution)/shard_map/unpack_levels/pallas_call | solution.py:421
  (6 shorter events, 0.1 us)
Async XLA Ops:
  1.6 0.7 copy-start.1
  1.6 0.7 copy-start.2
  1.6 1.0 %copy-start = (f32[4,12,17,128]{3,0,2,1:T(4,128)S(1)}, f32[4,12,17,128]{3,0,2,1:T(4,128)}, u32[]{:S(2)}) copy-start(f32[4,12,17,128]{3,0,2,1:T(4,128)} %param.11) | copy-start | bytes 1253380
  2.8 30.3 %collective-permute-start.2 = (f32[284,128]{1,0:T(8,128)S(1)}, f32[284,128]{1,0:T(8,128)S(1)}, u32[]{:S(2)}, u32[]{:S(2)}) collective-permute-start(f32[284,128]{1,0:T(8,128)S(1)} %get-tuple-element.22), channel_id=1, source_target_pairs={{0,4},{4,8},{8,12},{12,16},{16,20},{20,24},{24,28},{28,32},{32,36}... | collective-permute-start | bytes 436232 | tf_op jit(solution)/shard_map/ppermute | solution.py:35
  7.6 25.5 %collective-permute-start.3 = (f32[284,128]{1,0:T(8,128)S(1)}, f32[284,128]{1,0:T(8,128)S(1)}, u32[]{:S(2)}, u32[]{:S(2)}) collective-permute-start(f32[284,128]{1,0:T(8,128)S(1)} %get-tuple-element.23), channel_id=1, source_target_pairs={{0,188},{4,0},{8,4},{12,8},{16,12},{20,16},{24,20},{28,24},{32,28}... | collective-permute-start | bytes 436232 | tf_op jit(solution)/shard_map/ppermute | solution.py:35
  23.5 31.7 %collective-permute-start.1 = (f32[12,17,4,128]{3,2,1,0:T(4,128)S(1)}, f32[12,17,4,128]{3,2,1,0:T(4,128)S(1)}, u32[]{:S(2)}, u32[]{:S(2)}) collective-permute-start(f32[12,17,4,128]{3,2,1,0:T(4,128)S(1)} %bitcast.24), channel_id=1, source_target_pairs={{0,4},{4,8},{8,12},{12,16},{16,20},{20,24},{24,28},{28,32},{32,36}... | collective-permute-start | bytes 1253384 | tf_op jit(solution)/shard_map/ppermute | solution.py:35
  25.5 29.7 %collective-permute-start = (f32[12,17,4,128]{3,2,1,0:T(4,128)S(1)}, f32[12,17,4,128]{3,2,1,0:T(4,128)S(1)}, u32[]{:S(2)}, u32[]{:S(2)}) collective-permute-start(f32[12,17,4,128]{3,2,1,0:T(4,128)S(1)} %bitcast.25), channel_id=1, source_target_pairs={{0,188},{4,0},{8,4},{12,8},{16,12},{20,16},{24,20},{28,24},{32,28}... | collective-permute-start | bytes 1253384 | tf_op jit(solution)/shard_map/ppermute | solution.py:35
  33.8 14.9 %all-to-all-start = ((f32[4,120,128]{2,1,0:T(8,128)}), f32[4,120,128]{2,1,0:T(8,128)S(1)}, u32[]{:S(2)}, u32[]{:S(2)}) async-start(f32[4,120,128]{2,1,0:T(8,128)} %bitcast.10), calls=%async_computation | async-start | bytes 491520 | tf_op jit(solution)/shard_map/all_to_all | solution.py:525
  49.0 8.1 %collective-permute-start.4 = (f32[558,128]{1,0:T(8,128)S(1)}, f32[558,128]{1,0:T(8,128)S(1)}, u32[]{:S(2)}, u32[]{:S(2)}) collective-permute-start(f32[558,128]{1,0:T(8,128)S(1)} %get-tuple-element.24), channel_id=1, source_target_pairs={{0,1},{1,2},{2,3},{3,192},{192,193},{193,194},{194,195},{195,384},... | collective-permute-start | bytes 857096 | tf_op jit(solution)/shard_map/ppermute | solution.py:35
  53.3 8.0 %collective-permute-start.5 = (f32[558,128]{1,0:T(8,128)S(1)}, f32[558,128]{1,0:T(8,128)S(1)}, u32[]{:S(2)}, u32[]{:S(2)}) collective-permute-start(f32[558,128]{1,0:T(8,128)S(1)} %get-tuple-element.25), channel_id=1, source_target_pairs={{0,579},{1,0},{2,1},{3,2},{192,3},{193,192},{194,193},{195,194},{3... | collective-permute-start | bytes 857096 | tf_op jit(solution)/shard_map/ppermute | solution.py:35
